TPU v7x, 32 devices: a whole 2x2x4 slice. The times are simulated.
32 devices in a mesh: row: 8 (over z, x), col: 4 (over y, core).
Axes of the slice: x: 2, y: 2, z: 4, core: 2. Of those that a mesh axis runs over, the one named last changes fastest.
Arguments:
- blocks: bfloat16 [8, 4, 256, 128, 128], P('row', 'col'), may hold values from -0.25 to 0.25
- block_rows: int32 [8, 4, 256], P('row', 'col'), may hold values from 0 to 255
- block_cols: int32 [8, 4, 256], P('row', 'col'), may hold values from 0 to 255
- counts: int32 [8, 4], P('row', 'col'), may hold values from 85 to 256, as said below
- data: float32 [262144], P('row'), may hold values from -16 to 16
Outputs:
- solution: float32 [131072], P('col')
- search: float32 [131072], P('col')
- data_basis: float32 [262144], P('row')
Inputs may be any that keep to these rules, and one draw needn't show every extreme that they name: `counts`: every tile has between 85 and 256 live slots; some tile has exactly 256.
All inputs are finite; a program needn't handle non-finite values.
Results may differ from a plain program's by a relative error of at most 0.013.
Values sent between devices are 32-bit elements; how exact they have to be, the bound alone decides.
No kernel may reach another device: no remote copies, remote signals or barrier semaphores. Data moves between devices by JAX's collectives and lax.ppermute only.
A program may use at most 64 MiB of HBM per device.

v0:
```python
import jax
import jax.numpy as jnp
from jax import lax
from jax.sharding import PartitionSpec as P

TILE_COLS = 256
ITERS = 3


EPS = 1e-06


def local_forward(tile_blocks, rows, cols, count, vector, tile_rows):
    width = tile_blocks.shape[-1]
    vec_b = vector.astype(jnp.bfloat16).reshape(-1, width)
    picked = jnp.take(vec_b, cols, axis=0)
    prod = jnp.einsum("kij,kj->ki", tile_blocks, picked, preferred_element_type=jnp.float32)
    live = (jnp.arange(tile_blocks.shape[0], dtype=jnp.int32) < count).astype(jnp.float32)
    prod = prod * live[:, None]
    return jax.ops.segment_sum(prod, rows, num_segments=tile_rows).reshape(-1)


def local_adjoint(tile_blocks, rows, cols, count, vector, tile_cols):
    width = tile_blocks.shape[-1]
    vec_b = vector.astype(jnp.bfloat16).reshape(-1, width)
    picked = jnp.take(vec_b, rows, axis=0)
    prod = jnp.einsum("kij,ki->kj", tile_blocks, picked, preferred_element_type=jnp.float32)
    live = (jnp.arange(tile_blocks.shape[0], dtype=jnp.int32) < count).astype(jnp.float32)
    prod = prod * live[:, None]
    return jax.ops.segment_sum(prod, cols, num_segments=tile_cols).reshape(-1)


def first_norm(data):
    return jnp.sqrt(lax.psum(jnp.sum(data * data), "row") + EPS)


def new_data_basis(partial_value, previous, alpha):
    summed = lax.psum(partial_value, "col")
    temp = summed - alpha * previous
    return (temp, None)


def new_model_basis(partial_value, previous, beta):
    summed = lax.psum(partial_value, "row")
    temp = summed - beta * previous
    alpha = jnp.sqrt(lax.psum(jnp.sum(temp * temp), "col") + EPS)
    return (temp / alpha, alpha)


def per_device(blocks, block_rows, block_cols, counts, data):
    tile_blocks = blocks[0, 0]
    rows = block_rows[0, 0]
    cols = block_cols[0, 0]
    count = counts[0, 0]
    width = tile_blocks.shape[-1]
    tile_rows = data.shape[0] // width
    tile_cols = TILE_COLS
    beta = first_norm(data)
    data_basis = data / beta
    zero_model = jnp.zeros((tile_cols * width,), jnp.float32)
    model_basis, alpha = new_model_basis(
        local_adjoint(tile_blocks, rows, cols, count, data_basis, tile_cols),
        zero_model,
        jnp.float32(0.0),
    )
    search = model_basis
    solution = zero_model
    phibar = beta
    rhobar = alpha
    for step in range(ITERS):
        partial_value = local_forward(tile_blocks, rows, cols, count, model_basis, tile_rows)
        temp, unused = new_data_basis(partial_value, data_basis, alpha)
        beta = first_norm(temp)
        data_basis = temp / beta
        partial_model = local_adjoint(tile_blocks, rows, cols, count, data_basis, tile_cols)
        model_basis, alpha = new_model_basis(partial_model, model_basis, beta)
        rho = jnp.sqrt(rhobar * rhobar + beta * beta)
        cosine = rhobar / rho
        sine = beta / rho
        theta = sine * alpha
        rhobar = -cosine * alpha
        phi = cosine * phibar
        phibar = sine * phibar
        solution = solution + phi / rho * search
        search = model_basis - theta / rho * search
    return (solution, search, data_basis)


def solution(mesh):
    in_specs = (
        P("row", "col", None, None, None),
        P("row", "col", None),
        P("row", "col", None),
        P("row", "col"),
        P("row"),
    )
    out_specs = (P("col"), P("col"), P("row"))
    return jax.shard_map(
        per_device, mesh=mesh, in_specs=in_specs, out_specs=out_specs, check_vma=False
    )
```

profile of v0, /device:TPU:0, one launch (start us, length us, event | category | flops | bytes accessed | tf_op | source)
XLA Modules:
  0.0 587.4 jit_solution(584488901513735829)
XLA Ops:
  8.6 1.5 multiply_reduce_fusion.7
  10.8 23.8 %psum.105 = f32[]{:T(128)} all-reduce(f32[]{:T(128)} %multiply_reduce_fusion.7), channel_id=1, replica_groups=mesh['row'=8,'col'=4] {'row'}, use_global_device_ids=true, to_apply=%region_1.0 | all-reduce | flops 1 | bytes 8 | tf_op jit(solution)/shard_map/psum | solution.py:34
  35.3 0.9 convert_bitcast_fusion.6
  36.2 0.9 gather_fusion
  37.2 5.7 fusion.12
  42.9 2.1 scatter_custom_fusion
  45.1 67.9 %all-reduce.8.cloned.1.call-done = f32[32768]{0:T(1024)} async-done(((f32[32768]{0:T(1024)}), f32[32768]{0:T(1024)}) %all-reduce.8.cloned.1.call-update) | async-done | bytes 131088 | tf_op jit(solution)/shard_map/psum | solution.py:44
  113.0 1.5 multiply_reduce_fusion.6
  114.5 6.3 %psum.107 = f32[]{:T(128)} all-reduce(f32[]{:T(128)} %multiply_reduce_fusion.6), channel_id=1, replica_groups=mesh['row'=8,'col'=4] {'col'}, use_global_device_ids=true, to_apply=%region_5.7 | all-reduce | flops 1 | bytes 8 | tf_op jit(solution)/shard_map/psum | solution.py:46
  121.5 0.9 convert_bitcast_fusion.5
  122.4 0.9 gather_fusion.1
  123.4 7.8 %fusion.10 = f32[256,1,128]{2,1,0:T(1,128)S(1)} fusion(bf16[1,1,256,128,128]{4,3,2,1,0:T(8,128)(2,1)} %param.7, bf16[256,128,1]{1,0,2:T(8,128)(2,1)S(1)} %select_bitcast_fusion.5), kind=kOutput, calls=%fused_computation.24 | convolution fusion | flops 8388608 | bytes 8585216 | tf_op jit(solution)/shard_map/kij,kj->ki/dot_general | solution.py:17
  131.2 2.3 scatter_custom_fusion.1
  133.6 31.2 %all-reduce.10.cloned.1.call-done = f32[32768]{0:T(1024)} async-done(((f32[32768]{0:T(1024)}), f32[32768]{0:T(1024)}) %all-reduce.10.cloned.1.call-update) | async-done | bytes 131088 | tf_op jit(solution)/shard_map/psum | solution.py:38
  164.8 1.6 multiply_reduce_fusion.5
  166.4 22.0 %psum.109 = f32[]{:T(128)} all-reduce(f32[]{:T(128)} %get-tuple-element.10), channel_id=1, replica_groups=mesh['row'=8,'col'=4] {'row'}, use_global_device_ids=true, to_apply=%region_9.11 | all-reduce | flops 1 | bytes 8 | tf_op jit(solution)/shard_map/psum | solution.py:34
  189.0 0.9 gather_fusion.2
  190.0 5.7 fusion.8
  195.7 2.1 scatter_custom_fusion.2
  197.9 66.9 %all-reduce.12.cloned.1.call-done = f32[32768]{0:T(1024)} async-done(((f32[32768]{0:T(1024)}), f32[32768]{0:T(1024)}) %all-reduce.12.cloned.1.call-update) | async-done | bytes 131088 | tf_op jit(solution)/shard_map/psum | solution.py:44
  264.8 1.6 multiply_reduce_fusion.4
  266.3 6.4 %psum.111 = f32[]{:T(128)} all-reduce(f32[]{:T(128)} %multiply_reduce_fusion.4), channel_id=1, replica_groups=mesh['row'=8,'col'=4] {'col'}, use_global_device_ids=true, to_apply=%region_13.15 | all-reduce | flops 1 | bytes 8 | tf_op jit(solution)/shard_map/psum | solution.py:46
  273.4 0.9 convert_bitcast_fusion.3
  274.4 0.9 gather_fusion.3
  275.4 7.8 %fusion.6 = f32[256,1,128]{2,1,0:T(1,128)S(1)} fusion(bf16[1,1,256,128,128]{4,3,2,1,0:T(8,128)(2,1)} %param.7, bf16[256,128,1]{1,0,2:T(8,128)(2,1)S(1)} %select_bitcast_fusion.3), kind=kOutput, calls=%fused_computation.20 | convolution fusion | flops 8388608 | bytes 8585216 | tf_op jit(solution)/shard_map/kij,kj->ki/dot_general | solution.py:17
  283.1 2.3 scatter_custom_fusion.3
  285.5 31.2 %all-reduce.14.cloned.1.call-done = f32[32768]{0:T(1024)} async-done(((f32[32768]{0:T(1024)}), f32[32768]{0:T(1024)}) %all-reduce.14.cloned.1.call-update) | async-done | bytes 131088 | tf_op jit(solution)/shard_map/psum | solution.py:38
  316.7 1.5 multiply_reduce_fusion.3
  318.3 22.0 %psum.113 = f32[]{:T(128)} all-reduce(f32[]{:T(128)} %get-tuple-element.6), channel_id=1, replica_groups=mesh['row'=8,'col'=4] {'row'}, use_global_device_ids=true, to_apply=%region_17.19 | all-reduce | flops 1 | bytes 8 | tf_op jit(solution)/shard_map/psum | solution.py:34
  341.9 5.7 fusion.4
  347.6 2.1 scatter_custom_fusion.4
  349.8 66.8 %all-reduce.16.cloned.1.call-done = f32[32768]{0:T(1024)} async-done(((f32[32768]{0:T(1024)}), f32[32768]{0:T(1024)}) %all-reduce.16.cloned.1.call-update) | async-done | bytes 131088 | tf_op jit(solution)/shard_map/psum | solution.py:44
  416.6 1.5 multiply_reduce_fusion.2
  418.2 6.3 %psum.115 = f32[]{:T(128)} all-reduce(f32[]{:T(128)} %multiply_reduce_fusion.2), channel_id=1, replica_groups=mesh['row'=8,'col'=4] {'col'}, use_global_device_ids=true, to_apply=%region_21.23 | all-reduce | flops 1 | bytes 8 | tf_op jit(solution)/shard_map/psum | solution.py:46
  425.2 0.9 convert_bitcast_fusion.1
  426.1 0.9 gather_fusion.5
  427.1 7.8 %fusion.2 = f32[256,1,128]{2,1,0:T(1,128)S(1)} fusion(bf16[1,1,256,128,128]{4,3,2,1,0:T(8,128)(2,1)} %param.7, bf16[256,128,1]{1,0,2:T(8,128)(2,1)S(1)} %select_bitcast_fusion.1), kind=kOutput, calls=%fused_computation.16 | convolution fusion | flops 8388608 | bytes 8585216 | tf_op jit(solution)/shard_map/kij,kj->ki/dot_general | solution.py:17
  434.9 2.3 scatter_custom_fusion.5
  437.2 31.2 %all-reduce.18.cloned.1.call-done = f32[32768]{0:T(1024)} async-done(((f32[32768]{0:T(1024)}), f32[32768]{0:T(1024)}) %all-reduce.18.cloned.1.call-update) | async-done | bytes 131088 | tf_op jit(solution)/shard_map/psum | solution.py:38
  468.5 1.5 multiply_reduce_fusion.1
  470.0 22.2 %psum.117 = f32[]{:T(128)} all-reduce(f32[]{:T(128)} %multiply_reduce_fusion.1), channel_id=1, replica_groups=mesh['row'=8,'col'=4] {'row'}, use_global_device_ids=true, to_apply=%region_25.27 | all-reduce | flops 1 | bytes 8 | tf_op jit(solution)/shard_map/psum | solution.py:34
  492.9 1.6 convert_bitcast_fusion
  495.5 5.7 fusion
  501.1 2.1 scatter_custom_fusion.6
  503.9 66.4 %all-reduce.20.cloned.1.call-done = f32[32768]{0:T(1024)} async-done(((f32[32768]{0:T(1024)}), f32[32768]{0:T(1024)}) %all-reduce.20.cloned.1.call-update) | async-done | bytes 131088 | tf_op jit(solution)/shard_map/psum | solution.py:44
  570.2 1.6 multiply_reduce_fusion
  571.8 6.3 %psum.119 = f32[]{:T(128)} all-reduce(f32[]{:T(128)} %multiply_reduce_fusion), channel_id=1, replica_groups=mesh['row'=8,'col'=4] {'col'}, use_global_device_ids=true, to_apply=%region_29.31 | all-reduce | flops 1 | bytes 8 | tf_op jit(solution)/shard_map/psum | solution.py:46
  578.8 1.7 multiply_subtract_fusion
  (40 shorter events, 4.3 us)
Async XLA Ops:
  7.2 35.7 %copy-start.3 = (s32[1,1,256]{2,1,0:T(1,128)S(1)}, s32[1,1,256]{2,1,0:T(1,128)}, u32[]{:S(2)}) copy-start(s32[1,1,256]{2,1,0:T(1,128)} %param.9) | copy-start | bytes 3076
  7.2 105.8 %all-reduce.8.cloned.1.call-start = ((), (), s32[]{:S(2)}) async-start(), calls=%async_computation | async-start | bytes 262144 | tf_op jit(solution)/shard_map/psum | solution.py:44
  37.2 127.6 %copy-start.2 = (f32[32768]{0:T(1024)S(1)}, f32[32768]{0:T(1024)}, u32[]{:S(2)}) copy-start(f32[32768]{0:T(1024)} %param.11) | copy-start | bytes 393220
  45.0 119.8 %all-reduce.10.cloned.1.call-start = ((), (), s32[]{:S(2)}) async-start(), calls=%async_computation.1 | async-start | bytes 262144 | tf_op jit(solution)/shard_map/psum | solution.py:38
  123.4 141.4 %copy-start = (f32[32768]{0:T(1024)S(1)}, f32[32768]{0:T(1024)}, u32[]{:S(2)}) copy-start(f32[32768]{0:T(1024)} %all-reduce.8.cloned.1.call-done) | copy-start | bytes 393220
  133.5 131.2 %all-reduce.12.cloned.1.call-start = ((), (), s32[]{:S(2)}) async-start(), calls=%async_computation.2 | async-start | bytes 262144 | tf_op jit(solution)/shard_map/psum | solution.py:44
  197.8 118.9 %all-reduce.14.cloned.1.call-start = ((), (), s32[]{:S(2)}) async-start(), calls=%async_computation.3 | async-start | bytes 262144 | tf_op jit(solution)/shard_map/psum | solution.py:38
  285.5 131.2 %all-reduce.16.cloned.1.call-start = ((), (), s32[]{:S(2)}) async-start(), calls=%async_computation.4 | async-start | bytes 262144 | tf_op jit(solution)/shard_map/psum | solution.py:44
  349.8 118.7 %all-reduce.18.cloned.1.call-start = ((), (), s32[]{:S(2)}) async-start(), calls=%async_computation.5 | async-start | bytes 262144 | tf_op jit(solution)/shard_map/psum | solution.py:38
  427.1 143.2 %copy-start.1 = (f32[32768]{0:T(1024)S(1)}, f32[32768]{0:T(1024)}, u32[]{:S(2)}) copy-start(f32[32768]{0:T(1024)} %all-reduce.16.cloned.1.call-done) | copy-start | bytes 393220
  437.2 133.0 %all-reduce.20.cloned.1.call-start = ((), (), s32[]{:S(2)}) async-start(), calls=%async_computation.6 | async-start | bytes 262144 | tf_op jit(solution)/shard_map/psum | solution.py:44
Sparse Core Ops, SparseCore 0:
  45.1 67.7 all-reduce.7
  133.6 31.1 all-reduce.9
  197.9 66.7 all-reduce.11
  285.6 31.1 all-reduce.13
  349.9 66.7 all-reduce.15
  437.3 31.1 all-reduce.17
  503.4 66.7 all-reduce.19
where the time goes:
time: 588 us; the launch traced here: 587 us
  waiting for transfers between devices  362 us (62%)
  blocking collectives  115 us (20%)
  matrix products  46 us (8%)
  other arithmetic  37 us (6%)
  between operations  21.2 us (4%)
  local copies, waits for them, and re-layouts  6 us (1%)
    psum x4, waiting for transfers between devices, new_model_basis(): summed = lax.psum(partial_value, 'row')  268 us
    psum x3, waiting for transfers between devices, new_data_basis(): summed = lax.psum(partial_value, 'col')  93.7 us
    psum x4, blocking collectives, first_norm(): return jnp.sqrt(lax.psum(jnp.sum(data * data), 'row') + EPS)  89.9 us
    psum x4, blocking collectives, new_model_basis(): alpha = jnp.sqrt(lax.psum(jnp.sum(temp * temp), 'col') + EPS)  25.3 us
    dot_general x3, matrix products, local_forward(): jnp.einsum('kij,kj->ki', tile_blocks, picked, preferred_element_type=jnp....  23.4 us
    dot_general x4, matrix products, local_adjoint(): jnp.einsum('kij,ki->kj', tile_blocks, picked, preferred_element_type=jnp....  22.6 us
  transfers between devices with their start and end apart: 7, of which 7 were waited for; matrix products, arithmetic and copies ran while one was open for 0% of the time, Pallas kernels for 0%

commit v1 on v0

v1 whole, which is shorter than its diff:
```python
import functools

import jax
import jax.numpy as jnp
from jax import lax
from jax.experimental import pallas as pl
from jax.experimental.pallas import tpu as pltpu
from jax.sharding import PartitionSpec as P

TILE_COLS = 256
ITERS = 3
EPS = 1e-06
GROUP = 16
RIDE = 8


def halves(values):
    high = values.astype(jnp.bfloat16)
    low = (values - high.astype(jnp.float32)).astype(jnp.bfloat16)
    return jnp.concatenate([high, low], 0)


def squares(vector):
    rows, width = vector.shape
    return jnp.sum((vector * vector).reshape(rows // RIDE, RIDE, width), 0)


def norm_row(tile):
    total = jnp.sum(jnp.sum(tile, 0, keepdims=True), 1, keepdims=True)
    return jnp.broadcast_to(jnp.sqrt(total + EPS), (1, tile.shape[1]))


def slot_products(pick_ref, vector, blocks_ref, picked_ref, prod_ref, transpose):
    picked_ref[...] = jnp.dot(
        pick_ref[...], vector.astype(jnp.bfloat16), preferred_element_type=jnp.float32
    ).astype(jnp.bfloat16)
    slots, width, _ = blocks_ref.shape
    if transpose:
        shape = (GROUP, GROUP * width)
        mine = lax.broadcasted_iota(jnp.int32, shape, 1) // width == lax.broadcasted_iota(jnp.int32, shape, 0)
    else:
        row = lax.broadcasted_iota(jnp.int32, (GROUP, width), 0)
    for at in range(0, slots, GROUP):
        piece = picked_ref[at : at + GROUP]
        stack = blocks_ref[at : at + GROUP].reshape(GROUP * width, width)
        if transpose:
            spread = jnp.where(mine, jnp.concatenate([piece] * GROUP, 1), jnp.bfloat16(0))
            prod_ref[at : at + GROUP] = jnp.dot(spread, stack, preferred_element_type=jnp.float32)
        else:
            every = lax.dot_general(
                piece, stack, (((1,), (1,)), ((), ())), preferred_element_type=jnp.float32
            )
            total = jnp.zeros((GROUP, width), jnp.float32)
            for slot in range(GROUP):
                total = total + jnp.where(row == slot, every[:, slot * width : (slot + 1) * width], 0.0)
            prod_ref[at : at + GROUP] = total


def send(put_ref, vector, prod_ref, out_ref):
    put = put_ref[...]
    rows = put.shape[0]
    out_ref[:rows] = jnp.dot(
        jnp.concatenate([put, put], 1), halves(prod_ref[...]), preferred_element_type=jnp.float32
    )
    out_ref[rows:] = squares(vector)


def first_kernel(pick_ref, put_ref, data_ref, blocks_ref, out_ref, picked_ref, prod_ref):
    vector = data_ref[...]
    slot_products(pick_ref, vector, blocks_ref, picked_ref, prod_ref, True)
    send(put_ref, vector, prod_ref, out_ref)


def recur(summed_ref, previous):
    rows = summed_ref.shape[0] - RIDE
    norm = norm_row(summed_ref[rows:])
    vector = summed_ref[:rows] * (1.0 / norm)
    if previous:
        before_ref, before_norm_ref = previous
        vector = vector - (norm / before_norm_ref[:1]) * before_ref[...]
    return vector, norm


def step_kernel(transpose, pick_ref, put_ref, summed_ref, *refs):
    *previous, blocks_ref, out_ref, vector_ref, norm_ref, picked_ref, prod_ref = refs
    vector, norm = recur(summed_ref, previous)
    vector_ref[...] = vector
    norm_ref[...] = jnp.broadcast_to(norm, norm_ref.shape)
    slot_products(pick_ref, vector, blocks_ref, picked_ref, prod_ref, transpose)
    send(put_ref, vector, prod_ref, out_ref)


def last_kernel(steps, summed_ref, data_vector_ref, *refs):
    norms, refs = refs[: 2 * steps], refs[2 * steps :]
    alphas, betas = [r[:1] for r in norms[:steps]], [r[:1] for r in norms[steps:]]
    models, (solution_ref, search_ref, vector_ref, basis_ref, square_ref, coef_ref) = refs[:steps], refs[steps:]
    vector, beta = recur(summed_ref, (models[-1], norms[steps - 1]))
    betas.append(beta)
    vector_ref[...] = vector
    square_ref[...] = squares(vector)
    basis_ref[...] = data_vector_ref[...] * (1.0 / beta)
    search = models[0][...] * (1.0 / alphas[0])
    solution = jnp.zeros_like(search)
    phibar, rhobar = betas[0], alphas[0]
    for step in range(steps):
        rho = jnp.sqrt(rhobar * rhobar + betas[step + 1] * betas[step + 1])
        cosine, sine = rhobar / rho, betas[step + 1] / rho
        solution = solution + (cosine * phibar / rho) * search
        phibar = sine * phibar
        if step + 1 < steps:
            rhobar = -cosine * alphas[step + 1]
            search = models[step + 1][...] * (1.0 / alphas[step + 1]) - (sine * alphas[step + 1] / rho) * search
    solution_ref[...] = solution
    search_ref[...] = search
    coef_ref[...] = jnp.broadcast_to(sine / rho, coef_ref.shape)


def search_kernel(square_ref, vector_ref, search_ref, coef_ref, out_ref):
    alpha = norm_row(square_ref[...])
    out_ref[...] = vector_ref[...] * (1.0 / alpha) - (coef_ref[:1] * alpha) * search_ref[...]


def call(kernel, outs, args, slots=None, width=None):
    spec = pl.BlockSpec(memory_space=pltpu.VMEM)
    scratch = [] if slots is None else [pltpu.VMEM((slots, width), jnp.bfloat16), pltpu.VMEM((slots, width), jnp.float32)]
    return pl.pallas_call(
        kernel,
        out_shape=[jax.ShapeDtypeStruct(shape, jnp.float32) for shape in outs],
        in_specs=[spec] * len(args),
        out_specs=[spec] * len(outs),
        scratch_shapes=scratch,
        compiler_params=pltpu.CompilerParams(vmem_limit_bytes=32 * 1024 * 1024),
    )(*args)


def all_sum(values, axis, size):
    bit = 1
    while bit < size:
        values = values + lax.ppermute(values, axis, [(i, i ^ bit) for i in range(size)])
        bit *= 2
    return values


def per_device(n_row, n_col, blocks, block_rows, block_cols, counts, data):
    tile_blocks = blocks[0, 0]
    slots, _, width = tile_blocks.shape
    data = data.reshape(-1, width)
    tile_rows, tile_cols = data.shape[0], TILE_COLS
    live = jnp.arange(slots, dtype=jnp.int32) < counts[0, 0]

    def picks(index, size):
        index = jnp.where(live, index, -1)
        places = jnp.arange(size, dtype=jnp.int32)
        pick = (index[:, None] == places[None, :]).astype(jnp.bfloat16)
        put = (places[:, None] == index[None, :]).astype(jnp.bfloat16)
        return pick, put

    pick_row, put_row = picks(block_rows[0, 0], tile_rows)
    pick_col, put_col = picks(block_cols[0, 0], tile_cols)
    tile, model, basis = (RIDE, width), (tile_cols, width), (tile_rows, width)
    to_model, to_basis = (tile_cols + RIDE, width), (tile_rows + RIDE, width)
    (part,) = call(first_kernel, [to_model], [pick_row, put_col, data, tile_blocks], slots, width)
    summed = all_sum(part, "row", n_row)
    alphas, betas, models = [], [], []
    bases = [data]
    for step in range(ITERS):
        previous = [models[-1], alphas[-1]] if models else []
        part, vector, beta = call(
            functools.partial(step_kernel, False),
            [to_basis, model, tile],
            [pick_col, put_row, summed, *previous, tile_blocks],
            slots,
            width,
        )
        models.append(vector)
        betas.append(beta)
        summed = all_sum(part, "col", n_col)
        part, vector, alpha = call(
            functools.partial(step_kernel, True),
            [to_model, basis, tile],
            [pick_row, put_col, summed, bases[-1], beta, tile_blocks],
            slots,
            width,
        )
        bases.append(vector)
        alphas.append(alpha)
        summed = all_sum(part, "row", n_row)
    solution, search, vector, data_basis, square, coef = call(
        functools.partial(last_kernel, ITERS),
        [model, model, model, basis, tile, tile],
        [summed, bases[-1], *alphas, *betas, *models],
    )
    square = all_sum(square, "col", n_col)
    (search,) = call(search_kernel, [model], [square, vector, search, coef])
    return solution.reshape(-1), search.reshape(-1), data_basis.reshape(-1)


def solution(mesh):
    in_specs = (
        P("row", "col", None, None, None),
        P("row", "col", None),
        P("row", "col", None),
        P("row", "col"),
        P("row"),
    )
    out_specs = (P("col"), P("col"), P("row"))
    return jax.shard_map(
        functools.partial(per_device, mesh.shape["row"], mesh.shape["col"]),
        mesh=mesh,
        in_specs=in_specs,
        out_specs=out_specs,
        check_vma=False,
    )
```

time: 588 us -> 121 us (0.21)
  waiting for transfers between devices: 362 us -> 70.5 us
  blocking collectives: 115 us -> 0 us
  matrix products: 46 us -> 0 us
  other arithmetic: 37 us -> 1.25 us
  starting transfers between devices: 0.29 us -> 27.3 us
  between operations: 21.2 us -> 1.43 us
  Pallas kernels: 0 us -> 16.5 us
    psum x7 -> x0, waiting for transfers between devices: 362 us -> none  [the longest x4 268 us: new_model_basis(): summed = lax.psum(partial_value, 'row')]
    psum x8 -> x0, blocking collectives: 115 us -> none  [the longest x4 89.9 us: first_norm(): return jnp.sqrt(lax.psum(jnp.sum(data * data), 'row') + EPS)]
    ppermute x0 -> x20, waiting for transfers between devices: none -> 70.5 us  [all_sum(): lax.ppermute(values, axis, [(i, i ^ bit) for i in range(size)])]
    dot_general x7 -> x0, matrix products: 46 us -> none  [the longest x3 23.4 us: local_forward(): jnp.einsum('kij,kj->ki', tile_blocks, picked, preferred_element_type=jnp....]
    ppermute x0 -> x20, starting transfers between devices: none -> 27.3 us  [all_sum(): lax.ppermute(values, axis, [(i, i ^ bit) for i in range(size)])]
    pallas_call x0 -> x9, Pallas kernels: none -> 16.5 us  [call(): pl.pallas_call(kernel, out_shape=[jax.ShapeDtypeStruct(shape, jnp.float32...]
    scatter-add x7 -> x0, other arithmetic: 15.5 us -> none  [the longest x4 8.57 us: local_adjoint(): return jax.ops.segment_sum(prod, cols, num_segments=tile_cols).reshape(-1)]
    reduce_sum x8 -> x0, other arithmetic: 12.4 us -> none  [the longest x4 6.19 us: first_norm(): return jnp.sqrt(lax.psum(jnp.sum(data * data), 'row') + EPS)]
  transfers between devices with their start and end apart: 7 -> 20, of which waited for: 7 -> 20; matrix products, arithmetic and copies ran while one was open for 0% -> 0% of each run, Pallas kernels for 0% -> 0%
where the time goes in v1:
time: 121 us
  waiting for transfers between devices  70.5 us (58%)
  starting transfers between devices  27.3 us (23%)
  Pallas kernels  16.5 us (14%)
  local copies, waits for them, and re-layouts  4.28 us (4%)
  between operations  1.43 us (1%)
  other arithmetic  1.25 us (1%)
    ppermute x20, waiting for transfers between devices, all_sum(): lax.ppermute(values, axis, [(i, i ^ bit) for i in range(size)])  70.5 us
    ppermute x20, starting transfers between devices, all_sum(): lax.ppermute(values, axis, [(i, i ^ bit) for i in range(size)])  27.3 us
    pallas_call x9, Pallas kernels, call(): pl.pallas_call(kernel, out_shape=[jax.ShapeDtypeStruct(shape, jnp.float32...  16.5 us
    unnamed x6, local copies, waits for them, and re-layouts  4.28 us
  transfers between devices with their start and end apart: 20, of which 20 were waited for; matrix products, arithmetic and copies ran while one was open for 0% of the time, Pallas kernels for 0%

profile of v1, /device:TPU:0, one launch (start us, length us, event | category | flops | bytes accessed | tf_op | source)
XLA Modules:
  0.0 121.2 jit_solution(8253146952156515604)
XLA Ops:
  1.3 0.7 fusion.4
  2.0 0.1 fusion.2
  2.2 3.4 %copy-done = bf16[1,1,256,128,128]{4,3,2,1,0:T(8,128)(2,1)S(1)} copy-done((bf16[1,1,256,128,128]{4,3,2,1,0:T(8,128)(2,1)S(1)}, bf16[1,1,256,128,128]{4,3,2,1,0:T(8,128)(2,1)}, u32[]{:S(2)}) %copy-start) | copy-done | bytes 8388632
  5.6 0.9 copy-done.2
  6.5 1.6 %shard_map.76 = f32[264,128]{1,0:T(8,128)S(1)} custom-call(bf16[256,256]{1,0:T(8,128)(2,1)S(1)} %get-tuple-element.52.pick_ref, bf16[256,256]{1,0:T(8,128)(2,1)S(1)} %get-tuple-element.54.put_ref, f32[256,128]{1,0:T(8,128)S(1)} %bitcast.16, bf16[256,128,128]{2,1,0:T(8,128)(2,1)S(1)} %bitcast.9), custom_call_target="tpu_custom_call" | custom-call | tf_op jit(solution)/shard_map/pallas_call | solution.py:126
  8.1 3.0 %collective-permute-start = (f32[264,128]{1,0:T(8,128)S(1)}, f32[264,128]{1,0:T(8,128)S(1)}, u32[]{:S(2)}, u32[]{:S(2)}) collective-permute-start(f32[264,128]{1,0:T(8,128)S(1)} %shard_map.76), channel_id=1, source_target_pairs={{0,4},{4,0},{8,12},{12,8},{16,20},{20,16},{24,28},{28,24},{1,5},{5... | collective-permute-start | bytes 405512 | tf_op jit(solution)/shard_map/ppermute | solution.py:139
  11.1 3.6 %collective-permute-done = f32[264,128]{1,0:T(8,128)S(1)} collective-permute-done((f32[264,128]{1,0:T(8,128)S(1)}, f32[264,128]{1,0:T(8,128)S(1)}, u32[]{:S(2)}, u32[]{:S(2)}) %collective-permute-start) | collective-permute-done | bytes 135200 | tf_op jit(solution)/shard_map/ppermute | solution.py:139
  14.7 1.9 %collective-permute-start.1 = (f32[264,128]{1,0:T(8,128)S(1)}, f32[264,128]{1,0:T(8,128)S(1)}, u32[]{:S(2)}, u32[]{:S(2)}) collective-permute-start(f32[264,128]{1,0:T(8,128)S(1)} %add.60), channel_id=1, source_target_pairs={{0,8},{4,12},{8,0},{12,4},{16,24},{20,28},{24,16},{28,20},{1,9},{5... | collective-permute-start | bytes 405512 | tf_op jit(solution)/shard_map/ppermute | solution.py:139
  16.6 3.2 %collective-permute-done.1 = f32[264,128]{1,0:T(8,128)S(1)} collective-permute-done((f32[264,128]{1,0:T(8,128)S(1)}, f32[264,128]{1,0:T(8,128)S(1)}, u32[]{:S(2)}, u32[]{:S(2)}) %collective-permute-start.1) | collective-permute-done | bytes 135200 | tf_op jit(solution)/shard_map/ppermute | solution.py:139
  19.8 2.9 %collective-permute-start.2 = (f32[264,128]{1,0:T(8,128)S(1)}, f32[264,128]{1,0:T(8,128)S(1)}, u32[]{:S(2)}, u32[]{:S(2)}) collective-permute-start(f32[264,128]{1,0:T(8,128)S(1)} %add.61), channel_id=1, source_target_pairs={{0,16},{4,20},{8,24},{12,28},{16,0},{20,4},{24,8},{28,12},{1,17},{... | collective-permute-start | bytes 405512 | tf_op jit(solution)/shard_map/ppermute | solution.py:139
  22.7 4.6 %collective-permute-done.2 = f32[264,128]{1,0:T(8,128)S(1)} collective-permute-done((f32[264,128]{1,0:T(8,128)S(1)}, f32[264,128]{1,0:T(8,128)S(1)}, u32[]{:S(2)}, u32[]{:S(2)}) %collective-permute-start.2) | collective-permute-done | bytes 135200 | tf_op jit(solution)/shard_map/ppermute | solution.py:139
  27.3 2.7 %shard_map.77 = (f32[264,128]{1,0:T(8,128)S(1)}, f32[256,128]{1,0:T(8,128)S(1)}, f32[8,128]{1,0:T(8,128)S(1)}) custom-call(bf16[256,256]{1,0:T(8,128)(2,1)S(1)} %get-tuple-element.53.pick_ref, bf16[256,256]{1,0:T(8,128)(2,1)S(1)} %get-tuple-element.51.put_ref, f32[264,128]{1,0:T(8,128)S(1)} %add.62.summed_ref, bf16[256,128,128]{2,1,0:T(8,128)(2,1)S(1)} %bitcast.10), custom_call_target="tpu_custom_call" | custom-call | tf_op jit(solution)/shard_map/pallas_call | solution.py:126
  30.1 1.3 %collective-permute-done.3 = f32[264,128]{1,0:T(8,128)S(1)} collective-permute-done((f32[264,128]{1,0:T(8,128)S(1)}, f32[264,128]{1,0:T(8,128)S(1)}, u32[]{:S(2)}, u32[]{:S(2)}) %collective-permute-start.3) | collective-permute-done | bytes 135200 | tf_op jit(solution)/shard_map/ppermute | solution.py:139
  31.5 1.8 %collective-permute-start.4 = (f32[264,128]{1,0:T(8,128)S(1)}, f32[264,128]{1,0:T(8,128)S(1)}, u32[]{:S(2)}, u32[]{:S(2)}) collective-permute-start(f32[264,128]{1,0:T(8,128)S(1)} %add.63), channel_id=1, source_target_pairs={{0,2},{1,3},{2,0},{3,1},{4,6},{5,7},{6,4},{7,5},{8,10},{9,11},{10,... | collective-permute-start | bytes 405512 | tf_op jit(solution)/shard_map/ppermute | solution.py:139
  33.3 3.9 %collective-permute-done.4 = f32[264,128]{1,0:T(8,128)S(1)} collective-permute-done((f32[264,128]{1,0:T(8,128)S(1)}, f32[264,128]{1,0:T(8,128)S(1)}, u32[]{:S(2)}, u32[]{:S(2)}) %collective-permute-start.4) | collective-permute-done | bytes 135200 | tf_op jit(solution)/shard_map/ppermute | solution.py:139
  37.2 1.7 %shard_map.78 = (f32[264,128]{1,0:T(8,128)S(1)}, f32[256,128]{1,0:T(8,128)S(1)}, f32[8,128]{1,0:T(8,128)S(1)}) custom-call(bf16[256,256]{1,0:T(8,128)(2,1)S(1)} %get-tuple-element.52.pick_ref, bf16[256,256]{1,0:T(8,128)(2,1)S(1)} %get-tuple-element.54.put_ref, f32[264,128]{1,0:T(8,128)S(1)} %add.64.summed_ref, f32[256,128]{1,0:T(8,128)S(1)} %bitcast.17, ...), custom_call_target="tpu_custom_call" | custom-call | tf_op jit(solution)/shard_map/pallas_call | solution.py:126
  38.9 1.8 %collective-permute-start.5 = (f32[264,128]{1,0:T(8,128)S(1)}, f32[264,128]{1,0:T(8,128)S(1)}, u32[]{:S(2)}, u32[]{:S(2)}) collective-permute-start(f32[264,128]{1,0:T(8,128)S(1)} %get-tuple-element.29), channel_id=1, source_target_pairs={{0,4},{4,0},{8,12},{12,8},{16,20},{20,16},{24,28},{28,24},{1,5},{5... | collective-permute-start | bytes 405512 | tf_op jit(solution)/shard_map/ppermute | solution.py:139
  40.7 3.3 %collective-permute-done.5 = f32[264,128]{1,0:T(8,128)S(1)} collective-permute-done((f32[264,128]{1,0:T(8,128)S(1)}, f32[264,128]{1,0:T(8,128)S(1)}, u32[]{:S(2)}, u32[]{:S(2)}) %collective-permute-start.5) | collective-permute-done | bytes 135200 | tf_op jit(solution)/shard_map/ppermute | solution.py:139
  44.0 1.0 collective-permute-start.6
  44.9 4.1 %collective-permute-done.6 = f32[264,128]{1,0:T(8,128)S(1)} collective-permute-done((f32[264,128]{1,0:T(8,128)S(1)}, f32[264,128]{1,0:T(8,128)S(1)}, u32[]{:S(2)}, u32[]{:S(2)}) %collective-permute-start.6) | collective-permute-done | bytes 135200 | tf_op jit(solution)/shard_map/ppermute | solution.py:139
  49.1 2.4 %collective-permute-start.7 = (f32[264,128]{1,0:T(8,128)S(1)}, f32[264,128]{1,0:T(8,128)S(1)}, u32[]{:S(2)}, u32[]{:S(2)}) collective-permute-start(f32[264,128]{1,0:T(8,128)S(1)} %add.66), channel_id=1, source_target_pairs={{0,16},{4,20},{8,24},{12,28},{16,0},{20,4},{24,8},{28,12},{1,17},{... | collective-permute-start | bytes 405512 | tf_op jit(solution)/shard_map/ppermute | solution.py:139
  51.4 5.1 %collective-permute-done.7 = f32[264,128]{1,0:T(8,128)S(1)} collective-permute-done((f32[264,128]{1,0:T(8,128)S(1)}, f32[264,128]{1,0:T(8,128)S(1)}, u32[]{:S(2)}, u32[]{:S(2)}) %collective-permute-start.7) | collective-permute-done | bytes 135200 | tf_op jit(solution)/shard_map/ppermute | solution.py:139
  56.5 2.7 %shard_map.79 = (f32[264,128]{1,0:T(8,128)S(1)}, f32[256,128]{1,0:T(8,128)S(1)}, f32[8,128]{1,0:T(8,128)S(1)}) custom-call(bf16[256,256]{1,0:T(8,128)(2,1)S(1)} %get-tuple-element.53.pick_ref, bf16[256,256]{1,0:T(8,128)(2,1)S(1)} %get-tuple-element.51.put_ref, f32[264,128]{1,0:T(8,128)S(1)} %add.67.summed_ref, ...), custom_call_target="tpu_custom_call" | custom-call | tf_op jit(solution)/shard_map/pallas_call | solution.py:126
  59.4 1.3 %collective-permute-done.8 = f32[264,128]{1,0:T(8,128)S(1)} collective-permute-done((f32[264,128]{1,0:T(8,128)S(1)}, f32[264,128]{1,0:T(8,128)S(1)}, u32[]{:S(2)}, u32[]{:S(2)}) %collective-permute-start.8) | collective-permute-done | bytes 135200 | tf_op jit(solution)/shard_map/ppermute | solution.py:139
  60.7 1.8 %collective-permute-start.9 = (f32[264,128]{1,0:T(8,128)S(1)}, f32[264,128]{1,0:T(8,128)S(1)}, u32[]{:S(2)}, u32[]{:S(2)}) collective-permute-start(f32[264,128]{1,0:T(8,128)S(1)} %add.68), channel_id=1, source_target_pairs={{0,2},{1,3},{2,0},{3,1},{4,6},{5,7},{6,4},{7,5},{8,10},{9,11},{10,... | collective-permute-start | bytes 405512 | tf_op jit(solution)/shard_map/ppermute | solution.py:139
  62.5 3.9 %collective-permute-done.9 = f32[264,128]{1,0:T(8,128)S(1)} collective-permute-done((f32[264,128]{1,0:T(8,128)S(1)}, f32[264,128]{1,0:T(8,128)S(1)}, u32[]{:S(2)}, u32[]{:S(2)}) %collective-permute-start.9) | collective-permute-done | bytes 135200 | tf_op jit(solution)/shard_map/ppermute | solution.py:139
  66.4 1.7 %shard_map.80 = (f32[264,128]{1,0:T(8,128)S(1)}, f32[256,128]{1,0:T(8,128)S(1)}, f32[8,128]{1,0:T(8,128)S(1)}) custom-call(bf16[256,256]{1,0:T(8,128)(2,1)S(1)} %get-tuple-element.52.pick_ref, bf16[256,256]{1,0:T(8,128)(2,1)S(1)} %get-tuple-element.54.put_ref, f32[264,128]{1,0:T(8,128)S(1)} %add.69.summed_ref, f32[256,128]{1,0:T(8,128)S(1)} %get-tuple-element.33.refs_0_, ...), custom_call_target="tpu_custom_call" | custom-call | tf_op jit(solution)/shard_map/pallas_call | solution.py:126
  68.1 1.8 %collective-permute-start.10 = (f32[264,128]{1,0:T(8,128)S(1)}, f32[264,128]{1,0:T(8,128)S(1)}, u32[]{:S(2)}, u32[]{:S(2)}) collective-permute-start(f32[264,128]{1,0:T(8,128)S(1)} %get-tuple-element.35), channel_id=1, source_target_pairs={{0,4},{4,0},{8,12},{12,8},{16,20},{20,16},{24,28},{28,24},{1,5},{5... | collective-permute-start | bytes 405512 | tf_op jit(solution)/shard_map/ppermute | solution.py:139
  69.9 3.3 %collective-permute-done.10 = f32[264,128]{1,0:T(8,128)S(1)} collective-permute-done((f32[264,128]{1,0:T(8,128)S(1)}, f32[264,128]{1,0:T(8,128)S(1)}, u32[]{:S(2)}, u32[]{:S(2)}) %collective-permute-start.10) | collective-permute-done | bytes 135200 | tf_op jit(solution)/shard_map/ppermute | solution.py:139
  73.2 0.4 collective-permute-start.11
  73.7 4.6 %collective-permute-done.11 = f32[264,128]{1,0:T(8,128)S(1)} collective-permute-done((f32[264,128]{1,0:T(8,128)S(1)}, f32[264,128]{1,0:T(8,128)S(1)}, u32[]{:S(2)}, u32[]{:S(2)}) %collective-permute-start.11) | collective-permute-done | bytes 135200 | tf_op jit(solution)/shard_map/ppermute | solution.py:139
  78.3 1.9 %collective-permute-start.12 = (f32[264,128]{1,0:T(8,128)S(1)}, f32[264,128]{1,0:T(8,128)S(1)}, u32[]{:S(2)}, u32[]{:S(2)}) collective-permute-start(f32[264,128]{1,0:T(8,128)S(1)} %add.71), channel_id=1, source_target_pairs={{0,16},{4,20},{8,24},{12,28},{16,0},{20,4},{24,8},{28,12},{1,17},{... | collective-permute-start | bytes 405512 | tf_op jit(solution)/shard_map/ppermute | solution.py:139
  80.2 5.6 %collective-permute-done.12 = f32[264,128]{1,0:T(8,128)S(1)} collective-permute-done((f32[264,128]{1,0:T(8,128)S(1)}, f32[264,128]{1,0:T(8,128)S(1)}, u32[]{:S(2)}, u32[]{:S(2)}) %collective-permute-start.12) | collective-permute-done | bytes 135200 | tf_op jit(solution)/shard_map/ppermute | solution.py:139
  85.8 2.8 %shard_map.81 = (f32[264,128]{1,0:T(8,128)S(1)}, f32[256,128]{1,0:T(8,128)S(1)}, f32[8,128]{1,0:T(8,128)S(1)}) custom-call(bf16[256,256]{1,0:T(8,128)(2,1)S(1)} %get-tuple-element.53.pick_ref, bf16[256,256]{1,0:T(8,128)(2,1)S(1)} %get-tuple-element.51.put_ref, f32[264,128]{1,0:T(8,128)S(1)} %add.72.summed_ref, ...), custom_call_target="tpu_custom_call" | custom-call | tf_op jit(solution)/shard_map/pallas_call | solution.py:126
  88.6 1.3 %collective-permute-done.13 = f32[264,128]{1,0:T(8,128)S(1)} collective-permute-done((f32[264,128]{1,0:T(8,128)S(1)}, f32[264,128]{1,0:T(8,128)S(1)}, u32[]{:S(2)}, u32[]{:S(2)}) %collective-permute-start.13) | collective-permute-done | bytes 135200 | tf_op jit(solution)/shard_map/ppermute | solution.py:139
  90.0 1.8 %collective-permute-start.14 = (f32[264,128]{1,0:T(8,128)S(1)}, f32[264,128]{1,0:T(8,128)S(1)}, u32[]{:S(2)}, u32[]{:S(2)}) collective-permute-start(f32[264,128]{1,0:T(8,128)S(1)} %add.73), channel_id=1, source_target_pairs={{0,2},{1,3},{2,0},{3,1},{4,6},{5,7},{6,4},{7,5},{8,10},{9,11},{10,... | collective-permute-start | bytes 405512 | tf_op jit(solution)/shard_map/ppermute | solution.py:139
  91.8 3.9 %collective-permute-done.14 = f32[264,128]{1,0:T(8,128)S(1)} collective-permute-done((f32[264,128]{1,0:T(8,128)S(1)}, f32[264,128]{1,0:T(8,128)S(1)}, u32[]{:S(2)}, u32[]{:S(2)}) %collective-permute-start.14) | collective-permute-done | bytes 135200 | tf_op jit(solution)/shard_map/ppermute | solution.py:139
  95.7 1.7 %shard_map.82 = (f32[264,128]{1,0:T(8,128)S(1)}, f32[256,128]{1,0:T(8,128)S(1)}, f32[8,128]{1,0:T(8,128)S(1)}) custom-call(bf16[256,256]{1,0:T(8,128)(2,1)S(1)} %get-tuple-element.52.pick_ref, bf16[256,256]{1,0:T(8,128)(2,1)S(1)} %get-tuple-element.54.put_ref, f32[264,128]{1,0:T(8,128)S(1)} %add.74.summed_ref, f32[256,128]{1,0:T(8,128)S(1)} %get-tuple-element.39.refs_0_, ...), custom_call_target="tpu_custom_call" | custom-call | tf_op jit(solution)/shard_map/pallas_call | solution.py:126
  97.4 1.8 %collective-permute-start.15 = (f32[264,128]{1,0:T(8,128)S(1)}, f32[264,128]{1,0:T(8,128)S(1)}, u32[]{:S(2)}, u32[]{:S(2)}) collective-permute-start(f32[264,128]{1,0:T(8,128)S(1)} %get-tuple-element.41), channel_id=1, source_target_pairs={{0,4},{4,0},{8,12},{12,8},{16,20},{20,16},{24,28},{28,24},{1,5},{5... | collective-permute-start | bytes 405512 | tf_op jit(solution)/shard_map/ppermute | solution.py:139
  99.1 3.3 %collective-permute-done.15 = f32[264,128]{1,0:T(8,128)S(1)} collective-permute-done((f32[264,128]{1,0:T(8,128)S(1)}, f32[264,128]{1,0:T(8,128)S(1)}, u32[]{:S(2)}, u32[]{:S(2)}) %collective-permute-start.15) | collective-permute-done | bytes 135200 | tf_op jit(solution)/shard_map/ppermute | solution.py:139
  102.5 5.0 %collective-permute-done.16 = f32[264,128]{1,0:T(8,128)S(1)} collective-permute-done((f32[264,128]{1,0:T(8,128)S(1)}, f32[264,128]{1,0:T(8,128)S(1)}, u32[]{:S(2)}, u32[]{:S(2)}) %collective-permute-start.16) | collective-permute-done | bytes 135200 | tf_op jit(solution)/shard_map/ppermute | solution.py:139
  107.6 1.3 %collective-permute-start.17 = (f32[264,128]{1,0:T(8,128)S(1)}, f32[264,128]{1,0:T(8,128)S(1)}, u32[]{:S(2)}, u32[]{:S(2)}) collective-permute-start(f32[264,128]{1,0:T(8,128)S(1)} %add.76), channel_id=1, source_target_pairs={{0,16},{4,20},{8,24},{12,28},{16,0},{20,4},{24,8},{28,12},{1,17},{... | collective-permute-start | bytes 405512 | tf_op jit(solution)/shard_map/ppermute | solution.py:139
  108.9 5.9 %collective-permute-done.17 = f32[264,128]{1,0:T(8,128)S(1)} collective-permute-done((f32[264,128]{1,0:T(8,128)S(1)}, f32[264,128]{1,0:T(8,128)S(1)}, u32[]{:S(2)}, u32[]{:S(2)}) %collective-permute-start.17) | collective-permute-done | bytes 135200 | tf_op jit(solution)/shard_map/ppermute | solution.py:139
  114.8 0.8 shard_map.83
  115.6 1.2 collective-permute-done.18
  116.8 1.5 %collective-permute-start.19 = (f32[8,128]{1,0:T(8,128)S(1)}, f32[8,128]{1,0:T(8,128)S(1)}, u32[]{:S(2)}, u32[]{:S(2)}) collective-permute-start(f32[8,128]{1,0:T(8,128)S(1)} %add.78), channel_id=1, source_target_pairs={{0,2},{1,3},{2,0},{3,1},{4,6},{5,7},{6,4},{7,5},{8,10},{9,11},{10,... | collective-permute-start | bytes 12296 | tf_op jit(solution)/shard_map/ppermute | solution.py:139
  118.3 2.1 %collective-permute-done.19 = f32[8,128]{1,0:T(8,128)S(1)} collective-permute-done((f32[8,128]{1,0:T(8,128)S(1)}, f32[8,128]{1,0:T(8,128)S(1)}, u32[]{:S(2)}, u32[]{:S(2)}) %collective-permute-start.19) | collective-permute-done | bytes 4128 | tf_op jit(solution)/shard_map/ppermute | solution.py:139
  120.4 0.8 shard_map.84
  (30 shorter events, 0.7 us)
Async XLA Ops:
  2.2 3.4 %copy-start = (bf16[1,1,256,128,128]{4,3,2,1,0:T(8,128)(2,1)S(1)}, bf16[1,1,256,128,128]{4,3,2,1,0:T(8,128)(2,1)}, u32[]{:S(2)}) copy-start(bf16[1,1,256,128,128]{4,3,2,1,0:T(8,128)(2,1)} %param.5) | copy-start | bytes 25165828
  5.6 0.9 copy-start.2
  6.5 20.8 %copy-start.1 = (bf16[1,1,256,128,128]{4,3,2,1,0:T(8,128)(2,1)S(1)}, bf16[1,1,256,128,128]{4,3,2,1,0:T(8,128)(2,1)}, u32[]{:S(2)}) copy-start(bf16[1,1,256,128,128]{4,3,2,1,0:T(8,128)(2,1)} %param.5) | copy-start | bytes 25165828
  8.1 6.6 %collective-permute-start = (f32[264,128]{1,0:T(8,128)S(1)}, f32[264,128]{1,0:T(8,128)S(1)}, u32[]{:S(2)}, u32[]{:S(2)}) collective-permute-start(f32[264,128]{1,0:T(8,128)S(1)} %shard_map.76), channel_id=1, source_target_pairs={{0,4},{4,0},{8,12},{12,8},{16,20},{20,16},{24,28},{28,24},{1,5},{5... | collective-permute-start | bytes 405512 | tf_op jit(solution)/shard_map/ppermute | solution.py:139
  14.7 5.1 %collective-permute-start.1 = (f32[264,128]{1,0:T(8,128)S(1)}, f32[264,128]{1,0:T(8,128)S(1)}, u32[]{:S(2)}, u32[]{:S(2)}) collective-permute-start(f32[264,128]{1,0:T(8,128)S(1)} %add.60), channel_id=1, source_target_pairs={{0,8},{4,12},{8,0},{12,4},{16,24},{20,28},{24,16},{28,20},{1,9},{5... | collective-permute-start | bytes 405512 | tf_op jit(solution)/shard_map/ppermute | solution.py:139
  19.8 7.5 %collective-permute-start.2 = (f32[264,128]{1,0:T(8,128)S(1)}, f32[264,128]{1,0:T(8,128)S(1)}, u32[]{:S(2)}, u32[]{:S(2)}) collective-permute-start(f32[264,128]{1,0:T(8,128)S(1)} %add.61), channel_id=1, source_target_pairs={{0,16},{4,20},{8,24},{12,28},{16,0},{20,4},{24,8},{28,12},{1,17},{... | collective-permute-start | bytes 405512 | tf_op jit(solution)/shard_map/ppermute | solution.py:139
  30.0 1.4 %collective-permute-start.3 = (f32[264,128]{1,0:T(8,128)S(1)}, f32[264,128]{1,0:T(8,128)S(1)}, u32[]{:S(2)}, u32[]{:S(2)}) collective-permute-start(f32[264,128]{1,0:T(8,128)S(1)} %get-tuple-element.27), channel_id=1, source_target_pairs={{0,1},{1,0},{2,3},{3,2},{4,5},{5,4},{6,7},{7,6},{8,9},{9,8},{10,11... | collective-permute-start | bytes 405512 | tf_op jit(solution)/shard_map/ppermute | solution.py:139
  31.5 5.7 %collective-permute-start.4 = (f32[264,128]{1,0:T(8,128)S(1)}, f32[264,128]{1,0:T(8,128)S(1)}, u32[]{:S(2)}, u32[]{:S(2)}) collective-permute-start(f32[264,128]{1,0:T(8,128)S(1)} %add.63), channel_id=1, source_target_pairs={{0,2},{1,3},{2,0},{3,1},{4,6},{5,7},{6,4},{7,5},{8,10},{9,11},{10,... | collective-permute-start | bytes 405512 | tf_op jit(solution)/shard_map/ppermute | solution.py:139
  38.9 5.1 %collective-permute-start.5 = (f32[264,128]{1,0:T(8,128)S(1)}, f32[264,128]{1,0:T(8,128)S(1)}, u32[]{:S(2)}, u32[]{:S(2)}) collective-permute-start(f32[264,128]{1,0:T(8,128)S(1)} %get-tuple-element.29), channel_id=1, source_target_pairs={{0,4},{4,0},{8,12},{12,8},{16,20},{20,16},{24,28},{28,24},{1,5},{5... | collective-permute-start | bytes 405512 | tf_op jit(solution)/shard_map/ppermute | solution.py:139
  44.0 5.1 %collective-permute-start.6 = (f32[264,128]{1,0:T(8,128)S(1)}, f32[264,128]{1,0:T(8,128)S(1)}, u32[]{:S(2)}, u32[]{:S(2)}) collective-permute-start(f32[264,128]{1,0:T(8,128)S(1)} %add.65), channel_id=1, source_target_pairs={{0,8},{4,12},{8,0},{12,4},{16,24},{20,28},{24,16},{28,20},{1,9},{5... | collective-permute-start | bytes 405512 | tf_op jit(solution)/shard_map/ppermute | solution.py:139
  49.1 7.4 %collective-permute-start.7 = (f32[264,128]{1,0:T(8,128)S(1)}, f32[264,128]{1,0:T(8,128)S(1)}, u32[]{:S(2)}, u32[]{:S(2)}) collective-permute-start(f32[264,128]{1,0:T(8,128)S(1)} %add.66), channel_id=1, source_target_pairs={{0,16},{4,20},{8,24},{12,28},{16,0},{20,4},{24,8},{28,12},{1,17},{... | collective-permute-start | bytes 405512 | tf_op jit(solution)/shard_map/ppermute | solution.py:139
  59.3 1.4 %collective-permute-start.8 = (f32[264,128]{1,0:T(8,128)S(1)}, f32[264,128]{1,0:T(8,128)S(1)}, u32[]{:S(2)}, u32[]{:S(2)}) collective-permute-start(f32[264,128]{1,0:T(8,128)S(1)} %get-tuple-element.32), channel_id=1, source_target_pairs={{0,1},{1,0},{2,3},{3,2},{4,5},{5,4},{6,7},{7,6},{8,9},{9,8},{10,11... | collective-permute-start | bytes 405512 | tf_op jit(solution)/shard_map/ppermute | solution.py:139
  60.7 5.7 %collective-permute-start.9 = (f32[264,128]{1,0:T(8,128)S(1)}, f32[264,128]{1,0:T(8,128)S(1)}, u32[]{:S(2)}, u32[]{:S(2)}) collective-permute-start(f32[264,128]{1,0:T(8,128)S(1)} %add.68), channel_id=1, source_target_pairs={{0,2},{1,3},{2,0},{3,1},{4,6},{5,7},{6,4},{7,5},{8,10},{9,11},{10,... | collective-permute-start | bytes 405512 | tf_op jit(solution)/shard_map/ppermute | solution.py:139
  68.1 5.1 %collective-permute-start.10 = (f32[264,128]{1,0:T(8,128)S(1)}, f32[264,128]{1,0:T(8,128)S(1)}, u32[]{:S(2)}, u32[]{:S(2)}) collective-permute-start(f32[264,128]{1,0:T(8,128)S(1)} %get-tuple-element.35), channel_id=1, source_target_pairs={{0,4},{4,0},{8,12},{12,8},{16,20},{20,16},{24,28},{28,24},{1,5},{5... | collective-permute-start | bytes 405512 | tf_op jit(solution)/shard_map/ppermute | solution.py:139
  73.2 5.1 %collective-permute-start.11 = (f32[264,128]{1,0:T(8,128)S(1)}, f32[264,128]{1,0:T(8,128)S(1)}, u32[]{:S(2)}, u32[]{:S(2)}) collective-permute-start(f32[264,128]{1,0:T(8,128)S(1)} %add.70), channel_id=1, source_target_pairs={{0,8},{4,12},{8,0},{12,4},{16,24},{20,28},{24,16},{28,20},{1,9},{5... | collective-permute-start | bytes 405512 | tf_op jit(solution)/shard_map/ppermute | solution.py:139
  78.3 7.4 %collective-permute-start.12 = (f32[264,128]{1,0:T(8,128)S(1)}, f32[264,128]{1,0:T(8,128)S(1)}, u32[]{:S(2)}, u32[]{:S(2)}) collective-permute-start(f32[264,128]{1,0:T(8,128)S(1)} %add.71), channel_id=1, source_target_pairs={{0,16},{4,20},{8,24},{12,28},{16,0},{20,4},{24,8},{28,12},{1,17},{... | collective-permute-start | bytes 405512 | tf_op jit(solution)/shard_map/ppermute | solution.py:139
  88.5 1.4 %collective-permute-start.13 = (f32[264,128]{1,0:T(8,128)S(1)}, f32[264,128]{1,0:T(8,128)S(1)}, u32[]{:S(2)}, u32[]{:S(2)}) collective-permute-start(f32[264,128]{1,0:T(8,128)S(1)} %get-tuple-element.38), channel_id=1, source_target_pairs={{0,1},{1,0},{2,3},{3,2},{4,5},{5,4},{6,7},{7,6},{8,9},{9,8},{10,11... | collective-permute-start | bytes 405512 | tf_op jit(solution)/shard_map/ppermute | solution.py:139
  90.0 5.7 %collective-permute-start.14 = (f32[264,128]{1,0:T(8,128)S(1)}, f32[264,128]{1,0:T(8,128)S(1)}, u32[]{:S(2)}, u32[]{:S(2)}) collective-permute-start(f32[264,128]{1,0:T(8,128)S(1)} %add.73), channel_id=1, source_target_pairs={{0,2},{1,3},{2,0},{3,1},{4,6},{5,7},{6,4},{7,5},{8,10},{9,11},{10,... | collective-permute-start | bytes 405512 | tf_op jit(solution)/shard_map/ppermute | solution.py:139
  97.4 5.1 %collective-permute-start.15 = (f32[264,128]{1,0:T(8,128)S(1)}, f32[264,128]{1,0:T(8,128)S(1)}, u32[]{:S(2)}, u32[]{:S(2)}) collective-permute-start(f32[264,128]{1,0:T(8,128)S(1)} %get-tuple-element.41), channel_id=1, source_target_pairs={{0,4},{4,0},{8,12},{12,8},{16,20},{20,16},{24,28},{28,24},{1,5},{5... | collective-permute-start | bytes 405512 | tf_op jit(solution)/shard_map/ppermute | solution.py:139
  102.5 5.1 %collective-permute-start.16 = (f32[264,128]{1,0:T(8,128)S(1)}, f32[264,128]{1,0:T(8,128)S(1)}, u32[]{:S(2)}, u32[]{:S(2)}) collective-permute-start(f32[264,128]{1,0:T(8,128)S(1)} %add.75), channel_id=1, source_target_pairs={{0,8},{4,12},{8,0},{12,4},{16,24},{20,28},{24,16},{28,20},{1,9},{5... | collective-permute-start | bytes 405512 | tf_op jit(solution)/shard_map/ppermute | solution.py:139
  107.6 7.2 %collective-permute-start.17 = (f32[264,128]{1,0:T(8,128)S(1)}, f32[264,128]{1,0:T(8,128)S(1)}, u32[]{:S(2)}, u32[]{:S(2)}) collective-permute-start(f32[264,128]{1,0:T(8,128)S(1)} %add.76), channel_id=1, source_target_pairs={{0,16},{4,20},{8,24},{12,28},{16,0},{20,4},{24,8},{28,12},{1,17},{... | collective-permute-start | bytes 405512 | tf_op jit(solution)/shard_map/ppermute | solution.py:139
  115.6 1.2 collective-permute-start.18
  116.8 3.6 %collective-permute-start.19 = (f32[8,128]{1,0:T(8,128)S(1)}, f32[8,128]{1,0:T(8,128)S(1)}, u32[]{:S(2)}, u32[]{:S(2)}) collective-permute-start(f32[8,128]{1,0:T(8,128)S(1)} %add.78), channel_id=1, source_target_pairs={{0,2},{1,3},{2,0},{3,1},{4,6},{5,7},{6,4},{7,5},{8,10},{9,11},{10,... | collective-permute-start | bytes 12296 | tf_op jit(solution)/shard_map/ppermute | solution.py:139

commit v2 on v1

v2 whole, which is shorter than its diff:
```python
import functools

import jax
import jax.numpy as jnp
from jax import lax
from jax.experimental import pallas as pl
from jax.experimental.pallas import tpu as pltpu
from jax.sharding import PartitionSpec as P

TILE_COLS = 256
ITERS = 3
EPS = 1e-06
VMEM_LIMIT = 4 * 1024 * 1024
GROUP = 16
FLIPS = 4
LOADS = (8, 6, 2)
AHEAD = 2
RIDE = 8


def halves(values):
    high = values.astype(jnp.bfloat16)
    low = (values - high.astype(jnp.float32)).astype(jnp.bfloat16)
    return jnp.concatenate([high, low], 0)


def squares(vector):
    rows, width = vector.shape
    return jnp.sum((vector * vector).reshape(rows // RIDE, RIDE, width), 0)


def norm_row(tile):
    total = jnp.sum(jnp.sum(tile, 0, keepdims=True), 1, keepdims=True)
    return jnp.broadcast_to(jnp.sqrt(total + EPS), (1, tile.shape[1]))


def slot_products(pick, vector, blocks_refs, picked_ref, prod_ref, ready=None):
    picked_ref[...] = jnp.dot(
        pick, vector.astype(jnp.bfloat16), preferred_element_type=jnp.float32
    ).astype(jnp.bfloat16)
    slots, width = picked_ref.shape
    shape = (GROUP, GROUP * width)
    mine = lax.broadcasted_iota(jnp.int32, shape, 1) // width == lax.broadcasted_iota(jnp.int32, shape, 0)
    share = blocks_refs[0].shape[0]
    for at in range(0, slots, GROUP):
        if ready:
            ready(at)
        piece = picked_ref[at : at + GROUP]
        spread = jnp.where(mine, jnp.concatenate([piece] * GROUP, 1), jnp.bfloat16(0))
        here = pl.ds(at % share, GROUP)
        stack = blocks_refs[at // share][here].reshape(GROUP * width, width)
        prod_ref[at : at + GROUP] = jnp.dot(spread, stack, preferred_element_type=jnp.float32)


def send(put_ref, vector, prod_ref, out_refs):
    top_ref, low_ref = out_refs
    put = put_ref[...]
    rows, top = put.shape[0], top_ref.shape[0]
    part = jnp.dot(
        jnp.concatenate([put, put], 1), halves(prod_ref[...]), preferred_element_type=jnp.float32
    )
    top_ref[...] = part[:top]
    low_ref[: rows - top] = part[top:]
    low_ref[rows - top :] = squares(vector)


def first_kernel(
    rows_hbm, cols_hbm, count_ref, data_hbm, blocks_hbm,
    top_ref, low_ref, data_ref, pick_row_ref, put_row_ref, pick_col_ref, put_col_ref, blocks_ref,
    picked_ref, prod_ref, rows_ref, cols_ref, small_sems, block_sems,
):
    slots = blocks_ref.shape[0]
    starts = [slots * sum(LOADS[:part]) // sum(LOADS) for part in range(len(LOADS))]
    small = []
    for at, pair in enumerate(((rows_hbm, rows_ref), (cols_hbm, cols_ref), (data_hbm, data_ref))):
        small.append(pltpu.make_async_copy(*pair, small_sems.at[at]))
        small[-1].start()
    copies = []
    for part, start in enumerate(starts):
        piece = pl.ds(start, slots * LOADS[part] // sum(LOADS))
        copies.append(pltpu.make_async_copy(blocks_hbm.at[piece], blocks_ref.at[piece], block_sems.at[part]))
    for copy in copies[:AHEAD]:
        copy.start()
    for copy, index_ref, pick_ref, put_ref in (
        (small[0], rows_ref, pick_row_ref, put_row_ref),
        (small[1], cols_ref, pick_col_ref, put_col_ref),
    ):
        copy.wait()
        shape = put_ref.shape
        live = lax.broadcasted_iota(jnp.int32, shape, 1) < count_ref[0, 0]
        chosen = (lax.broadcasted_iota(jnp.int32, shape, 0) == index_ref[...]) & live
        put = jnp.where(chosen, 1.0, 0.0)
        put_ref[...] = put.astype(jnp.bfloat16)
        pick_ref[...] = put.T.astype(jnp.bfloat16)
    small[2].wait()
    vector = data_ref[...]

    def ready(at):
        if at in starts:
            part = starts.index(at)
            copies[part].wait()
            for copy in copies[part + AHEAD : part + AHEAD + 1]:
                copy.start()

    slot_products(pick_row_ref[...], vector, [blocks_ref], picked_ref, prod_ref, ready)
    send(put_col_ref, vector, prod_ref, (top_ref, low_ref))


def flip_kernel(first, blocks_ref, flipped_ref):
    for slot in range(flipped_ref.shape[0]):
        flipped_ref[slot] = blocks_ref[first + slot].T


def recur(summed_refs, previous):
    top_ref, low_ref = summed_refs
    rows = low_ref.shape[0] - RIDE
    norm = norm_row(low_ref[rows:])
    vector = jnp.concatenate([top_ref[...], low_ref[:rows]], 0) * (1.0 / norm)
    if previous:
        before_ref, before_norm_ref = previous
        vector = vector - (norm / before_norm_ref[:1]) * before_ref[...]
    return vector, norm


def step_kernel(pieces, pick_ref, put_ref, top_in_ref, low_in_ref, *refs):
    blocks_refs, refs = refs[:pieces], refs[pieces:]
    *previous, top_ref, low_ref, vector_ref, norm_ref, picked_ref, prod_ref = refs
    vector, norm = recur((top_in_ref, low_in_ref), previous)
    vector_ref[...] = vector
    norm_ref[...] = jnp.broadcast_to(norm, norm_ref.shape)
    slot_products(pick_ref[...], vector, blocks_refs, picked_ref, prod_ref)
    send(put_ref, vector, prod_ref, (top_ref, low_ref))


def end_kernel(top_in_ref, low_in_ref, before_ref, before_norm_ref, square_ref, vector_ref, norm_ref):
    vector, norm = recur((top_in_ref, low_in_ref), (before_ref, before_norm_ref))
    square_ref[...] = squares(vector)
    vector_ref[...] = vector
    norm_ref[...] = jnp.broadcast_to(norm, norm_ref.shape)


def update_kernel(steps, data_vector_ref, *refs):
    alphas, refs = [r[:1] for r in refs[:steps]], refs[steps:]
    betas, refs = [r[:1] for r in refs[: steps + 1]], refs[steps + 1 :]
    models, (solution_ref, search_ref, basis_ref, coef_ref) = refs[:steps], refs[steps:]
    basis_ref[...] = data_vector_ref[...] * (1.0 / betas[-1])
    search = models[0][...] * (1.0 / alphas[0])
    solution = jnp.zeros_like(search)
    phibar, rhobar = betas[0], alphas[0]
    for step in range(steps):
        rho = jnp.sqrt(rhobar * rhobar + betas[step + 1] * betas[step + 1])
        cosine, sine = rhobar / rho, betas[step + 1] / rho
        solution = solution + (cosine * phibar / rho) * search
        phibar = sine * phibar
        if step + 1 < steps:
            rhobar = -cosine * alphas[step + 1]
            search = models[step + 1][...] * (1.0 / alphas[step + 1]) - (sine * alphas[step + 1] / rho) * search
    solution_ref[...] = solution
    search_ref[...] = search
    coef_ref[...] = jnp.broadcast_to(sine / rho, coef_ref.shape)


def search_kernel(square_ref, vector_ref, search_ref, coef_ref, out_ref):
    alpha = norm_row(square_ref[...])
    out_ref[...] = vector_ref[...] * (1.0 / alpha) - (coef_ref[:1] * alpha) * search_ref[...]


VMEM = pl.BlockSpec(memory_space=pltpu.VMEM)


def call(kernel, outs, args, scratch=(), specs=None):
    return pl.pallas_call(
        kernel,
        out_shape=[jax.ShapeDtypeStruct(o, jnp.float32) if isinstance(o, tuple) else o for o in outs],
        in_specs=specs or [VMEM] * len(args),
        out_specs=[VMEM] * len(outs),
        scratch_shapes=list(scratch),
        cost_estimate=pl.CostEstimate(flops=2 * 10**9, bytes_accessed=2**20, transcendentals=0),
        compiler_params=pltpu.CompilerParams(vmem_limit_bytes=VMEM_LIMIT),
    )(*args)


def all_sum(chunks, orders, axis, size):
    chunks = list(chunks)
    for stage in range(len(orders[0])):
        for at, order in enumerate(orders):
            pairs = [(i, i ^ order[stage]) for i in range(size)]
            chunks[at] = chunks[at] + lax.ppermute(chunks[at], axis, pairs)
    return chunks


def per_device(n_row, n_col, blocks, block_rows, block_cols, counts, data):
    tile_blocks = blocks[0, 0]
    slots, _, width = tile_blocks.shape
    data = data.reshape(-1, width)
    tile_rows, tile_cols = data.shape[0], TILE_COLS
    row_bits = [1 << k for k in range(n_row.bit_length() - 1)]
    col_bits = [1 << k for k in range(n_col.bit_length() - 1)]
    row_orders, col_orders = [row_bits, row_bits], [col_bits[::-1], col_bits]
    tile, model, basis = (RIDE, width), (tile_cols, width), (tile_rows, width)

    def chunks(rows):
        return [(rows // 2, width), (rows - rows // 2 + RIDE, width)]

    def coded(*shape):
        return jax.ShapeDtypeStruct(shape, jnp.bfloat16)

    scratch = [pltpu.VMEM((slots, width), jnp.bfloat16), pltpu.VMEM((slots, width), jnp.float32)]
    hbm = pl.BlockSpec(memory_space=pltpu.HBM)
    inputs = [
        pltpu.with_memory_space_constraint(a, pltpu.HBM) for a in (block_rows[0], block_cols[0], data, tile_blocks)
    ]
    *parts, data, pick_row, put_row, pick_col, put_col, tile_blocks = call(
        first_kernel,
        [
            *chunks(tile_cols), basis, coded(slots, tile_rows), coded(tile_rows, slots),
            coded(slots, tile_cols), coded(tile_cols, slots),
            coded(*tile_blocks.shape),
        ],
        [inputs[0], inputs[1], counts, inputs[2], inputs[3]],
        [
            *scratch, pltpu.VMEM((1, slots), jnp.int32), pltpu.VMEM((1, slots), jnp.int32),
            pltpu.SemaphoreType.DMA((3,)), pltpu.SemaphoreType.DMA((len(LOADS),)),
        ],
        [hbm, hbm, pl.BlockSpec(memory_space=pltpu.SMEM), hbm, hbm],
    )
    share = slots // FLIPS
    flipped = [
        call(functools.partial(flip_kernel, at * share), [coded(share, width, width)], [tile_blocks])[0]
        for at in range(FLIPS)
    ]
    summed = all_sum(parts, row_orders, "row", n_row)
    alphas, betas, models = [], [], []
    bases = [data]
    for step in range(ITERS):
        previous = [models[-1], alphas[-1]] if models else []
        *parts, vector, beta = call(
            functools.partial(step_kernel, FLIPS),
            [*chunks(tile_rows), model, tile],
            [pick_col, put_row, *summed, *flipped, *previous],
            scratch,
        )
        models.append(vector)
        betas.append(beta)
        summed = all_sum(parts, col_orders, "col", n_col)
        *parts, vector, alpha = call(
            functools.partial(step_kernel, 1),
            [*chunks(tile_cols), basis, tile],
            [pick_row, put_col, *summed, tile_blocks, bases[-1], beta],
            scratch,
        )
        bases.append(vector)
        alphas.append(alpha)
        summed = all_sum(parts, row_orders, "row", n_row)
    square, vector, beta = call(end_kernel, [tile, model, tile], [*summed, models[-1], alphas[-1]])
    solution, search, data_basis, coef = call(
        functools.partial(update_kernel, ITERS),
        [model, model, basis, tile],
        [bases[-1], *alphas, *betas, beta, *models],
    )
    (square,) = all_sum([square], [col_bits], "col", n_col)
    (search,) = call(search_kernel, [model], [square, vector, search, coef])
    return solution.reshape(-1), search.reshape(-1), data_basis.reshape(-1)


def solution(mesh):
    in_specs = (
        P("row", "col", None, None, None),
        P("row", "col", None),
        P("row", "col", None),
        P("row", "col"),
        P("row"),
    )
    out_specs = (P("col"), P("col"), P("row"))
    return jax.shard_map(
        functools.partial(per_device, mesh.shape["row"], mesh.shape["col"]),
        mesh=mesh,
        in_specs=in_specs,
        out_specs=out_specs,
        check_vma=False,
    )
```

time: 121 us -> 110 us (0.909)
  waiting for transfers between devices: 70.5 us -> 45 us
  starting transfers between devices: 27.3 us -> 43.8 us
  local copies, waits for them, and re-layouts: 4.28 us -> 0 us
  Pallas kernels: 16.5 us -> 18.6 us
    ppermute x20 -> x38, waiting for transfers between devices: 70.5 us -> 45 us  [all_sum(): chunks[at] = chunks[at] + lax.ppermute(chunks[at], axis, pairs)]
    ppermute x20 -> x38, starting transfers between devices: 27.3 us -> 43.8 us  [all_sum(): chunks[at] = chunks[at] + lax.ppermute(chunks[at], axis, pairs)]
    unnamed x6 -> x0, local copies, waits for them, and re-layouts: 4.28 us -> none
    pallas_call x9 -> x14, Pallas kernels: 16.5 us -> 18.6 us  [call(): pl.pallas_call(kernel, out_shape=[jax.ShapeDtypeStruct(o, jnp.float32) if...]
  transfers between devices with their start and end apart: 20 -> 38, of which waited for: 20 -> 29; matrix products, arithmetic and copies ran while one was open for 0% -> 0% of each run, Pallas kernels for 0% -> 3%
where the time goes in v2:
time: 110 us; the launch traced here: 109 us
  waiting for transfers between devices  45 us (41%)
  starting transfers between devices  43.8 us (40%)
  Pallas kernels  18.6 us (17%)
  between operations  1.6 us (1%)
    ppermute x38, waiting for transfers between devices, all_sum(): chunks[at] = chunks[at] + lax.ppermute(chunks[at], axis, pairs)  45 us
    ppermute x38, starting transfers between devices, all_sum(): chunks[at] = chunks[at] + lax.ppermute(chunks[at], axis, pairs)  43.8 us
    pallas_call x14, Pallas kernels, call(): pl.pallas_call(kernel, out_shape=[jax.ShapeDtypeStruct(o, jnp.float32) if...  18.6 us
  transfers between devices with their start and end apart: 38, of which 29 were waited for; matrix products, arithmetic and copies ran while one was open for 0% of the time, Pallas kernels for 3%

profile of v2, /device:TPU:0, one launch (start us, length us, event | category | flops | bytes accessed | tf_op | source)
XLA Modules:
  0.0 109.4 jit_solution(11643993831408619418)
XLA Ops:
  1.3 4.3 %shard_map.76 = (f32[128,128]{1,0:T(8,128)S(1)}, f32[136,128]{1,0:T(8,128)S(1)}, f32[256,128]{1,0:T(8,128)S(1)}, bf16[256,256]{1,0:T(8,128)(2,1)S(1)}, bf16[256,...) custom-call(s32[1,256]{1,0:T(1,128)} %bitcast.9, ...), custom_call_target="tpu_custom_call" | custom-call | flops 2000000000 | bytes 1048576 | tf_op jit(solution)/shard_map/pallas_call | solution.py:172
  5.6 3.0 %collective-permute-start = (f32[128,128]{1,0:T(8,128)S(1)}, f32[128,128]{1,0:T(8,128)S(1)}, u32[]{:S(2)}, u32[]{:S(2)}) collective-permute-start(f32[128,128]{1,0:T(8,128)S(1)} %get-tuple-element.46), channel_id=1, source_target_pairs={{0,4},{4,0},{8,12},{12,8},{16,20},{20,16},{24,28},{28,24},{1,5},{5... | collective-permute-start | bytes 196616 | tf_op jit(solution)/shard_map/ppermute | solution.py:188
  9.9 1.1 collective-permute-done
  11.0 2.7 %collective-permute-start.1 = (f32[128,128]{1,0:T(8,128)S(1)}, f32[128,128]{1,0:T(8,128)S(1)}, u32[]{:S(2)}, u32[]{:S(2)}) collective-permute-start(f32[128,128]{1,0:T(8,128)S(1)} %add.114), channel_id=1, source_target_pairs={{0,8},{4,12},{8,0},{12,4},{16,24},{20,28},{24,16},{28,20},{1,9},{5... | collective-permute-start | bytes 196616 | tf_op jit(solution)/shard_map/ppermute | solution.py:188
  13.7 0.9 collective-permute-start.4
  16.1 3.5 %collective-permute-start.2 = (f32[128,128]{1,0:T(8,128)S(1)}, f32[128,128]{1,0:T(8,128)S(1)}, u32[]{:S(2)}, u32[]{:S(2)}) collective-permute-start(f32[128,128]{1,0:T(8,128)S(1)} %add.115), channel_id=1, source_target_pairs={{0,16},{4,20},{8,24},{12,28},{16,0},{20,4},{24,8},{28,12},{1,17},{... | collective-permute-start | bytes 196616 | tf_op jit(solution)/shard_map/ppermute | solution.py:188
  19.6 1.2 %collective-permute-start.5 = (f32[136,128]{1,0:T(8,128)S(1)}, f32[136,128]{1,0:T(8,128)S(1)}, u32[]{:S(2)}, u32[]{:S(2)}) collective-permute-start(f32[136,128]{1,0:T(8,128)S(1)} %add.118), channel_id=1, source_target_pairs={{0,16},{4,20},{8,24},{12,28},{16,0},{20,4},{24,8},{28,12},{1,17},{... | collective-permute-start | bytes 208904 | tf_op jit(solution)/shard_map/ppermute | solution.py:188
  21.4 1.7 %collective-permute-done.2 = f32[128,128]{1,0:T(8,128)S(1)} collective-permute-done((f32[128,128]{1,0:T(8,128)S(1)}, f32[128,128]{1,0:T(8,128)S(1)}, u32[]{:S(2)}, u32[]{:S(2)}) %collective-permute-start.2) | collective-permute-done | bytes 65568 | tf_op jit(solution)/shard_map/ppermute | solution.py:188
  23.0 2.6 %collective-permute-done.5 = f32[136,128]{1,0:T(8,128)S(1)} collective-permute-done((f32[136,128]{1,0:T(8,128)S(1)}, f32[136,128]{1,0:T(8,128)S(1)}, u32[]{:S(2)}, u32[]{:S(2)}) %collective-permute-start.5) | collective-permute-done | bytes 69664 | tf_op jit(solution)/shard_map/ppermute | solution.py:188
  25.6 1.7 %shard_map.81 = (f32[128,128]{1,0:T(8,128)S(1)}, f32[136,128]{1,0:T(8,128)S(1)}, f32[256,128]{1,0:T(8,128)S(1)}, f32[8,128]{1,0:T(8,128)S(1)}) custom-call(bf16[256,256]{1,0:T(8,128)(2,1)S(1)} %get-tuple-element.44.pick_ref, bf16[256,256]{1,0:T(8,128)(2,1)S(1)} %get-tuple-element.45.put_ref, f32[128,128]{1,0:T(8,128)S(1)} %add.116.top_in_ref, ...), custom_call_target="tpu_custom_call" | custom-call | flops 2000000000 | bytes 1048576 | tf_op jit(solution)/shard_map/pallas_call | solution.py:172
  27.4 1.6 %collective-permute-start.6 = (f32[128,128]{1,0:T(8,128)S(1)}, f32[128,128]{1,0:T(8,128)S(1)}, u32[]{:S(2)}, u32[]{:S(2)}) collective-permute-start(f32[128,128]{1,0:T(8,128)S(1)} %get-tuple-element.49), channel_id=1, source_target_pairs={{0,2},{1,3},{2,0},{3,1},{4,6},{5,7},{6,4},{7,5},{8,10},{9,11},{10,... | collective-permute-start | bytes 196616 | tf_op jit(solution)/shard_map/ppermute | solution.py:188
  29.0 1.2 %collective-permute-start.9 = (f32[136,128]{1,0:T(8,128)S(1)}, f32[136,128]{1,0:T(8,128)S(1)}, u32[]{:S(2)}, u32[]{:S(2)}) collective-permute-start(f32[136,128]{1,0:T(8,128)S(1)} %add.122), channel_id=1, source_target_pairs={{0,2},{1,3},{2,0},{3,1},{4,6},{5,7},{6,4},{7,5},{8,10},{9,11},{10,... | collective-permute-start | bytes 208904 | tf_op jit(solution)/shard_map/ppermute | solution.py:188
  30.2 1.8 %collective-permute-done.6 = f32[128,128]{1,0:T(8,128)S(1)} collective-permute-done((f32[128,128]{1,0:T(8,128)S(1)}, f32[128,128]{1,0:T(8,128)S(1)}, u32[]{:S(2)}, u32[]{:S(2)}) %collective-permute-start.6) | collective-permute-done | bytes 65568 | tf_op jit(solution)/shard_map/ppermute | solution.py:188
  32.1 1.2 %collective-permute-done.7 = f32[128,128]{1,0:T(8,128)S(1)} collective-permute-done((f32[128,128]{1,0:T(8,128)S(1)}, f32[128,128]{1,0:T(8,128)S(1)}, u32[]{:S(2)}, u32[]{:S(2)}) %collective-permute-start.7) | collective-permute-done | bytes 65568 | tf_op jit(solution)/shard_map/ppermute | solution.py:188
  33.4 1.7 %shard_map.82 = (f32[128,128]{1,0:T(8,128)S(1)}, f32[136,128]{1,0:T(8,128)S(1)}, f32[256,128]{1,0:T(8,128)S(1)}, f32[8,128]{1,0:T(8,128)S(1)}) custom-call(bf16[256,256]{1,0:T(8,128)(2,1)S(1)} %get-tuple-element.42.pick_ref, bf16[256,256]{1,0:T(8,128)(2,1)S(1)} %get-tuple-element.43.put_ref, f32[128,128]{1,0:T(8,128)S(1)} %add.121.top_in_ref, ...), custom_call_target="tpu_custom_call" | custom-call | flops 2000000000 | bytes 1048576 | tf_op jit(solution)/shard_map/pallas_call | solution.py:172
  35.3 1.9 %collective-permute-start.10 = (f32[128,128]{1,0:T(8,128)S(1)}, f32[128,128]{1,0:T(8,128)S(1)}, u32[]{:S(2)}, u32[]{:S(2)}) collective-permute-start(f32[128,128]{1,0:T(8,128)S(1)} %get-tuple-element.53), channel_id=1, source_target_pairs={{0,4},{4,0},{8,12},{12,8},{16,20},{20,16},{24,28},{28,24},{1,5},{5... | collective-permute-start | bytes 196616 | tf_op jit(solution)/shard_map/ppermute | solution.py:188
  37.2 2.9 %collective-permute-done.13 = f32[136,128]{1,0:T(8,128)S(1)} collective-permute-done((f32[136,128]{1,0:T(8,128)S(1)}, f32[136,128]{1,0:T(8,128)S(1)}, u32[]{:S(2)}, u32[]{:S(2)}) %collective-permute-start.13) | collective-permute-done | bytes 69664 | tf_op jit(solution)/shard_map/ppermute | solution.py:188
  40.8 1.5 %collective-permute-start.11 = (f32[128,128]{1,0:T(8,128)S(1)}, f32[128,128]{1,0:T(8,128)S(1)}, u32[]{:S(2)}, u32[]{:S(2)}) collective-permute-start(f32[128,128]{1,0:T(8,128)S(1)} %add.124), channel_id=1, source_target_pairs={{0,8},{4,12},{8,0},{12,4},{16,24},{20,28},{24,16},{28,20},{1,9},{5... | collective-permute-start | bytes 196616 | tf_op jit(solution)/shard_map/ppermute | solution.py:188
  42.2 2.2 %collective-permute-done.14 = f32[136,128]{1,0:T(8,128)S(1)} collective-permute-done((f32[136,128]{1,0:T(8,128)S(1)}, f32[136,128]{1,0:T(8,128)S(1)}, u32[]{:S(2)}, u32[]{:S(2)}) %collective-permute-start.14) | collective-permute-done | bytes 69664 | tf_op jit(solution)/shard_map/ppermute | solution.py:188
  45.2 2.4 %collective-permute-start.12 = (f32[128,128]{1,0:T(8,128)S(1)}, f32[128,128]{1,0:T(8,128)S(1)}, u32[]{:S(2)}, u32[]{:S(2)}) collective-permute-start(f32[128,128]{1,0:T(8,128)S(1)} %add.125), channel_id=1, source_target_pairs={{0,16},{4,20},{8,24},{12,28},{16,0},{20,4},{24,8},{28,12},{1,17},{... | collective-permute-start | bytes 196616 | tf_op jit(solution)/shard_map/ppermute | solution.py:188
  47.5 3.5 %collective-permute-done.12 = f32[128,128]{1,0:T(8,128)S(1)} collective-permute-done((f32[128,128]{1,0:T(8,128)S(1)}, f32[128,128]{1,0:T(8,128)S(1)}, u32[]{:S(2)}, u32[]{:S(2)}) %collective-permute-start.12) | collective-permute-done | bytes 65568 | tf_op jit(solution)/shard_map/ppermute | solution.py:188
  51.1 1.7 %shard_map.83 = (f32[128,128]{1,0:T(8,128)S(1)}, f32[136,128]{1,0:T(8,128)S(1)}, f32[256,128]{1,0:T(8,128)S(1)}, f32[8,128]{1,0:T(8,128)S(1)}) custom-call(bf16[256,256]{1,0:T(8,128)(2,1)S(1)} %get-tuple-element.44.pick_ref, bf16[256,256]{1,0:T(8,128)(2,1)S(1)} %get-tuple-element.45.put_ref, f32[128,128]{1,0:T(8,128)S(1)} %add.126.top_in_ref, ...), custom_call_target="tpu_custom_call" | custom-call | flops 2000000000 | bytes 1048576 | tf_op jit(solution)/shard_map/pallas_call | solution.py:172
  52.9 1.9 %collective-permute-start.16 = (f32[128,128]{1,0:T(8,128)S(1)}, f32[128,128]{1,0:T(8,128)S(1)}, u32[]{:S(2)}, u32[]{:S(2)}) collective-permute-start(f32[128,128]{1,0:T(8,128)S(1)} %get-tuple-element.57), channel_id=1, source_target_pairs={{0,2},{1,3},{2,0},{3,1},{4,6},{5,7},{6,4},{7,5},{8,10},{9,11},{10,... | collective-permute-start | bytes 196616 | tf_op jit(solution)/shard_map/ppermute | solution.py:188
  54.8 1.2 %collective-permute-start.19 = (f32[136,128]{1,0:T(8,128)S(1)}, f32[136,128]{1,0:T(8,128)S(1)}, u32[]{:S(2)}, u32[]{:S(2)}) collective-permute-start(f32[136,128]{1,0:T(8,128)S(1)} %add.132), channel_id=1, source_target_pairs={{0,2},{1,3},{2,0},{3,1},{4,6},{5,7},{6,4},{7,5},{8,10},{9,11},{10,... | collective-permute-start | bytes 208904 | tf_op jit(solution)/shard_map/ppermute | solution.py:188
  56.1 1.4 %collective-permute-done.16 = f32[128,128]{1,0:T(8,128)S(1)} collective-permute-done((f32[128,128]{1,0:T(8,128)S(1)}, f32[128,128]{1,0:T(8,128)S(1)}, u32[]{:S(2)}, u32[]{:S(2)}) %collective-permute-start.16) | collective-permute-done | bytes 65568 | tf_op jit(solution)/shard_map/ppermute | solution.py:188
  57.6 1.2 %collective-permute-done.17 = f32[128,128]{1,0:T(8,128)S(1)} collective-permute-done((f32[128,128]{1,0:T(8,128)S(1)}, f32[128,128]{1,0:T(8,128)S(1)}, u32[]{:S(2)}, u32[]{:S(2)}) %collective-permute-start.17) | collective-permute-done | bytes 65568 | tf_op jit(solution)/shard_map/ppermute | solution.py:188
  59.2 1.7 %shard_map.84 = (f32[128,128]{1,0:T(8,128)S(1)}, f32[136,128]{1,0:T(8,128)S(1)}, f32[256,128]{1,0:T(8,128)S(1)}, f32[8,128]{1,0:T(8,128)S(1)}) custom-call(bf16[256,256]{1,0:T(8,128)(2,1)S(1)} %get-tuple-element.42.pick_ref, bf16[256,256]{1,0:T(8,128)(2,1)S(1)} %get-tuple-element.43.put_ref, f32[128,128]{1,0:T(8,128)S(1)} %add.131.top_in_ref, ...), custom_call_target="tpu_custom_call" | custom-call | flops 2000000000 | bytes 1048576 | tf_op jit(solution)/shard_map/pallas_call | solution.py:172
  61.3 1.7 %collective-permute-start.20 = (f32[128,128]{1,0:T(8,128)S(1)}, f32[128,128]{1,0:T(8,128)S(1)}, u32[]{:S(2)}, u32[]{:S(2)}) collective-permute-start(f32[128,128]{1,0:T(8,128)S(1)} %get-tuple-element.61), channel_id=1, source_target_pairs={{0,4},{4,0},{8,12},{12,8},{16,20},{20,16},{24,28},{28,24},{1,5},{5... | collective-permute-start | bytes 196616 | tf_op jit(solution)/shard_map/ppermute | solution.py:188
  63.0 2.6 %collective-permute-done.23 = f32[136,128]{1,0:T(8,128)S(1)} collective-permute-done((f32[136,128]{1,0:T(8,128)S(1)}, f32[136,128]{1,0:T(8,128)S(1)}, u32[]{:S(2)}, u32[]{:S(2)}) %collective-permute-start.23) | collective-permute-done | bytes 69664 | tf_op jit(solution)/shard_map/ppermute | solution.py:188
  65.6 1.3 %collective-permute-start.24 = (f32[136,128]{1,0:T(8,128)S(1)}, f32[136,128]{1,0:T(8,128)S(1)}, u32[]{:S(2)}, u32[]{:S(2)}) collective-permute-start(f32[136,128]{1,0:T(8,128)S(1)} %add.137), channel_id=1, source_target_pairs={{0,8},{4,12},{8,0},{12,4},{16,24},{20,28},{24,16},{28,20},{1,9},{5... | collective-permute-start | bytes 208904 | tf_op jit(solution)/shard_map/ppermute | solution.py:188
  67.7 2.2 %collective-permute-done.24 = f32[136,128]{1,0:T(8,128)S(1)} collective-permute-done((f32[136,128]{1,0:T(8,128)S(1)}, f32[136,128]{1,0:T(8,128)S(1)}, u32[]{:S(2)}, u32[]{:S(2)}) %collective-permute-start.24) | collective-permute-done | bytes 69664 | tf_op jit(solution)/shard_map/ppermute | solution.py:188
  69.9 1.7 %collective-permute-start.25 = (f32[136,128]{1,0:T(8,128)S(1)}, f32[136,128]{1,0:T(8,128)S(1)}, u32[]{:S(2)}, u32[]{:S(2)}) collective-permute-start(f32[136,128]{1,0:T(8,128)S(1)} %add.138), channel_id=1, source_target_pairs={{0,16},{4,20},{8,24},{12,28},{16,0},{20,4},{24,8},{28,12},{1,17},{... | collective-permute-start | bytes 208904 | tf_op jit(solution)/shard_map/ppermute | solution.py:188
  72.0 1.0 collective-permute-start.22
  73.0 4.9 %collective-permute-done.22 = f32[128,128]{1,0:T(8,128)S(1)} collective-permute-done((f32[128,128]{1,0:T(8,128)S(1)}, f32[128,128]{1,0:T(8,128)S(1)}, u32[]{:S(2)}, u32[]{:S(2)}) %collective-permute-start.22) | collective-permute-done | bytes 65568 | tf_op jit(solution)/shard_map/ppermute | solution.py:188
  78.0 1.8 %shard_map.85 = (f32[128,128]{1,0:T(8,128)S(1)}, f32[136,128]{1,0:T(8,128)S(1)}, f32[256,128]{1,0:T(8,128)S(1)}, f32[8,128]{1,0:T(8,128)S(1)}) custom-call(bf16[256,256]{1,0:T(8,128)(2,1)S(1)} %get-tuple-element.44.pick_ref, bf16[256,256]{1,0:T(8,128)(2,1)S(1)} %get-tuple-element.45.put_ref, f32[128,128]{1,0:T(8,128)S(1)} %add.136.top_in_ref, ...), custom_call_target="tpu_custom_call" | custom-call | flops 2000000000 | bytes 1048576 | tf_op jit(solution)/shard_map/pallas_call | solution.py:172
  79.9 2.2 %collective-permute-start.26 = (f32[128,128]{1,0:T(8,128)S(1)}, f32[128,128]{1,0:T(8,128)S(1)}, u32[]{:S(2)}, u32[]{:S(2)}) collective-permute-start(f32[128,128]{1,0:T(8,128)S(1)} %get-tuple-element.65), channel_id=1, source_target_pairs={{0,2},{1,3},{2,0},{3,1},{4,6},{5,7},{6,4},{7,5},{8,10},{9,11},{10,... | collective-permute-start | bytes 196616 | tf_op jit(solution)/shard_map/ppermute | solution.py:188
  82.1 1.2 %collective-permute-start.29 = (f32[136,128]{1,0:T(8,128)S(1)}, f32[136,128]{1,0:T(8,128)S(1)}, u32[]{:S(2)}, u32[]{:S(2)}) collective-permute-start(f32[136,128]{1,0:T(8,128)S(1)} %add.142), channel_id=1, source_target_pairs={{0,2},{1,3},{2,0},{3,1},{4,6},{5,7},{6,4},{7,5},{8,10},{9,11},{10,... | collective-permute-start | bytes 208904 | tf_op jit(solution)/shard_map/ppermute | solution.py:188
  83.4 1.4 %collective-permute-done.26 = f32[128,128]{1,0:T(8,128)S(1)} collective-permute-done((f32[128,128]{1,0:T(8,128)S(1)}, f32[128,128]{1,0:T(8,128)S(1)}, u32[]{:S(2)}, u32[]{:S(2)}) %collective-permute-start.26) | collective-permute-done | bytes 65568 | tf_op jit(solution)/shard_map/ppermute | solution.py:188
  84.9 1.2 %collective-permute-done.27 = f32[128,128]{1,0:T(8,128)S(1)} collective-permute-done((f32[128,128]{1,0:T(8,128)S(1)}, f32[128,128]{1,0:T(8,128)S(1)}, u32[]{:S(2)}, u32[]{:S(2)}) %collective-permute-start.27) | collective-permute-done | bytes 65568 | tf_op jit(solution)/shard_map/ppermute | solution.py:188
  86.5 1.7 %shard_map.86 = (f32[128,128]{1,0:T(8,128)S(1)}, f32[136,128]{1,0:T(8,128)S(1)}, f32[256,128]{1,0:T(8,128)S(1)}, f32[8,128]{1,0:T(8,128)S(1)}) custom-call(bf16[256,256]{1,0:T(8,128)(2,1)S(1)} %get-tuple-element.42.pick_ref, bf16[256,256]{1,0:T(8,128)(2,1)S(1)} %get-tuple-element.43.put_ref, f32[128,128]{1,0:T(8,128)S(1)} %add.141.top_in_ref, ...), custom_call_target="tpu_custom_call" | custom-call | flops 2000000000 | bytes 1048576 | tf_op jit(solution)/shard_map/pallas_call | solution.py:172
  89.0 1.3 %collective-permute-start.30 = (f32[128,128]{1,0:T(8,128)S(1)}, f32[128,128]{1,0:T(8,128)S(1)}, u32[]{:S(2)}, u32[]{:S(2)}) collective-permute-start(f32[128,128]{1,0:T(8,128)S(1)} %get-tuple-element.71), channel_id=1, source_target_pairs={{0,4},{4,0},{8,12},{12,8},{16,20},{20,16},{24,28},{28,24},{1,5},{5... | collective-permute-start | bytes 196616 | tf_op jit(solution)/shard_map/ppermute | solution.py:188
  90.3 2.6 %collective-permute-done.33 = f32[136,128]{1,0:T(8,128)S(1)} collective-permute-done((f32[136,128]{1,0:T(8,128)S(1)}, f32[136,128]{1,0:T(8,128)S(1)}, u32[]{:S(2)}, u32[]{:S(2)}) %collective-permute-start.33) | collective-permute-done | bytes 69664 | tf_op jit(solution)/shard_map/ppermute | solution.py:188
  93.6 1.5 %collective-permute-start.31 = (f32[128,128]{1,0:T(8,128)S(1)}, f32[128,128]{1,0:T(8,128)S(1)}, u32[]{:S(2)}, u32[]{:S(2)}) collective-permute-start(f32[128,128]{1,0:T(8,128)S(1)} %add.144), channel_id=1, source_target_pairs={{0,8},{4,12},{8,0},{12,4},{16,24},{20,28},{24,16},{28,20},{1,9},{5... | collective-permute-start | bytes 196616 | tf_op jit(solution)/shard_map/ppermute | solution.py:188
  95.1 2.2 %collective-permute-done.34 = f32[136,128]{1,0:T(8,128)S(1)} collective-permute-done((f32[136,128]{1,0:T(8,128)S(1)}, f32[136,128]{1,0:T(8,128)S(1)}, u32[]{:S(2)}, u32[]{:S(2)}) %collective-permute-start.34) | collective-permute-done | bytes 69664 | tf_op jit(solution)/shard_map/ppermute | solution.py:188
  98.0 2.4 %collective-permute-start.32 = (f32[128,128]{1,0:T(8,128)S(1)}, f32[128,128]{1,0:T(8,128)S(1)}, u32[]{:S(2)}, u32[]{:S(2)}) collective-permute-start(f32[128,128]{1,0:T(8,128)S(1)} %add.145), channel_id=1, source_target_pairs={{0,16},{4,20},{8,24},{12,28},{16,0},{20,4},{24,8},{28,12},{1,17},{... | collective-permute-start | bytes 196616 | tf_op jit(solution)/shard_map/ppermute | solution.py:188
  100.3 3.1 %collective-permute-done.32 = f32[128,128]{1,0:T(8,128)S(1)} collective-permute-done((f32[128,128]{1,0:T(8,128)S(1)}, f32[128,128]{1,0:T(8,128)S(1)}, u32[]{:S(2)}, u32[]{:S(2)}) %collective-permute-start.32) | collective-permute-done | bytes 65568 | tf_op jit(solution)/shard_map/ppermute | solution.py:188
  103.7 1.2 %collective-permute-done.36 = f32[8,128]{1,0:T(8,128)S(1)} collective-permute-done((f32[8,128]{1,0:T(8,128)S(1)}, f32[8,128]{1,0:T(8,128)S(1)}, u32[]{:S(2)}, u32[]{:S(2)}) %collective-permute-start.36) | collective-permute-done | bytes 4128 | tf_op jit(solution)/shard_map/ppermute | solution.py:188
  104.9 2.2 %collective-permute-start.37 = (f32[8,128]{1,0:T(8,128)S(1)}, f32[8,128]{1,0:T(8,128)S(1)}, u32[]{:S(2)}, u32[]{:S(2)}) collective-permute-start(f32[8,128]{1,0:T(8,128)S(1)} %add.150), channel_id=1, source_target_pairs={{0,2},{1,3},{2,0},{3,1},{4,6},{5,7},{6,4},{7,5},{8,10},{9,11},{10,... | collective-permute-start | bytes 12296 | tf_op jit(solution)/shard_map/ppermute | solution.py:188
  (80 shorter events, 12.8 us)
Async XLA Ops:
  5.6 5.4 %collective-permute-start = (f32[128,128]{1,0:T(8,128)S(1)}, f32[128,128]{1,0:T(8,128)S(1)}, u32[]{:S(2)}, u32[]{:S(2)}) collective-permute-start(f32[128,128]{1,0:T(8,128)S(1)} %get-tuple-element.46), channel_id=1, source_target_pairs={{0,4},{4,0},{8,12},{12,8},{16,20},{20,16},{24,28},{28,24},{1,5},{5... | collective-permute-start | bytes 196616 | tf_op jit(solution)/shard_map/ppermute | solution.py:188
  8.7 5.0 %collective-permute-start.3 = (f32[136,128]{1,0:T(8,128)S(1)}, f32[136,128]{1,0:T(8,128)S(1)}, u32[]{:S(2)}, u32[]{:S(2)}) collective-permute-start(f32[136,128]{1,0:T(8,128)S(1)} %get-tuple-element.47), channel_id=1, source_target_pairs={{0,4},{4,0},{8,12},{12,8},{16,20},{20,16},{24,28},{28,24},{1,5},{5... | collective-permute-start | bytes 208904 | tf_op jit(solution)/shard_map/ppermute | solution.py:188
  11.0 5.1 %collective-permute-start.1 = (f32[128,128]{1,0:T(8,128)S(1)}, f32[128,128]{1,0:T(8,128)S(1)}, u32[]{:S(2)}, u32[]{:S(2)}) collective-permute-start(f32[128,128]{1,0:T(8,128)S(1)} %add.114), channel_id=1, source_target_pairs={{0,8},{4,12},{8,0},{12,4},{16,24},{20,28},{24,16},{28,20},{1,9},{5... | collective-permute-start | bytes 196616 | tf_op jit(solution)/shard_map/ppermute | solution.py:188
  13.7 5.9 %collective-permute-start.4 = (f32[136,128]{1,0:T(8,128)S(1)}, f32[136,128]{1,0:T(8,128)S(1)}, u32[]{:S(2)}, u32[]{:S(2)}) collective-permute-start(f32[136,128]{1,0:T(8,128)S(1)} %add.117), channel_id=1, source_target_pairs={{0,8},{4,12},{8,0},{12,4},{16,24},{20,28},{24,16},{28,20},{1,9},{5... | collective-permute-start | bytes 208904 | tf_op jit(solution)/shard_map/ppermute | solution.py:188
  16.1 6.9 %collective-permute-start.2 = (f32[128,128]{1,0:T(8,128)S(1)}, f32[128,128]{1,0:T(8,128)S(1)}, u32[]{:S(2)}, u32[]{:S(2)}) collective-permute-start(f32[128,128]{1,0:T(8,128)S(1)} %add.115), channel_id=1, source_target_pairs={{0,16},{4,20},{8,24},{12,28},{16,0},{20,4},{24,8},{28,12},{1,17},{... | collective-permute-start | bytes 196616 | tf_op jit(solution)/shard_map/ppermute | solution.py:188
  19.6 6.0 %collective-permute-start.5 = (f32[136,128]{1,0:T(8,128)S(1)}, f32[136,128]{1,0:T(8,128)S(1)}, u32[]{:S(2)}, u32[]{:S(2)}) collective-permute-start(f32[136,128]{1,0:T(8,128)S(1)} %add.118), channel_id=1, source_target_pairs={{0,16},{4,20},{8,24},{12,28},{16,0},{20,4},{24,8},{28,12},{1,17},{... | collective-permute-start | bytes 208904 | tf_op jit(solution)/shard_map/ppermute | solution.py:188
  27.3 1.7 %collective-permute-start.8 = (f32[136,128]{1,0:T(8,128)S(1)}, f32[136,128]{1,0:T(8,128)S(1)}, u32[]{:S(2)}, u32[]{:S(2)}) collective-permute-start(f32[136,128]{1,0:T(8,128)S(1)} %get-tuple-element.50), channel_id=1, source_target_pairs={{0,1},{1,0},{2,3},{3,2},{4,5},{5,4},{6,7},{7,6},{8,9},{9,8},{10,11... | collective-permute-start | bytes 208904 | tf_op jit(solution)/shard_map/ppermute | solution.py:188
  27.4 4.6 %collective-permute-start.6 = (f32[128,128]{1,0:T(8,128)S(1)}, f32[128,128]{1,0:T(8,128)S(1)}, u32[]{:S(2)}, u32[]{:S(2)}) collective-permute-start(f32[128,128]{1,0:T(8,128)S(1)} %get-tuple-element.49), channel_id=1, source_target_pairs={{0,2},{1,3},{2,0},{3,1},{4,6},{5,7},{6,4},{7,5},{8,10},{9,11},{10,... | collective-permute-start | bytes 196616 | tf_op jit(solution)/shard_map/ppermute | solution.py:188
  29.0 4.4 %collective-permute-start.9 = (f32[136,128]{1,0:T(8,128)S(1)}, f32[136,128]{1,0:T(8,128)S(1)}, u32[]{:S(2)}, u32[]{:S(2)}) collective-permute-start(f32[136,128]{1,0:T(8,128)S(1)} %add.122), channel_id=1, source_target_pairs={{0,2},{1,3},{2,0},{3,1},{4,6},{5,7},{6,4},{7,5},{8,10},{9,11},{10,... | collective-permute-start | bytes 208904 | tf_op jit(solution)/shard_map/ppermute | solution.py:188
  32.0 1.3 %collective-permute-start.7 = (f32[128,128]{1,0:T(8,128)S(1)}, f32[128,128]{1,0:T(8,128)S(1)}, u32[]{:S(2)}, u32[]{:S(2)}) collective-permute-start(f32[128,128]{1,0:T(8,128)S(1)} %add.120), channel_id=1, source_target_pairs={{0,1},{1,0},{2,3},{3,2},{4,5},{5,4},{6,7},{7,6},{8,9},{9,8},{10,11... | collective-permute-start | bytes 196616 | tf_op jit(solution)/shard_map/ppermute | solution.py:188
  35.1 5.0 %collective-permute-start.13 = (f32[136,128]{1,0:T(8,128)S(1)}, f32[136,128]{1,0:T(8,128)S(1)}, u32[]{:S(2)}, u32[]{:S(2)}) collective-permute-start(f32[136,128]{1,0:T(8,128)S(1)} %get-tuple-element.54), channel_id=1, source_target_pairs={{0,4},{4,0},{8,12},{12,8},{16,20},{20,16},{24,28},{28,24},{1,5},{5... | collective-permute-start | bytes 208904 | tf_op jit(solution)/shard_map/ppermute | solution.py:188
  35.3 5.5 %collective-permute-start.10 = (f32[128,128]{1,0:T(8,128)S(1)}, f32[128,128]{1,0:T(8,128)S(1)}, u32[]{:S(2)}, u32[]{:S(2)}) collective-permute-start(f32[128,128]{1,0:T(8,128)S(1)} %get-tuple-element.53), channel_id=1, source_target_pairs={{0,4},{4,0},{8,12},{12,8},{16,20},{20,16},{24,28},{28,24},{1,5},{5... | collective-permute-start | bytes 196616 | tf_op jit(solution)/shard_map/ppermute | solution.py:188
  40.1 4.4 %collective-permute-start.14 = (f32[136,128]{1,0:T(8,128)S(1)}, f32[136,128]{1,0:T(8,128)S(1)}, u32[]{:S(2)}, u32[]{:S(2)}) collective-permute-start(f32[136,128]{1,0:T(8,128)S(1)} %add.127), channel_id=1, source_target_pairs={{0,8},{4,12},{8,0},{12,4},{16,24},{20,28},{24,16},{28,20},{1,9},{5... | collective-permute-start | bytes 208904 | tf_op jit(solution)/shard_map/ppermute | solution.py:188
  40.8 4.4 %collective-permute-start.11 = (f32[128,128]{1,0:T(8,128)S(1)}, f32[128,128]{1,0:T(8,128)S(1)}, u32[]{:S(2)}, u32[]{:S(2)}) collective-permute-start(f32[128,128]{1,0:T(8,128)S(1)} %add.124), channel_id=1, source_target_pairs={{0,8},{4,12},{8,0},{12,4},{16,24},{20,28},{24,16},{28,20},{1,9},{5... | collective-permute-start | bytes 196616 | tf_op jit(solution)/shard_map/ppermute | solution.py:188
  44.5 6.6 %collective-permute-start.15 = (f32[136,128]{1,0:T(8,128)S(1)}, f32[136,128]{1,0:T(8,128)S(1)}, u32[]{:S(2)}, u32[]{:S(2)}) collective-permute-start(f32[136,128]{1,0:T(8,128)S(1)} %add.128), channel_id=1, source_target_pairs={{0,16},{4,20},{8,24},{12,28},{16,0},{20,4},{24,8},{28,12},{1,17},{... | collective-permute-start | bytes 208904 | tf_op jit(solution)/shard_map/ppermute | solution.py:188
  45.2 5.9 %collective-permute-start.12 = (f32[128,128]{1,0:T(8,128)S(1)}, f32[128,128]{1,0:T(8,128)S(1)}, u32[]{:S(2)}, u32[]{:S(2)}) collective-permute-start(f32[128,128]{1,0:T(8,128)S(1)} %add.125), channel_id=1, source_target_pairs={{0,16},{4,20},{8,24},{12,28},{16,0},{20,4},{24,8},{28,12},{1,17},{... | collective-permute-start | bytes 196616 | tf_op jit(solution)/shard_map/ppermute | solution.py:188
  52.8 2.0 %collective-permute-start.18 = (f32[136,128]{1,0:T(8,128)S(1)}, f32[136,128]{1,0:T(8,128)S(1)}, u32[]{:S(2)}, u32[]{:S(2)}) collective-permute-start(f32[136,128]{1,0:T(8,128)S(1)} %get-tuple-element.58), channel_id=1, source_target_pairs={{0,1},{1,0},{2,3},{3,2},{4,5},{5,4},{6,7},{7,6},{8,9},{9,8},{10,11... | collective-permute-start | bytes 208904 | tf_op jit(solution)/shard_map/ppermute | solution.py:188
  52.9 4.6 %collective-permute-start.16 = (f32[128,128]{1,0:T(8,128)S(1)}, f32[128,128]{1,0:T(8,128)S(1)}, u32[]{:S(2)}, u32[]{:S(2)}) collective-permute-start(f32[128,128]{1,0:T(8,128)S(1)} %get-tuple-element.57), channel_id=1, source_target_pairs={{0,2},{1,3},{2,0},{3,1},{4,6},{5,7},{6,4},{7,5},{8,10},{9,11},{10,... | collective-permute-start | bytes 196616 | tf_op jit(solution)/shard_map/ppermute | solution.py:188
  54.8 4.4 %collective-permute-start.19 = (f32[136,128]{1,0:T(8,128)S(1)}, f32[136,128]{1,0:T(8,128)S(1)}, u32[]{:S(2)}, u32[]{:S(2)}) collective-permute-start(f32[136,128]{1,0:T(8,128)S(1)} %add.132), channel_id=1, source_target_pairs={{0,2},{1,3},{2,0},{3,1},{4,6},{5,7},{6,4},{7,5},{8,10},{9,11},{10,... | collective-permute-start | bytes 208904 | tf_op jit(solution)/shard_map/ppermute | solution.py:188
  57.5 1.3 %collective-permute-start.17 = (f32[128,128]{1,0:T(8,128)S(1)}, f32[128,128]{1,0:T(8,128)S(1)}, u32[]{:S(2)}, u32[]{:S(2)}) collective-permute-start(f32[128,128]{1,0:T(8,128)S(1)} %add.130), channel_id=1, source_target_pairs={{0,1},{1,0},{2,3},{3,2},{4,5},{5,4},{6,7},{7,6},{8,9},{9,8},{10,11... | collective-permute-start | bytes 196616 | tf_op jit(solution)/shard_map/ppermute | solution.py:188
  60.9 4.7 %collective-permute-start.23 = (f32[136,128]{1,0:T(8,128)S(1)}, f32[136,128]{1,0:T(8,128)S(1)}, u32[]{:S(2)}, u32[]{:S(2)}) collective-permute-start(f32[136,128]{1,0:T(8,128)S(1)} %get-tuple-element.62), channel_id=1, source_target_pairs={{0,4},{4,0},{8,12},{12,8},{16,20},{20,16},{24,28},{28,24},{1,5},{5... | collective-permute-start | bytes 208904 | tf_op jit(solution)/shard_map/ppermute | solution.py:188
  61.3 5.6 %collective-permute-start.20 = (f32[128,128]{1,0:T(8,128)S(1)}, f32[128,128]{1,0:T(8,128)S(1)}, u32[]{:S(2)}, u32[]{:S(2)}) collective-permute-start(f32[128,128]{1,0:T(8,128)S(1)} %get-tuple-element.61), channel_id=1, source_target_pairs={{0,4},{4,0},{8,12},{12,8},{16,20},{20,16},{24,28},{28,24},{1,5},{5... | collective-permute-start | bytes 196616 | tf_op jit(solution)/shard_map/ppermute | solution.py:188
  65.6 4.4 %collective-permute-start.24 = (f32[136,128]{1,0:T(8,128)S(1)}, f32[136,128]{1,0:T(8,128)S(1)}, u32[]{:S(2)}, u32[]{:S(2)}) collective-permute-start(f32[136,128]{1,0:T(8,128)S(1)} %add.137), channel_id=1, source_target_pairs={{0,8},{4,12},{8,0},{12,4},{16,24},{20,28},{24,16},{28,20},{1,9},{5... | collective-permute-start | bytes 208904 | tf_op jit(solution)/shard_map/ppermute | solution.py:188
  66.9 5.1 %collective-permute-start.21 = (f32[128,128]{1,0:T(8,128)S(1)}, f32[128,128]{1,0:T(8,128)S(1)}, u32[]{:S(2)}, u32[]{:S(2)}) collective-permute-start(f32[128,128]{1,0:T(8,128)S(1)} %add.134), channel_id=1, source_target_pairs={{0,8},{4,12},{8,0},{12,4},{16,24},{20,28},{24,16},{28,20},{1,9},{5... | collective-permute-start | bytes 196616 | tf_op jit(solution)/shard_map/ppermute | solution.py:188
  69.9 8.0 %collective-permute-start.25 = (f32[136,128]{1,0:T(8,128)S(1)}, f32[136,128]{1,0:T(8,128)S(1)}, u32[]{:S(2)}, u32[]{:S(2)}) collective-permute-start(f32[136,128]{1,0:T(8,128)S(1)} %add.138), channel_id=1, source_target_pairs={{0,16},{4,20},{8,24},{12,28},{16,0},{20,4},{24,8},{28,12},{1,17},{... | collective-permute-start | bytes 208904 | tf_op jit(solution)/shard_map/ppermute | solution.py:188
  72.0 5.9 %collective-permute-start.22 = (f32[128,128]{1,0:T(8,128)S(1)}, f32[128,128]{1,0:T(8,128)S(1)}, u32[]{:S(2)}, u32[]{:S(2)}) collective-permute-start(f32[128,128]{1,0:T(8,128)S(1)} %add.135), channel_id=1, source_target_pairs={{0,16},{4,20},{8,24},{12,28},{16,0},{20,4},{24,8},{28,12},{1,17},{... | collective-permute-start | bytes 196616 | tf_op jit(solution)/shard_map/ppermute | solution.py:188
  79.8 2.3 %collective-permute-start.28 = (f32[136,128]{1,0:T(8,128)S(1)}, f32[136,128]{1,0:T(8,128)S(1)}, u32[]{:S(2)}, u32[]{:S(2)}) collective-permute-start(f32[136,128]{1,0:T(8,128)S(1)} %get-tuple-element.66), channel_id=1, source_target_pairs={{0,1},{1,0},{2,3},{3,2},{4,5},{5,4},{6,7},{7,6},{8,9},{9,8},{10,11... | collective-permute-start | bytes 208904 | tf_op jit(solution)/shard_map/ppermute | solution.py:188
  79.9 4.9 %collective-permute-start.26 = (f32[128,128]{1,0:T(8,128)S(1)}, f32[128,128]{1,0:T(8,128)S(1)}, u32[]{:S(2)}, u32[]{:S(2)}) collective-permute-start(f32[128,128]{1,0:T(8,128)S(1)} %get-tuple-element.65), channel_id=1, source_target_pairs={{0,2},{1,3},{2,0},{3,1},{4,6},{5,7},{6,4},{7,5},{8,10},{9,11},{10,... | collective-permute-start | bytes 196616 | tf_op jit(solution)/shard_map/ppermute | solution.py:188
  82.1 4.4 %collective-permute-start.29 = (f32[136,128]{1,0:T(8,128)S(1)}, f32[136,128]{1,0:T(8,128)S(1)}, u32[]{:S(2)}, u32[]{:S(2)}) collective-permute-start(f32[136,128]{1,0:T(8,128)S(1)} %add.142), channel_id=1, source_target_pairs={{0,2},{1,3},{2,0},{3,1},{4,6},{5,7},{6,4},{7,5},{8,10},{9,11},{10,... | collective-permute-start | bytes 208904 | tf_op jit(solution)/shard_map/ppermute | solution.py:188
  84.8 1.3 %collective-permute-start.27 = (f32[128,128]{1,0:T(8,128)S(1)}, f32[128,128]{1,0:T(8,128)S(1)}, u32[]{:S(2)}, u32[]{:S(2)}) collective-permute-start(f32[128,128]{1,0:T(8,128)S(1)} %add.140), channel_id=1, source_target_pairs={{0,1},{1,0},{2,3},{3,2},{4,5},{5,4},{6,7},{7,6},{8,9},{9,8},{10,11... | collective-permute-start | bytes 196616 | tf_op jit(solution)/shard_map/ppermute | solution.py:188
  88.2 4.7 %collective-permute-start.33 = (f32[136,128]{1,0:T(8,128)S(1)}, f32[136,128]{1,0:T(8,128)S(1)}, u32[]{:S(2)}, u32[]{:S(2)}) collective-permute-start(f32[136,128]{1,0:T(8,128)S(1)} %get-tuple-element.72), channel_id=1, source_target_pairs={{0,4},{4,0},{8,12},{12,8},{16,20},{20,16},{24,28},{28,24},{1,5},{5... | collective-permute-start | bytes 208904 | tf_op jit(solution)/shard_map/ppermute | solution.py:188
  89.0 4.6 %collective-permute-start.30 = (f32[128,128]{1,0:T(8,128)S(1)}, f32[128,128]{1,0:T(8,128)S(1)}, u32[]{:S(2)}, u32[]{:S(2)}) collective-permute-start(f32[128,128]{1,0:T(8,128)S(1)} %get-tuple-element.71), channel_id=1, source_target_pairs={{0,4},{4,0},{8,12},{12,8},{16,20},{20,16},{24,28},{28,24},{1,5},{5... | collective-permute-start | bytes 196616 | tf_op jit(solution)/shard_map/ppermute | solution.py:188
  92.9 4.4 %collective-permute-start.34 = (f32[136,128]{1,0:T(8,128)S(1)}, f32[136,128]{1,0:T(8,128)S(1)}, u32[]{:S(2)}, u32[]{:S(2)}) collective-permute-start(f32[136,128]{1,0:T(8,128)S(1)} %add.147), channel_id=1, source_target_pairs={{0,8},{4,12},{8,0},{12,4},{16,24},{20,28},{24,16},{28,20},{1,9},{5... | collective-permute-start | bytes 208904 | tf_op jit(solution)/shard_map/ppermute | solution.py:188
  93.6 4.4 %collective-permute-start.31 = (f32[128,128]{1,0:T(8,128)S(1)}, f32[128,128]{1,0:T(8,128)S(1)}, u32[]{:S(2)}, u32[]{:S(2)}) collective-permute-start(f32[128,128]{1,0:T(8,128)S(1)} %add.144), channel_id=1, source_target_pairs={{0,8},{4,12},{8,0},{12,4},{16,24},{20,28},{24,16},{28,20},{1,9},{5... | collective-permute-start | bytes 196616 | tf_op jit(solution)/shard_map/ppermute | solution.py:188
  97.3 6.2 %collective-permute-start.35 = (f32[136,128]{1,0:T(8,128)S(1)}, f32[136,128]{1,0:T(8,128)S(1)}, u32[]{:S(2)}, u32[]{:S(2)}) collective-permute-start(f32[136,128]{1,0:T(8,128)S(1)} %add.148), channel_id=1, source_target_pairs={{0,16},{4,20},{8,24},{12,28},{16,0},{20,4},{24,8},{28,12},{1,17},{... | collective-permute-start | bytes 208904 | tf_op jit(solution)/shard_map/ppermute | solution.py:188
  98.0 5.5 %collective-permute-start.32 = (f32[128,128]{1,0:T(8,128)S(1)}, f32[128,128]{1,0:T(8,128)S(1)}, u32[]{:S(2)}, u32[]{:S(2)}) collective-permute-start(f32[128,128]{1,0:T(8,128)S(1)} %add.145), channel_id=1, source_target_pairs={{0,16},{4,20},{8,24},{12,28},{16,0},{20,4},{24,8},{28,12},{1,17},{... | collective-permute-start | bytes 196616 | tf_op jit(solution)/shard_map/ppermute | solution.py:188
  103.6 1.2 %collective-permute-start.36 = (f32[8,128]{1,0:T(8,128)S(1)}, f32[8,128]{1,0:T(8,128)S(1)}, u32[]{:S(2)}, u32[]{:S(2)}) collective-permute-start(f32[8,128]{1,0:T(8,128)S(1)} %get-tuple-element.76), channel_id=1, source_target_pairs={{0,1},{1,0},{2,3},{3,2},{4,5},{5,4},{6,7},{7,6},{8,9},{9,8},{10,11... | collective-permute-start | bytes 12296 | tf_op jit(solution)/shard_map/ppermute | solution.py:188
  104.9 3.8 %collective-permute-start.37 = (f32[8,128]{1,0:T(8,128)S(1)}, f32[8,128]{1,0:T(8,128)S(1)}, u32[]{:S(2)}, u32[]{:S(2)}) collective-permute-start(f32[8,128]{1,0:T(8,128)S(1)} %add.150), channel_id=1, source_target_pairs={{0,2},{1,3},{2,0},{3,1},{4,6},{5,7},{6,4},{7,5},{8,10},{9,11},{10,... | collective-permute-start | bytes 12296 | tf_op jit(solution)/shard_map/ppermute | solution.py:188

commit v3 on v2

v3 whole, which is shorter than its diff:
```python
import functools

import jax
import jax.numpy as jnp
from jax import lax
from jax.experimental import pallas as pl
from jax.experimental.pallas import tpu as pltpu
from jax.sharding import PartitionSpec as P


TILE_COLS = 256
ITERS = 3
EPS = 1e-06
VMEM_LIMIT = 4 * 1024 * 1024
GROUP = 16
PIECES = 2
LOADS = (8, 6, 2)
AHEAD = 2
TURNS = {"row": (1, 0), "col": (1, 0)}
RIDE = 8


def halves(values):
    high = values.astype(jnp.bfloat16)
    low = (values - high.astype(jnp.float32)).astype(jnp.bfloat16)
    return jnp.concatenate([high, low], 0)


def squares(vector):
    rows, width = vector.shape
    return jnp.sum((vector * vector).reshape(rows // RIDE, RIDE, width), 0)


def norm_row(tile):
    total = jnp.sum(jnp.sum(tile, 0, keepdims=True), 1, keepdims=True)
    return jnp.broadcast_to(jnp.sqrt(total + EPS), (1, tile.shape[1]))


def pick_pieces(pick, vector):
    return jnp.dot(
        pick, vector.astype(jnp.bfloat16), preferred_element_type=jnp.float32
    ).astype(jnp.bfloat16)


def group_products(picked, stack):
    group, width = picked.shape
    shape = (group, group * width)
    mine = lax.broadcasted_iota(jnp.int32, shape, 1) // width == lax.broadcasted_iota(jnp.int32, shape, 0)
    spread = jnp.where(mine, jnp.concatenate([picked] * group, 1), jnp.bfloat16(0))
    return jnp.dot(spread, stack.reshape(group * width, width), preferred_element_type=jnp.float32)


def put_products(put, products):
    return jnp.dot(
        jnp.concatenate([put, put], 1), halves(products), preferred_element_type=jnp.float32
    )


def first_kernel(
    rows_hbm, cols_hbm, count_ref, data_hbm, blocks_hbm,
    top_ref, low_ref, data_ref, pick_row_ref, put_row_ref, pick_col_ref, put_col_ref, order_ref, number_f_ref, number_a_ref, blocks_ref,
    prod_ref, rows_ref, cols_ref, small_sems, block_sems,
):
    slots = blocks_ref.shape[0]
    starts = [slots * sum(LOADS[:part]) // sum(LOADS) for part in range(len(LOADS))]
    small = []
    for at, pair in enumerate(((rows_hbm, rows_ref), (cols_hbm, cols_ref), (data_hbm, data_ref))):
        small.append(pltpu.make_async_copy(*pair, small_sems.at[at]))
        small[-1].start()
    copies = []
    for part, start in enumerate(starts):
        piece = pl.ds(start, slots * LOADS[part] // sum(LOADS))
        copies.append(pltpu.make_async_copy(blocks_hbm.at[piece], blocks_ref.at[piece], block_sems.at[part]))
    for copy in copies[:AHEAD]:
        copy.start()
    square = (slots, slots)
    slot = lax.broadcasted_iota(jnp.int32, (1, slots), 1)
    down = lax.broadcasted_iota(jnp.int32, square, 0)
    live = slot < count_ref[0, 0]

    def one_hot(index_ref, size):
        places = lax.broadcasted_iota(jnp.int32, (size, slots), 0)
        put = jnp.where((places == index_ref[...]) & live, 1.0, 0.0)
        return put.T.astype(jnp.bfloat16), put.astype(jnp.bfloat16)

    def ordered(index_ref, size):
        late = index_ref[...] < size // 2
        key = (jnp.where(live, jnp.where(late, 2, 0), 1) * slots + slot).astype(jnp.float32)
        keys = jnp.broadcast_to(key, square)
        place = jnp.sum(jnp.where(keys.T < keys, 1.0, 0.0), 0, keepdims=True).astype(jnp.int32)
        moved = jnp.where(down == place, 1.0, 0.0).astype(jnp.bfloat16)
        ids = jnp.broadcast_to(slot, (RIDE, slots)).astype(jnp.float32).astype(jnp.bfloat16)
        order = lax.dot_general(ids, moved, (((1,), (1,)), ((), ())), preferred_element_type=jnp.float32)
        number = jnp.sum(jnp.where(live & late, 1.0, 0.0), 1, keepdims=True)
        return moved, order[:1].astype(jnp.int32), jnp.broadcast_to(number, number_f_ref.shape).astype(jnp.int32)

    for copy in small[:2]:
        copy.wait()
    sizes = data_ref.shape[0], put_col_ref.shape[0]
    pick_row, put_row = one_hot(rows_ref, sizes[0])
    pick_col, put_col = one_hot(cols_ref, sizes[1])
    moved_f, order_ref[:1], number_f_ref[...] = ordered(cols_ref, sizes[1])
    moved_a, order_ref[1:], number_a_ref[...] = ordered(rows_ref, sizes[0])
    for moved, pick, put, to_pick_ref, to_put_ref in (
        (moved_f, pick_col, put_row, pick_col_ref, put_row_ref),
        (moved_a, pick_row, put_col, pick_row_ref, put_col_ref),
    ):
        to_pick_ref[...] = jnp.dot(moved, pick, preferred_element_type=jnp.float32).astype(jnp.bfloat16)
        to_put_ref[...] = lax.dot_general(
            put, moved, (((1,), (1,)), ((), ())), preferred_element_type=jnp.float32
        ).astype(jnp.bfloat16)
    small[2].wait()
    vector = data_ref[...]
    picked = pick_pieces(pick_row, vector)
    for at in range(0, slots, GROUP):
        if at in starts:
            part = starts.index(at)
            copies[part].wait()
            for copy in copies[part + AHEAD : part + AHEAD + 1]:
                copy.start()
        here = slice(at, at + GROUP)
        prod_ref[here] = group_products(picked[here], blocks_ref[here])
    part = put_products(put_col, prod_ref[...])
    rows, top = part.shape[0], top_ref.shape[0]
    top_ref[...] = part[:top]
    low_ref[: rows - top] = part[top:]
    low_ref[rows - top :] = squares(vector)


def arrange_kernel(first, order_ref, blocks_ref, plain_ref, flipped_ref):
    for slot in range(flipped_ref.shape[0]):
        flipped_ref[slot] = blocks_ref[order_ref[0, first + slot]].T
        plain_ref[slot] = blocks_ref[order_ref[1, first + slot]]


def recur(summed, norm, previous, here):
    vector = summed * (1.0 / norm)
    if previous:
        before_ref, before_norm_ref = previous
        vector = vector - (norm / before_norm_ref[:1]) * before_ref[here]
    return vector


def stack_of(blocks_refs, at):
    share = blocks_refs[0].shape[0]
    return blocks_refs[at // share][at % share : at % share + GROUP]


def early_kernel(pieces, pick_ref, low_in_ref, *refs):
    blocks_refs, refs = refs[:pieces], refs[pieces:]
    *previous, vector_ref, norm_ref, early_ref = refs
    rows, early = vector_ref.shape[0], early_ref.shape[0]
    norm = norm_row(low_in_ref[rows:])
    norm_ref[...] = jnp.broadcast_to(norm, norm_ref.shape)
    size = pick_ref.shape[1]
    vector = recur(low_in_ref[:rows], norm, previous, slice(size - rows, size))
    vector_ref[...] = vector
    picked = pick_pieces(pick_ref[:early, size - rows :], vector)
    for at in range(0, early, GROUP):
        early_ref[at : at + GROUP] = group_products(picked[at : at + GROUP], stack_of(blocks_refs, at))


def rest_kernel(pieces, number_ref, pick_ref, put_ref, top_in_ref, low_vector_ref, norm_ref, early_ref, *refs):
    blocks_refs, refs = refs[:pieces], refs[pieces:]
    *previous, top_ref, low_ref, vector_ref, picked_ref, prod_ref = refs
    top = top_in_ref.shape[0]
    vector_ref[:top] = recur(top_in_ref[...], norm_ref[:1], previous, slice(0, top))
    vector_ref[top:] = low_vector_ref[...]
    vector = vector_ref[...]
    slots, early, share = pick_ref.shape[0], early_ref.shape[0], blocks_refs[0].shape[0]
    picked_ref[...] = pick_pieces(pick_ref[...], vector)
    prod_ref[:early] = early_ref[...]
    for at in range(early, slots, GROUP):
        prod_ref[at : at + GROUP] = group_products(picked_ref[at : at + GROUP], stack_of(blocks_refs, at))

    @pl.when(jnp.max(number_ref[...]) > slots - early)
    def _():
        for piece, blocks_ref in enumerate(blocks_refs[: pl.cdiv(early, share)]):

            @pl.loop(0, min(share, early - piece * share) // GROUP)
            def _(group):
                at = pl.multiple_of(group * GROUP, GROUP)
                here = pl.ds(pl.multiple_of(piece * share + at, GROUP), GROUP)
                prod_ref[here] = group_products(picked_ref[here], blocks_ref[pl.ds(at, GROUP)])

    part = put_products(put_ref[...], prod_ref[...])
    rows, top = part.shape[0], top_ref.shape[0]
    top_ref[...] = part[:top]
    low_ref[: rows - top] = part[top:]
    low_ref[rows - top :] = squares(vector)


def end_kernel(top_in_ref, low_in_ref, before_ref, before_norm_ref, square_ref, vector_ref, norm_ref):
    rows = low_in_ref.shape[0] - RIDE
    norm = norm_row(low_in_ref[rows:])
    summed = jnp.concatenate([top_in_ref[...], low_in_ref[:rows]], 0)
    vector = recur(summed, norm, (before_ref, before_norm_ref), slice(None))
    square_ref[...] = squares(vector)
    vector_ref[...] = vector
    norm_ref[...] = jnp.broadcast_to(norm, norm_ref.shape)


def update_kernel(steps, data_vector_ref, *refs):
    alphas, refs = [r[:1] for r in refs[:steps]], refs[steps:]
    betas, refs = [r[:1] for r in refs[: steps + 1]], refs[steps + 1 :]
    models, (solution_ref, search_ref, basis_ref, coef_ref) = refs[:steps], refs[steps:]
    basis_ref[...] = data_vector_ref[...] * (1.0 / betas[-1])
    search = models[0][...] * (1.0 / alphas[0])
    solution = jnp.zeros_like(search)
    phibar, rhobar = betas[0], alphas[0]
    for step in range(steps):
        rho = jnp.sqrt(rhobar * rhobar + betas[step + 1] * betas[step + 1])
        cosine, sine = rhobar / rho, betas[step + 1] / rho
        solution = solution + (cosine * phibar / rho) * search
        phibar = sine * phibar
        if step + 1 < steps:
            rhobar = -cosine * alphas[step + 1]
            search = models[step + 1][...] * (1.0 / alphas[step + 1]) - (sine * alphas[step + 1] / rho) * search
    solution_ref[...] = solution
    search_ref[...] = search
    coef_ref[...] = jnp.broadcast_to(sine / rho, coef_ref.shape)


def search_kernel(square_ref, vector_ref, search_ref, coef_ref, out_ref):
    alpha = norm_row(square_ref[...])
    out_ref[...] = vector_ref[...] * (1.0 / alpha) - (coef_ref[:1] * alpha) * search_ref[...]


VMEM = pl.BlockSpec(memory_space=pltpu.VMEM)


def call(kernel, outs, args, scratch=(), specs=None):
    return pl.pallas_call(
        kernel,
        out_shape=[jax.ShapeDtypeStruct(o, jnp.float32) if isinstance(o, tuple) else o for o in outs],
        in_specs=specs or [VMEM] * len(args),
        out_specs=[VMEM] * len(outs),
        scratch_shapes=list(scratch),
        cost_estimate=pl.CostEstimate(flops=2 * 10**9, bytes_accessed=2**20, transcendentals=0),
        compiler_params=pltpu.CompilerParams(vmem_limit_bytes=VMEM_LIMIT),
    )(*args)


def all_sum(chunks, orders, turns, axis, size):
    chunks = list(chunks)
    stages = len(orders[0])
    for stage in range(stages):
        for at in turns:
            pairs = [(i, i ^ orders[at][stage]) for i in range(size)]
            other = lax.ppermute(chunks[at], axis, pairs)
            chunks[at] = chunks[at] + other
    return chunks


def per_device(n_row, n_col, blocks, block_rows, block_cols, counts, data):
    tile_blocks = blocks[0, 0]
    slots, _, width = tile_blocks.shape
    data = data.reshape(-1, width)
    tile_rows, tile_cols = data.shape[0], TILE_COLS
    row_bits = [1 << k for k in range(n_row.bit_length() - 1)]
    col_bits = [1 << k for k in range(n_col.bit_length() - 1)]
    row_orders, col_orders = [row_bits, row_bits], [col_bits[::-1], col_bits]
    tile, model, basis = (RIDE, width), (tile_cols, width), (tile_rows, width)

    def chunks(rows):
        return [(rows // 2, width), (rows - rows // 2 + RIDE, width)]

    def coded(*shape):
        return jax.ShapeDtypeStruct(shape, jnp.bfloat16)

    products = pltpu.VMEM((slots, width), jnp.float32)
    hbm, smem = pl.BlockSpec(memory_space=pltpu.HBM), pl.BlockSpec(memory_space=pltpu.SMEM)
    inputs = [
        pltpu.with_memory_space_constraint(a, pltpu.HBM) for a in (block_rows[0], block_cols[0], data, tile_blocks)
    ]
    *parts, data, pick_row, put_row, pick_col, put_col, order, number_f, number_a, tile_blocks = call(
        first_kernel,
        [
            *chunks(tile_cols), basis, coded(slots, tile_rows), coded(tile_rows, slots),
            coded(slots, tile_cols), coded(tile_cols, slots),
            *[jax.ShapeDtypeStruct(shape, jnp.int32) for shape in ((2, slots), tile, tile)], coded(*tile_blocks.shape),
        ],
        [inputs[0], inputs[1], counts, inputs[2], inputs[3]],
        [
            products, pltpu.VMEM((1, slots), jnp.int32), pltpu.VMEM((1, slots), jnp.int32),
            pltpu.SemaphoreType.DMA((3,)), pltpu.SemaphoreType.DMA((len(LOADS),)),
        ],
        [hbm, hbm, smem, hbm, hbm],
    )
    share = slots // PIECES
    plain, flipped = [], []
    for at in range(PIECES):
        pieces = call(
            functools.partial(arrange_kernel, at * share),
            [coded(share, width, width)] * 2,
            [order, tile_blocks],
            specs=[smem, VMEM],
        )
        plain.append(pieces[0])
        flipped.append(pieces[1])
    early = (slots // GROUP // 2 - 1) * GROUP

    def product(number, pick, put, parts, orders, axis, size, stacks, previous, out_rows, vector_rows):
        top, low = all_sum(parts, orders, TURNS[axis], axis, size)
        low_rows = low.shape[0] - RIDE
        low_vector, norm, done = call(
            functools.partial(early_kernel, PIECES),
            [(low_rows, width), tile, (early, width)],
            [pick, low, *stacks, *previous],
        )
        *parts, vector = call(
            functools.partial(rest_kernel, PIECES),
            [*chunks(out_rows), (vector_rows, width)],
            [number, pick, put, top, low_vector, norm, done, *stacks, *previous],
            [pltpu.VMEM((slots, width), jnp.bfloat16), products],
        )
        return parts, vector, norm

    alphas, betas, models = [], [], []
    bases = [data]
    for _ in range(ITERS):
        previous = [models[-1], alphas[-1]] if models else []
        parts, vector, beta = product(
            number_f, pick_col, put_row, parts, row_orders, "row", n_row, flipped, previous, tile_rows, tile_cols
        )
        models.append(vector)
        betas.append(beta)
        parts, vector, alpha = product(
            number_a, pick_row, put_col, parts, col_orders, "col", n_col, plain,
            [bases[-1], beta], tile_cols, tile_rows,
        )
        bases.append(vector)
        alphas.append(alpha)
    summed = all_sum(parts, row_orders, TURNS["row"], "row", n_row)
    square, vector, beta = call(end_kernel, [tile, model, tile], [*summed, models[-1], alphas[-1]])
    solution, search, data_basis, coef = call(
        functools.partial(update_kernel, ITERS),
        [model, model, basis, tile],
        [bases[-1], *alphas, *betas, beta, *models],
    )
    (square,) = all_sum([square], [col_bits], [0], "col", n_col)
    (search,) = call(search_kernel, [model], [square, vector, search, coef])
    return solution.reshape(-1), search.reshape(-1), data_basis.reshape(-1)


def solution(mesh):
    in_specs = (
        P("row", "col", None, None, None),
        P("row", "col", None),
        P("row", "col", None),
        P("row", "col"),
        P("row"),
    )
    out_specs = (P("col"), P("col"), P("row"))
    return jax.shard_map(
        functools.partial(per_device, mesh.shape["row"], mesh.shape["col"]),
        mesh=mesh,
        in_specs=in_specs,
        out_specs=out_specs,
        check_vma=False,
    )
```

time: 110 us -> 113 us (1.027)
  Pallas kernels: 18.6 us -> 21.9 us
    pallas_call x14 -> x18, Pallas kernels: 18.6 us -> 21.9 us  [call(): pl.pallas_call(kernel, out_shape=[jax.ShapeDtypeStruct(o, jnp.float32) if...]
  transfers between devices with their start and end apart: 38 -> 38, of which waited for: 29 -> 27; matrix products, arithmetic and copies ran while one was open for 0% -> 0% of each run, Pallas kernels for 3% -> 4%
where the time goes in v3:
time: 113 us
  waiting for transfers between devices  45.2 us (40%)
  starting transfers between devices  43.6 us (39%)
  Pallas kernels  21.9 us (19%)
  between operations  1.59 us (1%)
    ppermute x38, waiting for transfers between devices, all_sum(): other = lax.ppermute(chunks[at], axis, pairs)  45.2 us
    ppermute x38, starting transfers between devices, all_sum(): other = lax.ppermute(chunks[at], axis, pairs)  43.6 us
    pallas_call x18, Pallas kernels, call(): pl.pallas_call(kernel, out_shape=[jax.ShapeDtypeStruct(o, jnp.float32) if...  21.9 us
  transfers between devices with their start and end apart: 38, of which 27 were waited for; matrix products, arithmetic and copies ran while one was open for 0% of the time, Pallas kernels for 4%

profile of v3, /device:TPU:0, one launch (start us, length us, event | category | flops | bytes accessed | tf_op | source)
XLA Modules:
  0.0 112.7 jit_solution(3100060085515761709)
XLA Ops:
  1.3 4.3 %shard_map.76 = (f32[128,128]{1,0:T(8,128)S(1)}, f32[136,128]{1,0:T(8,128)S(1)}, f32[256,128]{1,0:T(8,128)S(1)}, bf16[256,256]{1,0:T(8,128)(2,1)S(1)}, bf16[256,...) custom-call(s32[1,256]{1,0:T(1,128)} %bitcast.9, ...), custom_call_target="tpu_custom_call" | custom-call | flops 2000000000 | bytes 1048576 | tf_op jit(solution)/shard_map/pallas_call | solution.py:233
  5.6 3.0 %collective-permute-start.3 = (f32[136,128]{1,0:T(8,128)S(1)}, f32[136,128]{1,0:T(8,128)S(1)}, u32[]{:S(2)}, u32[]{:S(2)}) collective-permute-start(f32[136,128]{1,0:T(8,128)S(1)} %get-tuple-element.68), channel_id=1, source_target_pairs={{0,4},{4,0},{8,12},{12,8},{16,20},{20,16},{24,28},{28,24},{1,5},{5... | collective-permute-start | bytes 208904 | tf_op jit(solution)/shard_map/ppermute | solution.py:250
  8.7 4.2 %collective-permute-done = f32[128,128]{1,0:T(8,128)S(1)} collective-permute-done((f32[128,128]{1,0:T(8,128)S(1)}, f32[128,128]{1,0:T(8,128)S(1)}, u32[]{:S(2)}, u32[]{:S(2)}) %collective-permute-start) | collective-permute-done | bytes 65568 | tf_op jit(solution)/shard_map/ppermute | solution.py:250
  12.9 1.6 %collective-permute-start.1 = (f32[128,128]{1,0:T(8,128)S(1)}, f32[128,128]{1,0:T(8,128)S(1)}, u32[]{:S(2)}, u32[]{:S(2)}) collective-permute-start(f32[128,128]{1,0:T(8,128)S(1)} %add.114), channel_id=1, source_target_pairs={{0,8},{4,12},{8,0},{12,4},{16,24},{20,28},{24,16},{28,20},{1,9},{5... | collective-permute-start | bytes 196616 | tf_op jit(solution)/shard_map/ppermute | solution.py:250
  15.1 1.9 %shard_map.78 = (bf16[128,128,128]{2,1,0:T(8,128)(2,1)S(1)}, bf16[128,128,128]{2,1,0:T(8,128)(2,1)S(1)}) custom-call(s32[2,256]{1,0:T(2,128)S(1)} %get-tuple-element.69.order_ref, bf16[256,128,128]{2,1,0:T(8,128)(2,1)S(1)} %get-tuple-element.70.blocks_ref), custom_call_target="tpu_custom_call" | custom-call | flops 2000000000 | bytes 1048576 | tf_op jit(solution)/shard_map/pallas_call | solution.py:233
  17.8 2.7 %collective-permute-start.2 = (f32[128,128]{1,0:T(8,128)S(1)}, f32[128,128]{1,0:T(8,128)S(1)}, u32[]{:S(2)}, u32[]{:S(2)}) collective-permute-start(f32[128,128]{1,0:T(8,128)S(1)} %add.115), channel_id=1, source_target_pairs={{0,16},{4,20},{8,24},{12,28},{16,0},{20,4},{24,8},{28,12},{1,17},{... | collective-permute-start | bytes 196616 | tf_op jit(solution)/shard_map/ppermute | solution.py:250
  20.4 1.8 %collective-permute-start.5 = (f32[136,128]{1,0:T(8,128)S(1)}, f32[136,128]{1,0:T(8,128)S(1)}, u32[]{:S(2)}, u32[]{:S(2)}) collective-permute-start(f32[136,128]{1,0:T(8,128)S(1)} %add.118), channel_id=1, source_target_pairs={{0,16},{4,20},{8,24},{12,28},{16,0},{20,4},{24,8},{28,12},{1,17},{... | collective-permute-start | bytes 208904 | tf_op jit(solution)/shard_map/ppermute | solution.py:250
  22.2 1.9 %shard_map.77 = (bf16[128,128,128]{2,1,0:T(8,128)(2,1)S(1)}, bf16[128,128,128]{2,1,0:T(8,128)(2,1)S(1)}) custom-call(s32[2,256]{1,0:T(2,128)S(1)} %get-tuple-element.69.order_ref, bf16[256,128,128]{2,1,0:T(8,128)(2,1)S(1)} %get-tuple-element.70.blocks_ref), custom_call_target="tpu_custom_call" | custom-call | flops 2000000000 | bytes 1048576 | tf_op jit(solution)/shard_map/pallas_call | solution.py:233
  24.7 1.8 %collective-permute-done.5 = f32[136,128]{1,0:T(8,128)S(1)} collective-permute-done((f32[136,128]{1,0:T(8,128)S(1)}, f32[136,128]{1,0:T(8,128)S(1)}, u32[]{:S(2)}, u32[]{:S(2)}) %collective-permute-start.5) | collective-permute-done | bytes 69664 | tf_op jit(solution)/shard_map/ppermute | solution.py:250
  27.3 1.2 %shard_map.80 = (f32[128,128]{1,0:T(8,128)S(1)}, f32[136,128]{1,0:T(8,128)S(1)}, f32[256,128]{1,0:T(8,128)S(1)}) custom-call(s32[8,128]{1,0:T(8,128)S(1)} %get-tuple-element.64.number_ref, bf16[256,256]{1,0:T(8,128)(2,1)S(1)} %get-tuple-element.65.pick_ref, bf16[256,256]{1,0:T(8,128)(2,1)S(1)} %get-tuple-element.66.put_ref, f32[128,128]{1,0:T(8,128)S(1)} %add.116.top_in_ref, ...), custom_call_target="tpu_custom_call" | custom-call | flops 2000000000 | bytes 1048576 | tf_op jit(solution)/shard_map/pallas_call | solution.py:233
  28.6 1.6 %collective-permute-start.6 = (f32[128,128]{1,0:T(8,128)S(1)}, f32[128,128]{1,0:T(8,128)S(1)}, u32[]{:S(2)}, u32[]{:S(2)}) collective-permute-start(f32[128,128]{1,0:T(8,128)S(1)} %get-tuple-element.76), channel_id=1, source_target_pairs={{0,2},{1,3},{2,0},{3,1},{4,6},{5,7},{6,4},{7,5},{8,10},{9,11},{10,... | collective-permute-start | bytes 196616 | tf_op jit(solution)/shard_map/ppermute | solution.py:250
  30.2 1.2 %collective-permute-start.9 = (f32[136,128]{1,0:T(8,128)S(1)}, f32[136,128]{1,0:T(8,128)S(1)}, u32[]{:S(2)}, u32[]{:S(2)}) collective-permute-start(f32[136,128]{1,0:T(8,128)S(1)} %add.122), channel_id=1, source_target_pairs={{0,2},{1,3},{2,0},{3,1},{4,6},{5,7},{6,4},{7,5},{8,10},{9,11},{10,... | collective-permute-start | bytes 208904 | tf_op jit(solution)/shard_map/ppermute | solution.py:250
  31.4 1.7 %collective-permute-done.6 = f32[128,128]{1,0:T(8,128)S(1)} collective-permute-done((f32[128,128]{1,0:T(8,128)S(1)}, f32[128,128]{1,0:T(8,128)S(1)}, u32[]{:S(2)}, u32[]{:S(2)}) %collective-permute-start.6) | collective-permute-done | bytes 65568 | tf_op jit(solution)/shard_map/ppermute | solution.py:250
  33.2 1.2 %collective-permute-done.7 = f32[128,128]{1,0:T(8,128)S(1)} collective-permute-done((f32[128,128]{1,0:T(8,128)S(1)}, f32[128,128]{1,0:T(8,128)S(1)}, u32[]{:S(2)}, u32[]{:S(2)}) %collective-permute-start.7) | collective-permute-done | bytes 65568 | tf_op jit(solution)/shard_map/ppermute | solution.py:250
  35.4 1.2 %shard_map.82 = (f32[128,128]{1,0:T(8,128)S(1)}, f32[136,128]{1,0:T(8,128)S(1)}, f32[256,128]{1,0:T(8,128)S(1)}) custom-call(s32[8,128]{1,0:T(8,128)S(1)} %get-tuple-element.61.number_ref, bf16[256,256]{1,0:T(8,128)(2,1)S(1)} %get-tuple-element.62.pick_ref, bf16[256,256]{1,0:T(8,128)(2,1)S(1)} %get-tuple-element.63.put_ref, f32[128,128]{1,0:T(8,128)S(1)} %add.121.top_in_ref, ...), custom_call_target="tpu_custom_call" | custom-call | flops 2000000000 | bytes 1048576 | tf_op jit(solution)/shard_map/pallas_call | solution.py:233
  36.6 2.0 %collective-permute-start.10 = (f32[128,128]{1,0:T(8,128)S(1)}, f32[128,128]{1,0:T(8,128)S(1)}, u32[]{:S(2)}, u32[]{:S(2)}) collective-permute-start(f32[128,128]{1,0:T(8,128)S(1)} %get-tuple-element.84), channel_id=1, source_target_pairs={{0,4},{4,0},{8,12},{12,8},{16,20},{20,16},{24,28},{28,24},{1,5},{5... | collective-permute-start | bytes 196616 | tf_op jit(solution)/shard_map/ppermute | solution.py:250
  38.6 2.9 %collective-permute-done.13 = f32[136,128]{1,0:T(8,128)S(1)} collective-permute-done((f32[136,128]{1,0:T(8,128)S(1)}, f32[136,128]{1,0:T(8,128)S(1)}, u32[]{:S(2)}, u32[]{:S(2)}) %collective-permute-start.13) | collective-permute-done | bytes 69664 | tf_op jit(solution)/shard_map/ppermute | solution.py:250
  42.2 1.5 %collective-permute-start.11 = (f32[128,128]{1,0:T(8,128)S(1)}, f32[128,128]{1,0:T(8,128)S(1)}, u32[]{:S(2)}, u32[]{:S(2)}) collective-permute-start(f32[128,128]{1,0:T(8,128)S(1)} %add.124), channel_id=1, source_target_pairs={{0,8},{4,12},{8,0},{12,4},{16,24},{20,28},{24,16},{28,20},{1,9},{5... | collective-permute-start | bytes 196616 | tf_op jit(solution)/shard_map/ppermute | solution.py:250
  43.7 2.2 %collective-permute-done.14 = f32[136,128]{1,0:T(8,128)S(1)} collective-permute-done((f32[136,128]{1,0:T(8,128)S(1)}, f32[136,128]{1,0:T(8,128)S(1)}, u32[]{:S(2)}, u32[]{:S(2)}) %collective-permute-start.14) | collective-permute-done | bytes 69664 | tf_op jit(solution)/shard_map/ppermute | solution.py:250
  47.1 1.9 %collective-permute-start.12 = (f32[128,128]{1,0:T(8,128)S(1)}, f32[128,128]{1,0:T(8,128)S(1)}, u32[]{:S(2)}, u32[]{:S(2)}) collective-permute-start(f32[128,128]{1,0:T(8,128)S(1)} %add.125), channel_id=1, source_target_pairs={{0,16},{4,20},{8,24},{12,28},{16,0},{20,4},{24,8},{28,12},{1,17},{... | collective-permute-start | bytes 196616 | tf_op jit(solution)/shard_map/ppermute | solution.py:250
  49.0 3.5 %collective-permute-done.12 = f32[128,128]{1,0:T(8,128)S(1)} collective-permute-done((f32[128,128]{1,0:T(8,128)S(1)}, f32[128,128]{1,0:T(8,128)S(1)}, u32[]{:S(2)}, u32[]{:S(2)}) %collective-permute-start.12) | collective-permute-done | bytes 65568 | tf_op jit(solution)/shard_map/ppermute | solution.py:250
  53.4 1.3 %shard_map.84 = (f32[128,128]{1,0:T(8,128)S(1)}, f32[136,128]{1,0:T(8,128)S(1)}, f32[256,128]{1,0:T(8,128)S(1)}) custom-call(s32[8,128]{1,0:T(8,128)S(1)} %get-tuple-element.64.number_ref, bf16[256,256]{1,0:T(8,128)(2,1)S(1)} %get-tuple-element.65.pick_ref, bf16[256,256]{1,0:T(8,128)(2,1)S(1)} %get-tuple-element.66.put_ref, f32[128,128]{1,0:T(8,128)S(1)} %add.126.top_in_ref, ...), custom_call_target="tpu_custom_call" | custom-call | flops 2000000000 | bytes 1048576 | tf_op jit(solution)/shard_map/pallas_call | solution.py:233
  54.8 1.9 %collective-permute-start.16 = (f32[128,128]{1,0:T(8,128)S(1)}, f32[128,128]{1,0:T(8,128)S(1)}, u32[]{:S(2)}, u32[]{:S(2)}) collective-permute-start(f32[128,128]{1,0:T(8,128)S(1)} %get-tuple-element.90), channel_id=1, source_target_pairs={{0,2},{1,3},{2,0},{3,1},{4,6},{5,7},{6,4},{7,5},{8,10},{9,11},{10,... | collective-permute-start | bytes 196616 | tf_op jit(solution)/shard_map/ppermute | solution.py:250
  56.7 1.2 %collective-permute-start.19 = (f32[136,128]{1,0:T(8,128)S(1)}, f32[136,128]{1,0:T(8,128)S(1)}, u32[]{:S(2)}, u32[]{:S(2)}) collective-permute-start(f32[136,128]{1,0:T(8,128)S(1)} %add.132), channel_id=1, source_target_pairs={{0,2},{1,3},{2,0},{3,1},{4,6},{5,7},{6,4},{7,5},{8,10},{9,11},{10,... | collective-permute-start | bytes 208904 | tf_op jit(solution)/shard_map/ppermute | solution.py:250
  58.0 1.4 %collective-permute-done.16 = f32[128,128]{1,0:T(8,128)S(1)} collective-permute-done((f32[128,128]{1,0:T(8,128)S(1)}, f32[128,128]{1,0:T(8,128)S(1)}, u32[]{:S(2)}, u32[]{:S(2)}) %collective-permute-start.16) | collective-permute-done | bytes 65568 | tf_op jit(solution)/shard_map/ppermute | solution.py:250
  59.5 1.2 %collective-permute-done.17 = f32[128,128]{1,0:T(8,128)S(1)} collective-permute-done((f32[128,128]{1,0:T(8,128)S(1)}, f32[128,128]{1,0:T(8,128)S(1)}, u32[]{:S(2)}, u32[]{:S(2)}) %collective-permute-start.17) | collective-permute-done | bytes 65568 | tf_op jit(solution)/shard_map/ppermute | solution.py:250
  61.9 1.2 %shard_map.86 = (f32[128,128]{1,0:T(8,128)S(1)}, f32[136,128]{1,0:T(8,128)S(1)}, f32[256,128]{1,0:T(8,128)S(1)}) custom-call(s32[8,128]{1,0:T(8,128)S(1)} %get-tuple-element.61.number_ref, bf16[256,256]{1,0:T(8,128)(2,1)S(1)} %get-tuple-element.62.pick_ref, bf16[256,256]{1,0:T(8,128)(2,1)S(1)} %get-tuple-element.63.put_ref, f32[128,128]{1,0:T(8,128)S(1)} %add.131.top_in_ref, ...), custom_call_target="tpu_custom_call" | custom-call | flops 2000000000 | bytes 1048576 | tf_op jit(solution)/shard_map/pallas_call | solution.py:233
  63.1 1.5 %collective-permute-start.23 = (f32[136,128]{1,0:T(8,128)S(1)}, f32[136,128]{1,0:T(8,128)S(1)}, u32[]{:S(2)}, u32[]{:S(2)}) collective-permute-start(f32[136,128]{1,0:T(8,128)S(1)} %get-tuple-element.97), channel_id=1, source_target_pairs={{0,4},{4,0},{8,12},{12,8},{16,20},{20,16},{24,28},{28,24},{1,5},{5... | collective-permute-start | bytes 208904 | tf_op jit(solution)/shard_map/ppermute | solution.py:250
  65.2 3.0 %collective-permute-done.23 = f32[136,128]{1,0:T(8,128)S(1)} collective-permute-done((f32[136,128]{1,0:T(8,128)S(1)}, f32[136,128]{1,0:T(8,128)S(1)}, u32[]{:S(2)}, u32[]{:S(2)}) %collective-permute-start.23) | collective-permute-done | bytes 69664 | tf_op jit(solution)/shard_map/ppermute | solution.py:250
  68.2 1.2 %collective-permute-start.24 = (f32[136,128]{1,0:T(8,128)S(1)}, f32[136,128]{1,0:T(8,128)S(1)}, u32[]{:S(2)}, u32[]{:S(2)}) collective-permute-start(f32[136,128]{1,0:T(8,128)S(1)} %add.137), channel_id=1, source_target_pairs={{0,8},{4,12},{8,0},{12,4},{16,24},{20,28},{24,16},{28,20},{1,9},{5... | collective-permute-start | bytes 208904 | tf_op jit(solution)/shard_map/ppermute | solution.py:250
  70.4 2.2 %collective-permute-done.24 = f32[136,128]{1,0:T(8,128)S(1)} collective-permute-done((f32[136,128]{1,0:T(8,128)S(1)}, f32[136,128]{1,0:T(8,128)S(1)}, u32[]{:S(2)}, u32[]{:S(2)}) %collective-permute-start.24) | collective-permute-done | bytes 69664 | tf_op jit(solution)/shard_map/ppermute | solution.py:250
  72.6 1.4 %collective-permute-start.25 = (f32[136,128]{1,0:T(8,128)S(1)}, f32[136,128]{1,0:T(8,128)S(1)}, u32[]{:S(2)}, u32[]{:S(2)}) collective-permute-start(f32[136,128]{1,0:T(8,128)S(1)} %add.138), channel_id=1, source_target_pairs={{0,16},{4,20},{8,24},{12,28},{16,0},{20,4},{24,8},{28,12},{1,17},{... | collective-permute-start | bytes 208904 | tf_op jit(solution)/shard_map/ppermute | solution.py:250
  74.4 1.6 %collective-permute-start.22 = (f32[128,128]{1,0:T(8,128)S(1)}, f32[128,128]{1,0:T(8,128)S(1)}, u32[]{:S(2)}, u32[]{:S(2)}) collective-permute-start(f32[128,128]{1,0:T(8,128)S(1)} %add.135), channel_id=1, source_target_pairs={{0,16},{4,20},{8,24},{12,28},{16,0},{20,4},{24,8},{28,12},{1,17},{... | collective-permute-start | bytes 196616 | tf_op jit(solution)/shard_map/ppermute | solution.py:250
  76.0 3.7 %collective-permute-done.22 = f32[128,128]{1,0:T(8,128)S(1)} collective-permute-done((f32[128,128]{1,0:T(8,128)S(1)}, f32[128,128]{1,0:T(8,128)S(1)}, u32[]{:S(2)}, u32[]{:S(2)}) %collective-permute-start.22) | collective-permute-done | bytes 65568 | tf_op jit(solution)/shard_map/ppermute | solution.py:250
  80.5 1.2 %shard_map.88 = (f32[128,128]{1,0:T(8,128)S(1)}, f32[136,128]{1,0:T(8,128)S(1)}, f32[256,128]{1,0:T(8,128)S(1)}) custom-call(s32[8,128]{1,0:T(8,128)S(1)} %get-tuple-element.64.number_ref, bf16[256,256]{1,0:T(8,128)(2,1)S(1)} %get-tuple-element.65.pick_ref, bf16[256,256]{1,0:T(8,128)(2,1)S(1)} %get-tuple-element.66.put_ref, f32[128,128]{1,0:T(8,128)S(1)} %add.136.top_in_ref, ...), custom_call_target="tpu_custom_call" | custom-call | flops 2000000000 | bytes 1048576 | tf_op jit(solution)/shard_map/pallas_call | solution.py:233
  81.8 2.2 %collective-permute-start.26 = (f32[128,128]{1,0:T(8,128)S(1)}, f32[128,128]{1,0:T(8,128)S(1)}, u32[]{:S(2)}, u32[]{:S(2)}) collective-permute-start(f32[128,128]{1,0:T(8,128)S(1)} %get-tuple-element.102), channel_id=1, source_target_pairs={{0,2},{1,3},{2,0},{3,1},{4,6},{5,7},{6,4},{7,5},{8,10},{9,11},{10,... | collective-permute-start | bytes 196616 | tf_op jit(solution)/shard_map/ppermute | solution.py:250
  84.0 1.2 %collective-permute-start.29 = (f32[136,128]{1,0:T(8,128)S(1)}, f32[136,128]{1,0:T(8,128)S(1)}, u32[]{:S(2)}, u32[]{:S(2)}) collective-permute-start(f32[136,128]{1,0:T(8,128)S(1)} %add.142), channel_id=1, source_target_pairs={{0,2},{1,3},{2,0},{3,1},{4,6},{5,7},{6,4},{7,5},{8,10},{9,11},{10,... | collective-permute-start | bytes 208904 | tf_op jit(solution)/shard_map/ppermute | solution.py:250
  85.3 1.4 %collective-permute-done.26 = f32[128,128]{1,0:T(8,128)S(1)} collective-permute-done((f32[128,128]{1,0:T(8,128)S(1)}, f32[128,128]{1,0:T(8,128)S(1)}, u32[]{:S(2)}, u32[]{:S(2)}) %collective-permute-start.26) | collective-permute-done | bytes 65568 | tf_op jit(solution)/shard_map/ppermute | solution.py:250
  86.8 1.2 %collective-permute-done.27 = f32[128,128]{1,0:T(8,128)S(1)} collective-permute-done((f32[128,128]{1,0:T(8,128)S(1)}, f32[128,128]{1,0:T(8,128)S(1)}, u32[]{:S(2)}, u32[]{:S(2)}) %collective-permute-start.27) | collective-permute-done | bytes 65568 | tf_op jit(solution)/shard_map/ppermute | solution.py:250
  89.2 1.2 %shard_map.90 = (f32[128,128]{1,0:T(8,128)S(1)}, f32[136,128]{1,0:T(8,128)S(1)}, f32[256,128]{1,0:T(8,128)S(1)}) custom-call(s32[8,128]{1,0:T(8,128)S(1)} %get-tuple-element.61.number_ref, bf16[256,256]{1,0:T(8,128)(2,1)S(1)} %get-tuple-element.62.pick_ref, bf16[256,256]{1,0:T(8,128)(2,1)S(1)} %get-tuple-element.63.put_ref, f32[128,128]{1,0:T(8,128)S(1)} %add.141.top_in_ref, ...), custom_call_target="tpu_custom_call" | custom-call | flops 2000000000 | bytes 1048576 | tf_op jit(solution)/shard_map/pallas_call | solution.py:233
  91.3 1.2 %collective-permute-start.30 = (f32[128,128]{1,0:T(8,128)S(1)}, f32[128,128]{1,0:T(8,128)S(1)}, u32[]{:S(2)}, u32[]{:S(2)}) collective-permute-start(f32[128,128]{1,0:T(8,128)S(1)} %get-tuple-element.109), channel_id=1, source_target_pairs={{0,4},{4,0},{8,12},{12,8},{16,20},{20,16},{24,28},{28,24},{1,5},{5... | collective-permute-start | bytes 196616 | tf_op jit(solution)/shard_map/ppermute | solution.py:250
  92.5 2.6 %collective-permute-done.33 = f32[136,128]{1,0:T(8,128)S(1)} collective-permute-done((f32[136,128]{1,0:T(8,128)S(1)}, f32[136,128]{1,0:T(8,128)S(1)}, u32[]{:S(2)}, u32[]{:S(2)}) %collective-permute-start.33) | collective-permute-done | bytes 69664 | tf_op jit(solution)/shard_map/ppermute | solution.py:250
  95.1 1.3 %collective-permute-start.34 = (f32[136,128]{1,0:T(8,128)S(1)}, f32[136,128]{1,0:T(8,128)S(1)}, u32[]{:S(2)}, u32[]{:S(2)}) collective-permute-start(f32[136,128]{1,0:T(8,128)S(1)} %add.147), channel_id=1, source_target_pairs={{0,8},{4,12},{8,0},{12,4},{16,24},{20,28},{24,16},{28,20},{1,9},{5... | collective-permute-start | bytes 208904 | tf_op jit(solution)/shard_map/ppermute | solution.py:250
  97.3 2.2 %collective-permute-done.34 = f32[136,128]{1,0:T(8,128)S(1)} collective-permute-done((f32[136,128]{1,0:T(8,128)S(1)}, f32[136,128]{1,0:T(8,128)S(1)}, u32[]{:S(2)}, u32[]{:S(2)}) %collective-permute-start.34) | collective-permute-done | bytes 69664 | tf_op jit(solution)/shard_map/ppermute | solution.py:250
  99.5 1.7 %collective-permute-start.35 = (f32[136,128]{1,0:T(8,128)S(1)}, f32[136,128]{1,0:T(8,128)S(1)}, u32[]{:S(2)}, u32[]{:S(2)}) collective-permute-start(f32[136,128]{1,0:T(8,128)S(1)} %add.148), channel_id=1, source_target_pairs={{0,16},{4,20},{8,24},{12,28},{16,0},{20,4},{24,8},{28,12},{1,17},{... | collective-permute-start | bytes 208904 | tf_op jit(solution)/shard_map/ppermute | solution.py:250
  101.5 1.5 %collective-permute-start.32 = (f32[128,128]{1,0:T(8,128)S(1)}, f32[128,128]{1,0:T(8,128)S(1)}, u32[]{:S(2)}, u32[]{:S(2)}) collective-permute-start(f32[128,128]{1,0:T(8,128)S(1)} %add.145), channel_id=1, source_target_pairs={{0,16},{4,20},{8,24},{12,28},{16,0},{20,4},{24,8},{28,12},{1,17},{... | collective-permute-start | bytes 196616 | tf_op jit(solution)/shard_map/ppermute | solution.py:250
  103.0 3.7 %collective-permute-done.32 = f32[128,128]{1,0:T(8,128)S(1)} collective-permute-done((f32[128,128]{1,0:T(8,128)S(1)}, f32[128,128]{1,0:T(8,128)S(1)}, u32[]{:S(2)}, u32[]{:S(2)}) %collective-permute-start.32) | collective-permute-done | bytes 65568 | tf_op jit(solution)/shard_map/ppermute | solution.py:250
  108.2 2.2 %collective-permute-start.37 = (f32[8,128]{1,0:T(8,128)S(1)}, f32[8,128]{1,0:T(8,128)S(1)}, u32[]{:S(2)}, u32[]{:S(2)}) collective-permute-start(f32[8,128]{1,0:T(8,128)S(1)} %add.150), channel_id=1, source_target_pairs={{0,2},{1,3},{2,0},{3,1},{4,6},{5,7},{6,4},{7,5},{8,10},{9,11},{10,... | collective-permute-start | bytes 12296 | tf_op jit(solution)/shard_map/ppermute | solution.py:250
  (84 shorter events, 18.0 us)
Async XLA Ops:
  5.6 9.0 %collective-permute-start.3 = (f32[136,128]{1,0:T(8,128)S(1)}, f32[136,128]{1,0:T(8,128)S(1)}, u32[]{:S(2)}, u32[]{:S(2)}) collective-permute-start(f32[136,128]{1,0:T(8,128)S(1)} %get-tuple-element.68), channel_id=1, source_target_pairs={{0,4},{4,0},{8,12},{12,8},{16,20},{20,16},{24,28},{28,24},{1,5},{5... | collective-permute-start | bytes 208904 | tf_op jit(solution)/shard_map/ppermute | solution.py:250
  8.7 4.3 %collective-permute-start = (f32[128,128]{1,0:T(8,128)S(1)}, f32[128,128]{1,0:T(8,128)S(1)}, u32[]{:S(2)}, u32[]{:S(2)}) collective-permute-start(f32[128,128]{1,0:T(8,128)S(1)} %get-tuple-element.67), channel_id=1, source_target_pairs={{0,4},{4,0},{8,12},{12,8},{16,20},{20,16},{24,28},{28,24},{1,5},{5... | collective-permute-start | bytes 196616 | tf_op jit(solution)/shard_map/ppermute | solution.py:250
  12.9 4.8 %collective-permute-start.1 = (f32[128,128]{1,0:T(8,128)S(1)}, f32[128,128]{1,0:T(8,128)S(1)}, u32[]{:S(2)}, u32[]{:S(2)}) collective-permute-start(f32[128,128]{1,0:T(8,128)S(1)} %add.114), channel_id=1, source_target_pairs={{0,8},{4,12},{8,0},{12,4},{16,24},{20,28},{24,16},{28,20},{1,9},{5... | collective-permute-start | bytes 196616 | tf_op jit(solution)/shard_map/ppermute | solution.py:250
  14.6 5.8 %collective-permute-start.4 = (f32[136,128]{1,0:T(8,128)S(1)}, f32[136,128]{1,0:T(8,128)S(1)}, u32[]{:S(2)}, u32[]{:S(2)}) collective-permute-start(f32[136,128]{1,0:T(8,128)S(1)} %add.117), channel_id=1, source_target_pairs={{0,8},{4,12},{8,0},{12,4},{16,24},{20,28},{24,16},{28,20},{1,9},{5... | collective-permute-start | bytes 208904 | tf_op jit(solution)/shard_map/ppermute | solution.py:250
  17.8 6.9 %collective-permute-start.2 = (f32[128,128]{1,0:T(8,128)S(1)}, f32[128,128]{1,0:T(8,128)S(1)}, u32[]{:S(2)}, u32[]{:S(2)}) collective-permute-start(f32[128,128]{1,0:T(8,128)S(1)} %add.115), channel_id=1, source_target_pairs={{0,16},{4,20},{8,24},{12,28},{16,0},{20,4},{24,8},{28,12},{1,17},{... | collective-permute-start | bytes 196616 | tf_op jit(solution)/shard_map/ppermute | solution.py:250
  20.4 6.0 %collective-permute-start.5 = (f32[136,128]{1,0:T(8,128)S(1)}, f32[136,128]{1,0:T(8,128)S(1)}, u32[]{:S(2)}, u32[]{:S(2)}) collective-permute-start(f32[136,128]{1,0:T(8,128)S(1)} %add.118), channel_id=1, source_target_pairs={{0,16},{4,20},{8,24},{12,28},{16,0},{20,4},{24,8},{28,12},{1,17},{... | collective-permute-start | bytes 208904 | tf_op jit(solution)/shard_map/ppermute | solution.py:250
  28.5 1.7 %collective-permute-start.8 = (f32[136,128]{1,0:T(8,128)S(1)}, f32[136,128]{1,0:T(8,128)S(1)}, u32[]{:S(2)}, u32[]{:S(2)}) collective-permute-start(f32[136,128]{1,0:T(8,128)S(1)} %get-tuple-element.77), channel_id=1, source_target_pairs={{0,1},{1,0},{2,3},{3,2},{4,5},{5,4},{6,7},{7,6},{8,9},{9,8},{10,11... | collective-permute-start | bytes 208904 | tf_op jit(solution)/shard_map/ppermute | solution.py:250
  28.6 4.6 %collective-permute-start.6 = (f32[128,128]{1,0:T(8,128)S(1)}, f32[128,128]{1,0:T(8,128)S(1)}, u32[]{:S(2)}, u32[]{:S(2)}) collective-permute-start(f32[128,128]{1,0:T(8,128)S(1)} %get-tuple-element.76), channel_id=1, source_target_pairs={{0,2},{1,3},{2,0},{3,1},{4,6},{5,7},{6,4},{7,5},{8,10},{9,11},{10,... | collective-permute-start | bytes 196616 | tf_op jit(solution)/shard_map/ppermute | solution.py:250
  30.2 4.4 %collective-permute-start.9 = (f32[136,128]{1,0:T(8,128)S(1)}, f32[136,128]{1,0:T(8,128)S(1)}, u32[]{:S(2)}, u32[]{:S(2)}) collective-permute-start(f32[136,128]{1,0:T(8,128)S(1)} %add.122), channel_id=1, source_target_pairs={{0,2},{1,3},{2,0},{3,1},{4,6},{5,7},{6,4},{7,5},{8,10},{9,11},{10,... | collective-permute-start | bytes 208904 | tf_op jit(solution)/shard_map/ppermute | solution.py:250
  33.1 1.3 %collective-permute-start.7 = (f32[128,128]{1,0:T(8,128)S(1)}, f32[128,128]{1,0:T(8,128)S(1)}, u32[]{:S(2)}, u32[]{:S(2)}) collective-permute-start(f32[128,128]{1,0:T(8,128)S(1)} %add.120), channel_id=1, source_target_pairs={{0,1},{1,0},{2,3},{3,2},{4,5},{5,4},{6,7},{7,6},{8,9},{9,8},{10,11... | collective-permute-start | bytes 196616 | tf_op jit(solution)/shard_map/ppermute | solution.py:250
  36.6 5.0 %collective-permute-start.13 = (f32[136,128]{1,0:T(8,128)S(1)}, f32[136,128]{1,0:T(8,128)S(1)}, u32[]{:S(2)}, u32[]{:S(2)}) collective-permute-start(f32[136,128]{1,0:T(8,128)S(1)} %get-tuple-element.85), channel_id=1, source_target_pairs={{0,4},{4,0},{8,12},{12,8},{16,20},{20,16},{24,28},{28,24},{1,5},{5... | collective-permute-start | bytes 208904 | tf_op jit(solution)/shard_map/ppermute | solution.py:250
  36.6 5.6 %collective-permute-start.10 = (f32[128,128]{1,0:T(8,128)S(1)}, f32[128,128]{1,0:T(8,128)S(1)}, u32[]{:S(2)}, u32[]{:S(2)}) collective-permute-start(f32[128,128]{1,0:T(8,128)S(1)} %get-tuple-element.84), channel_id=1, source_target_pairs={{0,4},{4,0},{8,12},{12,8},{16,20},{20,16},{24,28},{28,24},{1,5},{5... | collective-permute-start | bytes 196616 | tf_op jit(solution)/shard_map/ppermute | solution.py:250
  41.5 4.4 %collective-permute-start.14 = (f32[136,128]{1,0:T(8,128)S(1)}, f32[136,128]{1,0:T(8,128)S(1)}, u32[]{:S(2)}, u32[]{:S(2)}) collective-permute-start(f32[136,128]{1,0:T(8,128)S(1)} %add.127), channel_id=1, source_target_pairs={{0,8},{4,12},{8,0},{12,4},{16,24},{20,28},{24,16},{28,20},{1,9},{5... | collective-permute-start | bytes 208904 | tf_op jit(solution)/shard_map/ppermute | solution.py:250
  42.2 4.8 %collective-permute-start.11 = (f32[128,128]{1,0:T(8,128)S(1)}, f32[128,128]{1,0:T(8,128)S(1)}, u32[]{:S(2)}, u32[]{:S(2)}) collective-permute-start(f32[128,128]{1,0:T(8,128)S(1)} %add.124), channel_id=1, source_target_pairs={{0,8},{4,12},{8,0},{12,4},{16,24},{20,28},{24,16},{28,20},{1,9},{5... | collective-permute-start | bytes 196616 | tf_op jit(solution)/shard_map/ppermute | solution.py:250
  45.9 6.6 %collective-permute-start.15 = (f32[136,128]{1,0:T(8,128)S(1)}, f32[136,128]{1,0:T(8,128)S(1)}, u32[]{:S(2)}, u32[]{:S(2)}) collective-permute-start(f32[136,128]{1,0:T(8,128)S(1)} %add.128), channel_id=1, source_target_pairs={{0,16},{4,20},{8,24},{12,28},{16,0},{20,4},{24,8},{28,12},{1,17},{... | collective-permute-start | bytes 208904 | tf_op jit(solution)/shard_map/ppermute | solution.py:250
  47.1 5.5 %collective-permute-start.12 = (f32[128,128]{1,0:T(8,128)S(1)}, f32[128,128]{1,0:T(8,128)S(1)}, u32[]{:S(2)}, u32[]{:S(2)}) collective-permute-start(f32[128,128]{1,0:T(8,128)S(1)} %add.125), channel_id=1, source_target_pairs={{0,16},{4,20},{8,24},{12,28},{16,0},{20,4},{24,8},{28,12},{1,17},{... | collective-permute-start | bytes 196616 | tf_op jit(solution)/shard_map/ppermute | solution.py:250
  54.7 2.0 %collective-permute-start.18 = (f32[136,128]{1,0:T(8,128)S(1)}, f32[136,128]{1,0:T(8,128)S(1)}, u32[]{:S(2)}, u32[]{:S(2)}) collective-permute-start(f32[136,128]{1,0:T(8,128)S(1)} %get-tuple-element.91), channel_id=1, source_target_pairs={{0,1},{1,0},{2,3},{3,2},{4,5},{5,4},{6,7},{7,6},{8,9},{9,8},{10,11... | collective-permute-start | bytes 208904 | tf_op jit(solution)/shard_map/ppermute | solution.py:250
  54.8 4.6 %collective-permute-start.16 = (f32[128,128]{1,0:T(8,128)S(1)}, f32[128,128]{1,0:T(8,128)S(1)}, u32[]{:S(2)}, u32[]{:S(2)}) collective-permute-start(f32[128,128]{1,0:T(8,128)S(1)} %get-tuple-element.90), channel_id=1, source_target_pairs={{0,2},{1,3},{2,0},{3,1},{4,6},{5,7},{6,4},{7,5},{8,10},{9,11},{10,... | collective-permute-start | bytes 196616 | tf_op jit(solution)/shard_map/ppermute | solution.py:250
  56.7 4.4 %collective-permute-start.19 = (f32[136,128]{1,0:T(8,128)S(1)}, f32[136,128]{1,0:T(8,128)S(1)}, u32[]{:S(2)}, u32[]{:S(2)}) collective-permute-start(f32[136,128]{1,0:T(8,128)S(1)} %add.132), channel_id=1, source_target_pairs={{0,2},{1,3},{2,0},{3,1},{4,6},{5,7},{6,4},{7,5},{8,10},{9,11},{10,... | collective-permute-start | bytes 208904 | tf_op jit(solution)/shard_map/ppermute | solution.py:250
  59.4 1.3 %collective-permute-start.17 = (f32[128,128]{1,0:T(8,128)S(1)}, f32[128,128]{1,0:T(8,128)S(1)}, u32[]{:S(2)}, u32[]{:S(2)}) collective-permute-start(f32[128,128]{1,0:T(8,128)S(1)} %add.130), channel_id=1, source_target_pairs={{0,1},{1,0},{2,3},{3,2},{4,5},{5,4},{6,7},{7,6},{8,9},{9,8},{10,11... | collective-permute-start | bytes 196616 | tf_op jit(solution)/shard_map/ppermute | solution.py:250
  63.1 5.1 %collective-permute-start.23 = (f32[136,128]{1,0:T(8,128)S(1)}, f32[136,128]{1,0:T(8,128)S(1)}, u32[]{:S(2)}, u32[]{:S(2)}) collective-permute-start(f32[136,128]{1,0:T(8,128)S(1)} %get-tuple-element.97), channel_id=1, source_target_pairs={{0,4},{4,0},{8,12},{12,8},{16,20},{20,16},{24,28},{28,24},{1,5},{5... | collective-permute-start | bytes 208904 | tf_op jit(solution)/shard_map/ppermute | solution.py:250
  64.6 4.7 %collective-permute-start.20 = (f32[128,128]{1,0:T(8,128)S(1)}, f32[128,128]{1,0:T(8,128)S(1)}, u32[]{:S(2)}, u32[]{:S(2)}) collective-permute-start(f32[128,128]{1,0:T(8,128)S(1)} %get-tuple-element.96), channel_id=1, source_target_pairs={{0,4},{4,0},{8,12},{12,8},{16,20},{20,16},{24,28},{28,24},{1,5},{5... | collective-permute-start | bytes 196616 | tf_op jit(solution)/shard_map/ppermute | solution.py:250
  68.2 4.4 %collective-permute-start.24 = (f32[136,128]{1,0:T(8,128)S(1)}, f32[136,128]{1,0:T(8,128)S(1)}, u32[]{:S(2)}, u32[]{:S(2)}) collective-permute-start(f32[136,128]{1,0:T(8,128)S(1)} %add.137), channel_id=1, source_target_pairs={{0,8},{4,12},{8,0},{12,4},{16,24},{20,28},{24,16},{28,20},{1,9},{5... | collective-permute-start | bytes 208904 | tf_op jit(solution)/shard_map/ppermute | solution.py:250
  69.4 5.0 %collective-permute-start.21 = (f32[128,128]{1,0:T(8,128)S(1)}, f32[128,128]{1,0:T(8,128)S(1)}, u32[]{:S(2)}, u32[]{:S(2)}) collective-permute-start(f32[128,128]{1,0:T(8,128)S(1)} %add.134), channel_id=1, source_target_pairs={{0,8},{4,12},{8,0},{12,4},{16,24},{20,28},{24,16},{28,20},{1,9},{5... | collective-permute-start | bytes 196616 | tf_op jit(solution)/shard_map/ppermute | solution.py:250
  72.6 7.1 %collective-permute-start.25 = (f32[136,128]{1,0:T(8,128)S(1)}, f32[136,128]{1,0:T(8,128)S(1)}, u32[]{:S(2)}, u32[]{:S(2)}) collective-permute-start(f32[136,128]{1,0:T(8,128)S(1)} %add.138), channel_id=1, source_target_pairs={{0,16},{4,20},{8,24},{12,28},{16,0},{20,4},{24,8},{28,12},{1,17},{... | collective-permute-start | bytes 208904 | tf_op jit(solution)/shard_map/ppermute | solution.py:250
  74.4 5.2 %collective-permute-start.22 = (f32[128,128]{1,0:T(8,128)S(1)}, f32[128,128]{1,0:T(8,128)S(1)}, u32[]{:S(2)}, u32[]{:S(2)}) collective-permute-start(f32[128,128]{1,0:T(8,128)S(1)} %add.135), channel_id=1, source_target_pairs={{0,16},{4,20},{8,24},{12,28},{16,0},{20,4},{24,8},{28,12},{1,17},{... | collective-permute-start | bytes 196616 | tf_op jit(solution)/shard_map/ppermute | solution.py:250
  81.7 2.3 %collective-permute-start.28 = (f32[136,128]{1,0:T(8,128)S(1)}, f32[136,128]{1,0:T(8,128)S(1)}, u32[]{:S(2)}, u32[]{:S(2)}) collective-permute-start(f32[136,128]{1,0:T(8,128)S(1)} %get-tuple-element.103), channel_id=1, source_target_pairs={{0,1},{1,0},{2,3},{3,2},{4,5},{5,4},{6,7},{7,6},{8,9},{9,8},{10,11... | collective-permute-start | bytes 208904 | tf_op jit(solution)/shard_map/ppermute | solution.py:250
  81.8 4.9 %collective-permute-start.26 = (f32[128,128]{1,0:T(8,128)S(1)}, f32[128,128]{1,0:T(8,128)S(1)}, u32[]{:S(2)}, u32[]{:S(2)}) collective-permute-start(f32[128,128]{1,0:T(8,128)S(1)} %get-tuple-element.102), channel_id=1, source_target_pairs={{0,2},{1,3},{2,0},{3,1},{4,6},{5,7},{6,4},{7,5},{8,10},{9,11},{10,... | collective-permute-start | bytes 196616 | tf_op jit(solution)/shard_map/ppermute | solution.py:250
  84.0 4.4 %collective-permute-start.29 = (f32[136,128]{1,0:T(8,128)S(1)}, f32[136,128]{1,0:T(8,128)S(1)}, u32[]{:S(2)}, u32[]{:S(2)}) collective-permute-start(f32[136,128]{1,0:T(8,128)S(1)} %add.142), channel_id=1, source_target_pairs={{0,2},{1,3},{2,0},{3,1},{4,6},{5,7},{6,4},{7,5},{8,10},{9,11},{10,... | collective-permute-start | bytes 208904 | tf_op jit(solution)/shard_map/ppermute | solution.py:250
  86.7 1.3 %collective-permute-start.27 = (f32[128,128]{1,0:T(8,128)S(1)}, f32[128,128]{1,0:T(8,128)S(1)}, u32[]{:S(2)}, u32[]{:S(2)}) collective-permute-start(f32[128,128]{1,0:T(8,128)S(1)} %add.140), channel_id=1, source_target_pairs={{0,1},{1,0},{2,3},{3,2},{4,5},{5,4},{6,7},{7,6},{8,9},{9,8},{10,11... | collective-permute-start | bytes 196616 | tf_op jit(solution)/shard_map/ppermute | solution.py:250
  90.4 4.7 %collective-permute-start.33 = (f32[136,128]{1,0:T(8,128)S(1)}, f32[136,128]{1,0:T(8,128)S(1)}, u32[]{:S(2)}, u32[]{:S(2)}) collective-permute-start(f32[136,128]{1,0:T(8,128)S(1)} %get-tuple-element.110), channel_id=1, source_target_pairs={{0,4},{4,0},{8,12},{12,8},{16,20},{20,16},{24,28},{28,24},{1,5},{5... | collective-permute-start | bytes 208904 | tf_op jit(solution)/shard_map/ppermute | solution.py:250
  91.3 5.1 %collective-permute-start.30 = (f32[128,128]{1,0:T(8,128)S(1)}, f32[128,128]{1,0:T(8,128)S(1)}, u32[]{:S(2)}, u32[]{:S(2)}) collective-permute-start(f32[128,128]{1,0:T(8,128)S(1)} %get-tuple-element.109), channel_id=1, source_target_pairs={{0,4},{4,0},{8,12},{12,8},{16,20},{20,16},{24,28},{28,24},{1,5},{5... | collective-permute-start | bytes 196616 | tf_op jit(solution)/shard_map/ppermute | solution.py:250
  95.1 4.4 %collective-permute-start.34 = (f32[136,128]{1,0:T(8,128)S(1)}, f32[136,128]{1,0:T(8,128)S(1)}, u32[]{:S(2)}, u32[]{:S(2)}) collective-permute-start(f32[136,128]{1,0:T(8,128)S(1)} %add.147), channel_id=1, source_target_pairs={{0,8},{4,12},{8,0},{12,4},{16,24},{20,28},{24,16},{28,20},{1,9},{5... | collective-permute-start | bytes 208904 | tf_op jit(solution)/shard_map/ppermute | solution.py:250
  96.4 5.1 %collective-permute-start.31 = (f32[128,128]{1,0:T(8,128)S(1)}, f32[128,128]{1,0:T(8,128)S(1)}, u32[]{:S(2)}, u32[]{:S(2)}) collective-permute-start(f32[128,128]{1,0:T(8,128)S(1)} %add.144), channel_id=1, source_target_pairs={{0,8},{4,12},{8,0},{12,4},{16,24},{20,28},{24,16},{28,20},{1,9},{5... | collective-permute-start | bytes 196616 | tf_op jit(solution)/shard_map/ppermute | solution.py:250
  99.5 7.3 %collective-permute-start.35 = (f32[136,128]{1,0:T(8,128)S(1)}, f32[136,128]{1,0:T(8,128)S(1)}, u32[]{:S(2)}, u32[]{:S(2)}) collective-permute-start(f32[136,128]{1,0:T(8,128)S(1)} %add.148), channel_id=1, source_target_pairs={{0,16},{4,20},{8,24},{12,28},{16,0},{20,4},{24,8},{28,12},{1,17},{... | collective-permute-start | bytes 208904 | tf_op jit(solution)/shard_map/ppermute | solution.py:250
  101.5 5.2 %collective-permute-start.32 = (f32[128,128]{1,0:T(8,128)S(1)}, f32[128,128]{1,0:T(8,128)S(1)}, u32[]{:S(2)}, u32[]{:S(2)}) collective-permute-start(f32[128,128]{1,0:T(8,128)S(1)} %add.145), channel_id=1, source_target_pairs={{0,16},{4,20},{8,24},{12,28},{16,0},{20,4},{24,8},{28,12},{1,17},{... | collective-permute-start | bytes 196616 | tf_op jit(solution)/shard_map/ppermute | solution.py:250
  106.9 1.2 %collective-permute-start.36 = (f32[8,128]{1,0:T(8,128)S(1)}, f32[8,128]{1,0:T(8,128)S(1)}, u32[]{:S(2)}, u32[]{:S(2)}) collective-permute-start(f32[8,128]{1,0:T(8,128)S(1)} %get-tuple-element.114), channel_id=1, source_target_pairs={{0,1},{1,0},{2,3},{3,2},{4,5},{5,4},{6,7},{7,6},{8,9},{9,8},{10,11... | collective-permute-start | bytes 12296 | tf_op jit(solution)/shard_map/ppermute | solution.py:250
  108.2 3.7 %collective-permute-start.37 = (f32[8,128]{1,0:T(8,128)S(1)}, f32[8,128]{1,0:T(8,128)S(1)}, u32[]{:S(2)}, u32[]{:S(2)}) collective-permute-start(f32[8,128]{1,0:T(8,128)S(1)} %add.150), channel_id=1, source_target_pairs={{0,2},{1,3},{2,0},{3,1},{4,6},{5,7},{6,4},{7,5},{8,10},{9,11},{10,... | collective-permute-start | bytes 12296 | tf_op jit(solution)/shard_map/ppermute | solution.py:250

commit v4 on v3

--- a/solution.py
+++ b/solution.py
@@ -14,7 +14,7 @@
 VMEM_LIMIT = 4 * 1024 * 1024
 GROUP = 16
 PIECES = 2
-LOADS = (8, 6, 2)
+LOADS = (9, 6, 1)
 AHEAD = 2
 TURNS = {"row": (1, 0), "col": (1, 0)}
 RIDE = 8
@@ -168,13 +168,24 @@
     vector_ref[top:] = low_vector_ref[...]
     vector = vector_ref[...]
     slots, early, share = pick_ref.shape[0], early_ref.shape[0], blocks_refs[0].shape[0]
-    picked_ref[...] = pick_pieces(pick_ref[...], vector)
+    picked = pick_pieces(pick_ref[early:], vector)
     prod_ref[:early] = early_ref[...]
     for at in range(early, slots, GROUP):
-        prod_ref[at : at + GROUP] = group_products(picked_ref[at : at + GROUP], stack_of(blocks_refs, at))
+        here = slice(at - early, at - early + GROUP)
+        prod_ref[at : at + GROUP] = group_products(picked[here], stack_of(blocks_refs, at))
+
+    def put():
+        part = put_products(put_ref[...], prod_ref[...])
+        rows = part.shape[0]
+        top_ref[...] = part[: top_ref.shape[0]]
+        low_ref[: rows - top_ref.shape[0]] = part[top_ref.shape[0] :]
+
+    put()
+    low_ref[low_ref.shape[0] - RIDE :] = squares(vector)
 
     @pl.when(jnp.max(number_ref[...]) > slots - early)
     def _():
+        picked_ref[...] = pick_pieces(pick_ref[:early], vector_ref[...])
         for piece, blocks_ref in enumerate(blocks_refs[: pl.cdiv(early, share)]):
 
             @pl.loop(0, min(share, early - piece * share) // GROUP)
@@ -183,11 +194,7 @@
                 here = pl.ds(pl.multiple_of(piece * share + at, GROUP), GROUP)
                 prod_ref[here] = group_products(picked_ref[here], blocks_ref[pl.ds(at, GROUP)])
 
-    part = put_products(put_ref[...], prod_ref[...])
-    rows, top = part.shape[0], top_ref.shape[0]
-    top_ref[...] = part[:top]
-    low_ref[: rows - top] = part[top:]
-    low_ref[rows - top :] = squares(vector)
+        put()
 
 
 def end_kernel(top_in_ref, low_in_ref, before_ref, before_norm_ref, square_ref, vector_ref, norm_ref):
@@ -312,7 +319,7 @@
             functools.partial(rest_kernel, PIECES),
             [*chunks(out_rows), (vector_rows, width)],
             [number, pick, put, top, low_vector, norm, done, *stacks, *previous],
-            [pltpu.VMEM((slots, width), jnp.bfloat16), products],
+            [pltpu.VMEM((early, width), jnp.bfloat16), products],
         )
         return parts, vector, norm
 

time: 113 us -> 112 us (level)
  no operation moved by 1% of the time
where the time goes in v4:
time: 112 us
  waiting for transfers between devices  45.2 us (40%)
  starting transfers between devices  43.6 us (39%)
  Pallas kernels  21.5 us (19%)
  between operations  1.6 us (1%)
    ppermute x38, waiting for transfers between devices, all_sum(): other = lax.ppermute(chunks[at], axis, pairs)  45.2 us
    ppermute x38, starting transfers between devices, all_sum(): other = lax.ppermute(chunks[at], axis, pairs)  43.6 us
    pallas_call x18, Pallas kernels, call(): pl.pallas_call(kernel, out_shape=[jax.ShapeDtypeStruct(o, jnp.float32) if...  21.5 us
  transfers between devices with their start and end apart: 38, of which 27 were waited for; matrix products, arithmetic and copies ran while one was open for 0% of the time, Pallas kernels for 4%

profile of v4, /device:TPU:0, one launch (start us, length us, event | category | flops | bytes accessed | tf_op | source)
XLA Modules:
  0.0 112.3 jit_solution(872653644905383217)
XLA Ops:
  1.3 4.4 %shard_map.76 = (f32[128,128]{1,0:T(8,128)S(1)}, f32[136,128]{1,0:T(8,128)S(1)}, f32[256,128]{1,0:T(8,128)S(1)}, bf16[256,256]{1,0:T(8,128)(2,1)S(1)}, bf16[256,...) custom-call(s32[1,256]{1,0:T(1,128)} %bitcast.9, ...), custom_call_target="tpu_custom_call" | custom-call | flops 2000000000 | bytes 1048576 | tf_op jit(solution)/shard_map/pallas_call | solution.py:240
  5.7 3.0 %collective-permute-start.3 = (f32[136,128]{1,0:T(8,128)S(1)}, f32[136,128]{1,0:T(8,128)S(1)}, u32[]{:S(2)}, u32[]{:S(2)}) collective-permute-start(f32[136,128]{1,0:T(8,128)S(1)} %get-tuple-element.68), channel_id=1, source_target_pairs={{0,4},{4,0},{8,12},{12,8},{16,20},{20,16},{24,28},{28,24},{1,5},{5... | collective-permute-start | bytes 208904 | tf_op jit(solution)/shard_map/ppermute | solution.py:257
  8.8 4.2 %collective-permute-done = f32[128,128]{1,0:T(8,128)S(1)} collective-permute-done((f32[128,128]{1,0:T(8,128)S(1)}, f32[128,128]{1,0:T(8,128)S(1)}, u32[]{:S(2)}, u32[]{:S(2)}) %collective-permute-start) | collective-permute-done | bytes 65568 | tf_op jit(solution)/shard_map/ppermute | solution.py:257
  13.0 1.6 %collective-permute-start.1 = (f32[128,128]{1,0:T(8,128)S(1)}, f32[128,128]{1,0:T(8,128)S(1)}, u32[]{:S(2)}, u32[]{:S(2)}) collective-permute-start(f32[128,128]{1,0:T(8,128)S(1)} %add.114), channel_id=1, source_target_pairs={{0,8},{4,12},{8,0},{12,4},{16,24},{20,28},{24,16},{28,20},{1,9},{5... | collective-permute-start | bytes 196616 | tf_op jit(solution)/shard_map/ppermute | solution.py:257
  15.1 1.9 %shard_map.78 = (bf16[128,128,128]{2,1,0:T(8,128)(2,1)S(1)}, bf16[128,128,128]{2,1,0:T(8,128)(2,1)S(1)}) custom-call(s32[2,256]{1,0:T(2,128)S(1)} %get-tuple-element.69.order_ref, bf16[256,128,128]{2,1,0:T(8,128)(2,1)S(1)} %get-tuple-element.70.blocks_ref), custom_call_target="tpu_custom_call" | custom-call | flops 2000000000 | bytes 1048576 | tf_op jit(solution)/shard_map/pallas_call | solution.py:240
  17.8 2.7 %collective-permute-start.2 = (f32[128,128]{1,0:T(8,128)S(1)}, f32[128,128]{1,0:T(8,128)S(1)}, u32[]{:S(2)}, u32[]{:S(2)}) collective-permute-start(f32[128,128]{1,0:T(8,128)S(1)} %add.115), channel_id=1, source_target_pairs={{0,16},{4,20},{8,24},{12,28},{16,0},{20,4},{24,8},{28,12},{1,17},{... | collective-permute-start | bytes 196616 | tf_op jit(solution)/shard_map/ppermute | solution.py:257
  20.5 1.8 %collective-permute-start.5 = (f32[136,128]{1,0:T(8,128)S(1)}, f32[136,128]{1,0:T(8,128)S(1)}, u32[]{:S(2)}, u32[]{:S(2)}) collective-permute-start(f32[136,128]{1,0:T(8,128)S(1)} %add.118), channel_id=1, source_target_pairs={{0,16},{4,20},{8,24},{12,28},{16,0},{20,4},{24,8},{28,12},{1,17},{... | collective-permute-start | bytes 208904 | tf_op jit(solution)/shard_map/ppermute | solution.py:257
  22.2 1.9 %shard_map.77 = (bf16[128,128,128]{2,1,0:T(8,128)(2,1)S(1)}, bf16[128,128,128]{2,1,0:T(8,128)(2,1)S(1)}) custom-call(s32[2,256]{1,0:T(2,128)S(1)} %get-tuple-element.69.order_ref, bf16[256,128,128]{2,1,0:T(8,128)(2,1)S(1)} %get-tuple-element.70.blocks_ref), custom_call_target="tpu_custom_call" | custom-call | flops 2000000000 | bytes 1048576 | tf_op jit(solution)/shard_map/pallas_call | solution.py:240
  24.7 1.8 %collective-permute-done.5 = f32[136,128]{1,0:T(8,128)S(1)} collective-permute-done((f32[136,128]{1,0:T(8,128)S(1)}, f32[136,128]{1,0:T(8,128)S(1)}, u32[]{:S(2)}, u32[]{:S(2)}) %collective-permute-start.5) | collective-permute-done | bytes 69664 | tf_op jit(solution)/shard_map/ppermute | solution.py:257
  28.5 1.6 %collective-permute-start.6 = (f32[128,128]{1,0:T(8,128)S(1)}, f32[128,128]{1,0:T(8,128)S(1)}, u32[]{:S(2)}, u32[]{:S(2)}) collective-permute-start(f32[128,128]{1,0:T(8,128)S(1)} %get-tuple-element.76), channel_id=1, source_target_pairs={{0,2},{1,3},{2,0},{3,1},{4,6},{5,7},{6,4},{7,5},{8,10},{9,11},{10,... | collective-permute-start | bytes 196616 | tf_op jit(solution)/shard_map/ppermute | solution.py:257
  30.1 1.2 %collective-permute-start.9 = (f32[136,128]{1,0:T(8,128)S(1)}, f32[136,128]{1,0:T(8,128)S(1)}, u32[]{:S(2)}, u32[]{:S(2)}) collective-permute-start(f32[136,128]{1,0:T(8,128)S(1)} %add.122), channel_id=1, source_target_pairs={{0,2},{1,3},{2,0},{3,1},{4,6},{5,7},{6,4},{7,5},{8,10},{9,11},{10,... | collective-permute-start | bytes 208904 | tf_op jit(solution)/shard_map/ppermute | solution.py:257
  31.3 1.7 %collective-permute-done.6 = f32[128,128]{1,0:T(8,128)S(1)} collective-permute-done((f32[128,128]{1,0:T(8,128)S(1)}, f32[128,128]{1,0:T(8,128)S(1)}, u32[]{:S(2)}, u32[]{:S(2)}) %collective-permute-start.6) | collective-permute-done | bytes 65568 | tf_op jit(solution)/shard_map/ppermute | solution.py:257
  33.2 1.2 %collective-permute-done.7 = f32[128,128]{1,0:T(8,128)S(1)} collective-permute-done((f32[128,128]{1,0:T(8,128)S(1)}, f32[128,128]{1,0:T(8,128)S(1)}, u32[]{:S(2)}, u32[]{:S(2)}) %collective-permute-start.7) | collective-permute-done | bytes 65568 | tf_op jit(solution)/shard_map/ppermute | solution.py:257
  35.3 1.1 shard_map.82
  36.5 2.0 %collective-permute-start.10 = (f32[128,128]{1,0:T(8,128)S(1)}, f32[128,128]{1,0:T(8,128)S(1)}, u32[]{:S(2)}, u32[]{:S(2)}) collective-permute-start(f32[128,128]{1,0:T(8,128)S(1)} %get-tuple-element.84), channel_id=1, source_target_pairs={{0,4},{4,0},{8,12},{12,8},{16,20},{20,16},{24,28},{28,24},{1,5},{5... | collective-permute-start | bytes 196616 | tf_op jit(solution)/shard_map/ppermute | solution.py:257
  38.5 2.9 %collective-permute-done.13 = f32[136,128]{1,0:T(8,128)S(1)} collective-permute-done((f32[136,128]{1,0:T(8,128)S(1)}, f32[136,128]{1,0:T(8,128)S(1)}, u32[]{:S(2)}, u32[]{:S(2)}) %collective-permute-start.13) | collective-permute-done | bytes 69664 | tf_op jit(solution)/shard_map/ppermute | solution.py:257
  42.1 1.5 %collective-permute-start.11 = (f32[128,128]{1,0:T(8,128)S(1)}, f32[128,128]{1,0:T(8,128)S(1)}, u32[]{:S(2)}, u32[]{:S(2)}) collective-permute-start(f32[128,128]{1,0:T(8,128)S(1)} %add.124), channel_id=1, source_target_pairs={{0,8},{4,12},{8,0},{12,4},{16,24},{20,28},{24,16},{28,20},{1,9},{5... | collective-permute-start | bytes 196616 | tf_op jit(solution)/shard_map/ppermute | solution.py:257
  43.6 2.2 %collective-permute-done.14 = f32[136,128]{1,0:T(8,128)S(1)} collective-permute-done((f32[136,128]{1,0:T(8,128)S(1)}, f32[136,128]{1,0:T(8,128)S(1)}, u32[]{:S(2)}, u32[]{:S(2)}) %collective-permute-start.14) | collective-permute-done | bytes 69664 | tf_op jit(solution)/shard_map/ppermute | solution.py:257
  45.8 1.1 collective-permute-start.15
  46.9 1.9 %collective-permute-start.12 = (f32[128,128]{1,0:T(8,128)S(1)}, f32[128,128]{1,0:T(8,128)S(1)}, u32[]{:S(2)}, u32[]{:S(2)}) collective-permute-start(f32[128,128]{1,0:T(8,128)S(1)} %add.125), channel_id=1, source_target_pairs={{0,16},{4,20},{8,24},{12,28},{16,0},{20,4},{24,8},{28,12},{1,17},{... | collective-permute-start | bytes 196616 | tf_op jit(solution)/shard_map/ppermute | solution.py:257
  48.9 3.5 %collective-permute-done.12 = f32[128,128]{1,0:T(8,128)S(1)} collective-permute-done((f32[128,128]{1,0:T(8,128)S(1)}, f32[128,128]{1,0:T(8,128)S(1)}, u32[]{:S(2)}, u32[]{:S(2)}) %collective-permute-start.12) | collective-permute-done | bytes 65568 | tf_op jit(solution)/shard_map/ppermute | solution.py:257
  53.2 1.3 %shard_map.84 = (f32[128,128]{1,0:T(8,128)S(1)}, f32[136,128]{1,0:T(8,128)S(1)}, f32[256,128]{1,0:T(8,128)S(1)}) custom-call(s32[8,128]{1,0:T(8,128)S(1)} %get-tuple-element.64.number_ref, bf16[256,256]{1,0:T(8,128)(2,1)S(1)} %get-tuple-element.65.pick_ref, bf16[256,256]{1,0:T(8,128)(2,1)S(1)} %get-tuple-element.66.put_ref, f32[128,128]{1,0:T(8,128)S(1)} %add.126.top_in_ref, ...), custom_call_target="tpu_custom_call" | custom-call | flops 2000000000 | bytes 1048576 | tf_op jit(solution)/shard_map/pallas_call | solution.py:240
  54.6 1.9 %collective-permute-start.16 = (f32[128,128]{1,0:T(8,128)S(1)}, f32[128,128]{1,0:T(8,128)S(1)}, u32[]{:S(2)}, u32[]{:S(2)}) collective-permute-start(f32[128,128]{1,0:T(8,128)S(1)} %get-tuple-element.90), channel_id=1, source_target_pairs={{0,2},{1,3},{2,0},{3,1},{4,6},{5,7},{6,4},{7,5},{8,10},{9,11},{10,... | collective-permute-start | bytes 196616 | tf_op jit(solution)/shard_map/ppermute | solution.py:257
  56.5 1.2 %collective-permute-start.19 = (f32[136,128]{1,0:T(8,128)S(1)}, f32[136,128]{1,0:T(8,128)S(1)}, u32[]{:S(2)}, u32[]{:S(2)}) collective-permute-start(f32[136,128]{1,0:T(8,128)S(1)} %add.132), channel_id=1, source_target_pairs={{0,2},{1,3},{2,0},{3,1},{4,6},{5,7},{6,4},{7,5},{8,10},{9,11},{10,... | collective-permute-start | bytes 208904 | tf_op jit(solution)/shard_map/ppermute | solution.py:257
  57.8 1.4 %collective-permute-done.16 = f32[128,128]{1,0:T(8,128)S(1)} collective-permute-done((f32[128,128]{1,0:T(8,128)S(1)}, f32[128,128]{1,0:T(8,128)S(1)}, u32[]{:S(2)}, u32[]{:S(2)}) %collective-permute-start.16) | collective-permute-done | bytes 65568 | tf_op jit(solution)/shard_map/ppermute | solution.py:257
  59.3 1.2 %collective-permute-done.17 = f32[128,128]{1,0:T(8,128)S(1)} collective-permute-done((f32[128,128]{1,0:T(8,128)S(1)}, f32[128,128]{1,0:T(8,128)S(1)}, u32[]{:S(2)}, u32[]{:S(2)}) %collective-permute-start.17) | collective-permute-done | bytes 65568 | tf_op jit(solution)/shard_map/ppermute | solution.py:257
  61.7 1.1 shard_map.86
  62.9 1.5 %collective-permute-start.23 = (f32[136,128]{1,0:T(8,128)S(1)}, f32[136,128]{1,0:T(8,128)S(1)}, u32[]{:S(2)}, u32[]{:S(2)}) collective-permute-start(f32[136,128]{1,0:T(8,128)S(1)} %get-tuple-element.97), channel_id=1, source_target_pairs={{0,4},{4,0},{8,12},{12,8},{16,20},{20,16},{24,28},{28,24},{1,5},{5... | collective-permute-start | bytes 208904 | tf_op jit(solution)/shard_map/ppermute | solution.py:257
  65.0 3.0 %collective-permute-done.23 = f32[136,128]{1,0:T(8,128)S(1)} collective-permute-done((f32[136,128]{1,0:T(8,128)S(1)}, f32[136,128]{1,0:T(8,128)S(1)}, u32[]{:S(2)}, u32[]{:S(2)}) %collective-permute-start.23) | collective-permute-done | bytes 69664 | tf_op jit(solution)/shard_map/ppermute | solution.py:257
  67.9 1.2 %collective-permute-start.24 = (f32[136,128]{1,0:T(8,128)S(1)}, f32[136,128]{1,0:T(8,128)S(1)}, u32[]{:S(2)}, u32[]{:S(2)}) collective-permute-start(f32[136,128]{1,0:T(8,128)S(1)} %add.137), channel_id=1, source_target_pairs={{0,8},{4,12},{8,0},{12,4},{16,24},{20,28},{24,16},{28,20},{1,9},{5... | collective-permute-start | bytes 208904 | tf_op jit(solution)/shard_map/ppermute | solution.py:257
  70.1 2.2 %collective-permute-done.24 = f32[136,128]{1,0:T(8,128)S(1)} collective-permute-done((f32[136,128]{1,0:T(8,128)S(1)}, f32[136,128]{1,0:T(8,128)S(1)}, u32[]{:S(2)}, u32[]{:S(2)}) %collective-permute-start.24) | collective-permute-done | bytes 69664 | tf_op jit(solution)/shard_map/ppermute | solution.py:257
  72.3 1.4 %collective-permute-start.25 = (f32[136,128]{1,0:T(8,128)S(1)}, f32[136,128]{1,0:T(8,128)S(1)}, u32[]{:S(2)}, u32[]{:S(2)}) collective-permute-start(f32[136,128]{1,0:T(8,128)S(1)} %add.138), channel_id=1, source_target_pairs={{0,16},{4,20},{8,24},{12,28},{16,0},{20,4},{24,8},{28,12},{1,17},{... | collective-permute-start | bytes 208904 | tf_op jit(solution)/shard_map/ppermute | solution.py:257
  74.2 1.6 %collective-permute-start.22 = (f32[128,128]{1,0:T(8,128)S(1)}, f32[128,128]{1,0:T(8,128)S(1)}, u32[]{:S(2)}, u32[]{:S(2)}) collective-permute-start(f32[128,128]{1,0:T(8,128)S(1)} %add.135), channel_id=1, source_target_pairs={{0,16},{4,20},{8,24},{12,28},{16,0},{20,4},{24,8},{28,12},{1,17},{... | collective-permute-start | bytes 196616 | tf_op jit(solution)/shard_map/ppermute | solution.py:257
  75.7 3.7 %collective-permute-done.22 = f32[128,128]{1,0:T(8,128)S(1)} collective-permute-done((f32[128,128]{1,0:T(8,128)S(1)}, f32[128,128]{1,0:T(8,128)S(1)}, u32[]{:S(2)}, u32[]{:S(2)}) %collective-permute-start.22) | collective-permute-done | bytes 65568 | tf_op jit(solution)/shard_map/ppermute | solution.py:257
  80.3 1.1 shard_map.88
  81.5 2.2 %collective-permute-start.26 = (f32[128,128]{1,0:T(8,128)S(1)}, f32[128,128]{1,0:T(8,128)S(1)}, u32[]{:S(2)}, u32[]{:S(2)}) collective-permute-start(f32[128,128]{1,0:T(8,128)S(1)} %get-tuple-element.102), channel_id=1, source_target_pairs={{0,2},{1,3},{2,0},{3,1},{4,6},{5,7},{6,4},{7,5},{8,10},{9,11},{10,... | collective-permute-start | bytes 196616 | tf_op jit(solution)/shard_map/ppermute | solution.py:257
  83.7 1.2 %collective-permute-start.29 = (f32[136,128]{1,0:T(8,128)S(1)}, f32[136,128]{1,0:T(8,128)S(1)}, u32[]{:S(2)}, u32[]{:S(2)}) collective-permute-start(f32[136,128]{1,0:T(8,128)S(1)} %add.142), channel_id=1, source_target_pairs={{0,2},{1,3},{2,0},{3,1},{4,6},{5,7},{6,4},{7,5},{8,10},{9,11},{10,... | collective-permute-start | bytes 208904 | tf_op jit(solution)/shard_map/ppermute | solution.py:257
  84.9 1.4 %collective-permute-done.26 = f32[128,128]{1,0:T(8,128)S(1)} collective-permute-done((f32[128,128]{1,0:T(8,128)S(1)}, f32[128,128]{1,0:T(8,128)S(1)}, u32[]{:S(2)}, u32[]{:S(2)}) %collective-permute-start.26) | collective-permute-done | bytes 65568 | tf_op jit(solution)/shard_map/ppermute | solution.py:257
  86.5 1.2 %collective-permute-done.27 = f32[128,128]{1,0:T(8,128)S(1)} collective-permute-done((f32[128,128]{1,0:T(8,128)S(1)}, f32[128,128]{1,0:T(8,128)S(1)}, u32[]{:S(2)}, u32[]{:S(2)}) %collective-permute-start.27) | collective-permute-done | bytes 65568 | tf_op jit(solution)/shard_map/ppermute | solution.py:257
  90.9 1.2 %collective-permute-start.30 = (f32[128,128]{1,0:T(8,128)S(1)}, f32[128,128]{1,0:T(8,128)S(1)}, u32[]{:S(2)}, u32[]{:S(2)}) collective-permute-start(f32[128,128]{1,0:T(8,128)S(1)} %get-tuple-element.109), channel_id=1, source_target_pairs={{0,4},{4,0},{8,12},{12,8},{16,20},{20,16},{24,28},{28,24},{1,5},{5... | collective-permute-start | bytes 196616 | tf_op jit(solution)/shard_map/ppermute | solution.py:257
  92.1 2.6 %collective-permute-done.33 = f32[136,128]{1,0:T(8,128)S(1)} collective-permute-done((f32[136,128]{1,0:T(8,128)S(1)}, f32[136,128]{1,0:T(8,128)S(1)}, u32[]{:S(2)}, u32[]{:S(2)}) %collective-permute-start.33) | collective-permute-done | bytes 69664 | tf_op jit(solution)/shard_map/ppermute | solution.py:257
  94.7 1.3 %collective-permute-start.34 = (f32[136,128]{1,0:T(8,128)S(1)}, f32[136,128]{1,0:T(8,128)S(1)}, u32[]{:S(2)}, u32[]{:S(2)}) collective-permute-start(f32[136,128]{1,0:T(8,128)S(1)} %add.147), channel_id=1, source_target_pairs={{0,8},{4,12},{8,0},{12,4},{16,24},{20,28},{24,16},{28,20},{1,9},{5... | collective-permute-start | bytes 208904 | tf_op jit(solution)/shard_map/ppermute | solution.py:257
  96.9 2.2 %collective-permute-done.34 = f32[136,128]{1,0:T(8,128)S(1)} collective-permute-done((f32[136,128]{1,0:T(8,128)S(1)}, f32[136,128]{1,0:T(8,128)S(1)}, u32[]{:S(2)}, u32[]{:S(2)}) %collective-permute-start.34) | collective-permute-done | bytes 69664 | tf_op jit(solution)/shard_map/ppermute | solution.py:257
  99.1 1.7 %collective-permute-start.35 = (f32[136,128]{1,0:T(8,128)S(1)}, f32[136,128]{1,0:T(8,128)S(1)}, u32[]{:S(2)}, u32[]{:S(2)}) collective-permute-start(f32[136,128]{1,0:T(8,128)S(1)} %add.148), channel_id=1, source_target_pairs={{0,16},{4,20},{8,24},{12,28},{16,0},{20,4},{24,8},{28,12},{1,17},{... | collective-permute-start | bytes 208904 | tf_op jit(solution)/shard_map/ppermute | solution.py:257
  101.1 1.5 %collective-permute-start.32 = (f32[128,128]{1,0:T(8,128)S(1)}, f32[128,128]{1,0:T(8,128)S(1)}, u32[]{:S(2)}, u32[]{:S(2)}) collective-permute-start(f32[128,128]{1,0:T(8,128)S(1)} %add.145), channel_id=1, source_target_pairs={{0,16},{4,20},{8,24},{12,28},{16,0},{20,4},{24,8},{28,12},{1,17},{... | collective-permute-start | bytes 196616 | tf_op jit(solution)/shard_map/ppermute | solution.py:257
  102.6 3.7 %collective-permute-done.32 = f32[128,128]{1,0:T(8,128)S(1)} collective-permute-done((f32[128,128]{1,0:T(8,128)S(1)}, f32[128,128]{1,0:T(8,128)S(1)}, u32[]{:S(2)}, u32[]{:S(2)}) %collective-permute-start.32) | collective-permute-done | bytes 65568 | tf_op jit(solution)/shard_map/ppermute | solution.py:257
  106.6 1.2 %collective-permute-done.36 = f32[8,128]{1,0:T(8,128)S(1)} collective-permute-done((f32[8,128]{1,0:T(8,128)S(1)}, f32[8,128]{1,0:T(8,128)S(1)}, u32[]{:S(2)}, u32[]{:S(2)}) %collective-permute-start.36) | collective-permute-done | bytes 4128 | tf_op jit(solution)/shard_map/ppermute | solution.py:257
  107.8 2.2 %collective-permute-start.37 = (f32[8,128]{1,0:T(8,128)S(1)}, f32[8,128]{1,0:T(8,128)S(1)}, u32[]{:S(2)}, u32[]{:S(2)}) collective-permute-start(f32[8,128]{1,0:T(8,128)S(1)} %add.150), channel_id=1, source_target_pairs={{0,2},{1,3},{2,0},{3,1},{4,6},{5,7},{6,4},{7,5},{8,10},{9,11},{10,... | collective-permute-start | bytes 12296 | tf_op jit(solution)/shard_map/ppermute | solution.py:257
  (84 shorter events, 18.0 us)
Async XLA Ops:
  5.7 9.0 %collective-permute-start.3 = (f32[136,128]{1,0:T(8,128)S(1)}, f32[136,128]{1,0:T(8,128)S(1)}, u32[]{:S(2)}, u32[]{:S(2)}) collective-permute-start(f32[136,128]{1,0:T(8,128)S(1)} %get-tuple-element.68), channel_id=1, source_target_pairs={{0,4},{4,0},{8,12},{12,8},{16,20},{20,16},{24,28},{28,24},{1,5},{5... | collective-permute-start | bytes 208904 | tf_op jit(solution)/shard_map/ppermute | solution.py:257
  8.7 4.3 %collective-permute-start = (f32[128,128]{1,0:T(8,128)S(1)}, f32[128,128]{1,0:T(8,128)S(1)}, u32[]{:S(2)}, u32[]{:S(2)}) collective-permute-start(f32[128,128]{1,0:T(8,128)S(1)} %get-tuple-element.67), channel_id=1, source_target_pairs={{0,4},{4,0},{8,12},{12,8},{16,20},{20,16},{24,28},{28,24},{1,5},{5... | collective-permute-start | bytes 196616 | tf_op jit(solution)/shard_map/ppermute | solution.py:257
  13.0 4.8 %collective-permute-start.1 = (f32[128,128]{1,0:T(8,128)S(1)}, f32[128,128]{1,0:T(8,128)S(1)}, u32[]{:S(2)}, u32[]{:S(2)}) collective-permute-start(f32[128,128]{1,0:T(8,128)S(1)} %add.114), channel_id=1, source_target_pairs={{0,8},{4,12},{8,0},{12,4},{16,24},{20,28},{24,16},{28,20},{1,9},{5... | collective-permute-start | bytes 196616 | tf_op jit(solution)/shard_map/ppermute | solution.py:257
  14.6 5.8 %collective-permute-start.4 = (f32[136,128]{1,0:T(8,128)S(1)}, f32[136,128]{1,0:T(8,128)S(1)}, u32[]{:S(2)}, u32[]{:S(2)}) collective-permute-start(f32[136,128]{1,0:T(8,128)S(1)} %add.117), channel_id=1, source_target_pairs={{0,8},{4,12},{8,0},{12,4},{16,24},{20,28},{24,16},{28,20},{1,9},{5... | collective-permute-start | bytes 208904 | tf_op jit(solution)/shard_map/ppermute | solution.py:257
  17.8 6.9 %collective-permute-start.2 = (f32[128,128]{1,0:T(8,128)S(1)}, f32[128,128]{1,0:T(8,128)S(1)}, u32[]{:S(2)}, u32[]{:S(2)}) collective-permute-start(f32[128,128]{1,0:T(8,128)S(1)} %add.115), channel_id=1, source_target_pairs={{0,16},{4,20},{8,24},{12,28},{16,0},{20,4},{24,8},{28,12},{1,17},{... | collective-permute-start | bytes 196616 | tf_op jit(solution)/shard_map/ppermute | solution.py:257
  20.5 6.0 %collective-permute-start.5 = (f32[136,128]{1,0:T(8,128)S(1)}, f32[136,128]{1,0:T(8,128)S(1)}, u32[]{:S(2)}, u32[]{:S(2)}) collective-permute-start(f32[136,128]{1,0:T(8,128)S(1)} %add.118), channel_id=1, source_target_pairs={{0,16},{4,20},{8,24},{12,28},{16,0},{20,4},{24,8},{28,12},{1,17},{... | collective-permute-start | bytes 208904 | tf_op jit(solution)/shard_map/ppermute | solution.py:257
  28.4 1.7 %collective-permute-start.8 = (f32[136,128]{1,0:T(8,128)S(1)}, f32[136,128]{1,0:T(8,128)S(1)}, u32[]{:S(2)}, u32[]{:S(2)}) collective-permute-start(f32[136,128]{1,0:T(8,128)S(1)} %get-tuple-element.77), channel_id=1, source_target_pairs={{0,1},{1,0},{2,3},{3,2},{4,5},{5,4},{6,7},{7,6},{8,9},{9,8},{10,11... | collective-permute-start | bytes 208904 | tf_op jit(solution)/shard_map/ppermute | solution.py:257
  28.5 4.6 %collective-permute-start.6 = (f32[128,128]{1,0:T(8,128)S(1)}, f32[128,128]{1,0:T(8,128)S(1)}, u32[]{:S(2)}, u32[]{:S(2)}) collective-permute-start(f32[128,128]{1,0:T(8,128)S(1)} %get-tuple-element.76), channel_id=1, source_target_pairs={{0,2},{1,3},{2,0},{3,1},{4,6},{5,7},{6,4},{7,5},{8,10},{9,11},{10,... | collective-permute-start | bytes 196616 | tf_op jit(solution)/shard_map/ppermute | solution.py:257
  30.1 4.4 %collective-permute-start.9 = (f32[136,128]{1,0:T(8,128)S(1)}, f32[136,128]{1,0:T(8,128)S(1)}, u32[]{:S(2)}, u32[]{:S(2)}) collective-permute-start(f32[136,128]{1,0:T(8,128)S(1)} %add.122), channel_id=1, source_target_pairs={{0,2},{1,3},{2,0},{3,1},{4,6},{5,7},{6,4},{7,5},{8,10},{9,11},{10,... | collective-permute-start | bytes 208904 | tf_op jit(solution)/shard_map/ppermute | solution.py:257
  33.1 1.3 %collective-permute-start.7 = (f32[128,128]{1,0:T(8,128)S(1)}, f32[128,128]{1,0:T(8,128)S(1)}, u32[]{:S(2)}, u32[]{:S(2)}) collective-permute-start(f32[128,128]{1,0:T(8,128)S(1)} %add.120), channel_id=1, source_target_pairs={{0,1},{1,0},{2,3},{3,2},{4,5},{5,4},{6,7},{7,6},{8,9},{9,8},{10,11... | collective-permute-start | bytes 196616 | tf_op jit(solution)/shard_map/ppermute | solution.py:257
  36.4 5.0 %collective-permute-start.13 = (f32[136,128]{1,0:T(8,128)S(1)}, f32[136,128]{1,0:T(8,128)S(1)}, u32[]{:S(2)}, u32[]{:S(2)}) collective-permute-start(f32[136,128]{1,0:T(8,128)S(1)} %get-tuple-element.85), channel_id=1, source_target_pairs={{0,4},{4,0},{8,12},{12,8},{16,20},{20,16},{24,28},{28,24},{1,5},{5... | collective-permute-start | bytes 208904 | tf_op jit(solution)/shard_map/ppermute | solution.py:257
  36.5 5.6 %collective-permute-start.10 = (f32[128,128]{1,0:T(8,128)S(1)}, f32[128,128]{1,0:T(8,128)S(1)}, u32[]{:S(2)}, u32[]{:S(2)}) collective-permute-start(f32[128,128]{1,0:T(8,128)S(1)} %get-tuple-element.84), channel_id=1, source_target_pairs={{0,4},{4,0},{8,12},{12,8},{16,20},{20,16},{24,28},{28,24},{1,5},{5... | collective-permute-start | bytes 196616 | tf_op jit(solution)/shard_map/ppermute | solution.py:257
  41.4 4.4 %collective-permute-start.14 = (f32[136,128]{1,0:T(8,128)S(1)}, f32[136,128]{1,0:T(8,128)S(1)}, u32[]{:S(2)}, u32[]{:S(2)}) collective-permute-start(f32[136,128]{1,0:T(8,128)S(1)} %add.127), channel_id=1, source_target_pairs={{0,8},{4,12},{8,0},{12,4},{16,24},{20,28},{24,16},{28,20},{1,9},{5... | collective-permute-start | bytes 208904 | tf_op jit(solution)/shard_map/ppermute | solution.py:257
  42.1 4.8 %collective-permute-start.11 = (f32[128,128]{1,0:T(8,128)S(1)}, f32[128,128]{1,0:T(8,128)S(1)}, u32[]{:S(2)}, u32[]{:S(2)}) collective-permute-start(f32[128,128]{1,0:T(8,128)S(1)} %add.124), channel_id=1, source_target_pairs={{0,8},{4,12},{8,0},{12,4},{16,24},{20,28},{24,16},{28,20},{1,9},{5... | collective-permute-start | bytes 196616 | tf_op jit(solution)/shard_map/ppermute | solution.py:257
  45.8 6.6 %collective-permute-start.15 = (f32[136,128]{1,0:T(8,128)S(1)}, f32[136,128]{1,0:T(8,128)S(1)}, u32[]{:S(2)}, u32[]{:S(2)}) collective-permute-start(f32[136,128]{1,0:T(8,128)S(1)} %add.128), channel_id=1, source_target_pairs={{0,16},{4,20},{8,24},{12,28},{16,0},{20,4},{24,8},{28,12},{1,17},{... | collective-permute-start | bytes 208904 | tf_op jit(solution)/shard_map/ppermute | solution.py:257
  46.9 5.5 %collective-permute-start.12 = (f32[128,128]{1,0:T(8,128)S(1)}, f32[128,128]{1,0:T(8,128)S(1)}, u32[]{:S(2)}, u32[]{:S(2)}) collective-permute-start(f32[128,128]{1,0:T(8,128)S(1)} %add.125), channel_id=1, source_target_pairs={{0,16},{4,20},{8,24},{12,28},{16,0},{20,4},{24,8},{28,12},{1,17},{... | collective-permute-start | bytes 196616 | tf_op jit(solution)/shard_map/ppermute | solution.py:257
  54.5 2.0 %collective-permute-start.18 = (f32[136,128]{1,0:T(8,128)S(1)}, f32[136,128]{1,0:T(8,128)S(1)}, u32[]{:S(2)}, u32[]{:S(2)}) collective-permute-start(f32[136,128]{1,0:T(8,128)S(1)} %get-tuple-element.91), channel_id=1, source_target_pairs={{0,1},{1,0},{2,3},{3,2},{4,5},{5,4},{6,7},{7,6},{8,9},{9,8},{10,11... | collective-permute-start | bytes 208904 | tf_op jit(solution)/shard_map/ppermute | solution.py:257
  54.6 4.6 %collective-permute-start.16 = (f32[128,128]{1,0:T(8,128)S(1)}, f32[128,128]{1,0:T(8,128)S(1)}, u32[]{:S(2)}, u32[]{:S(2)}) collective-permute-start(f32[128,128]{1,0:T(8,128)S(1)} %get-tuple-element.90), channel_id=1, source_target_pairs={{0,2},{1,3},{2,0},{3,1},{4,6},{5,7},{6,4},{7,5},{8,10},{9,11},{10,... | collective-permute-start | bytes 196616 | tf_op jit(solution)/shard_map/ppermute | solution.py:257
  56.5 4.4 %collective-permute-start.19 = (f32[136,128]{1,0:T(8,128)S(1)}, f32[136,128]{1,0:T(8,128)S(1)}, u32[]{:S(2)}, u32[]{:S(2)}) collective-permute-start(f32[136,128]{1,0:T(8,128)S(1)} %add.132), channel_id=1, source_target_pairs={{0,2},{1,3},{2,0},{3,1},{4,6},{5,7},{6,4},{7,5},{8,10},{9,11},{10,... | collective-permute-start | bytes 208904 | tf_op jit(solution)/shard_map/ppermute | solution.py:257
  59.2 1.3 %collective-permute-start.17 = (f32[128,128]{1,0:T(8,128)S(1)}, f32[128,128]{1,0:T(8,128)S(1)}, u32[]{:S(2)}, u32[]{:S(2)}) collective-permute-start(f32[128,128]{1,0:T(8,128)S(1)} %add.130), channel_id=1, source_target_pairs={{0,1},{1,0},{2,3},{3,2},{4,5},{5,4},{6,7},{7,6},{8,9},{9,8},{10,11... | collective-permute-start | bytes 196616 | tf_op jit(solution)/shard_map/ppermute | solution.py:257
  62.9 5.1 %collective-permute-start.23 = (f32[136,128]{1,0:T(8,128)S(1)}, f32[136,128]{1,0:T(8,128)S(1)}, u32[]{:S(2)}, u32[]{:S(2)}) collective-permute-start(f32[136,128]{1,0:T(8,128)S(1)} %get-tuple-element.97), channel_id=1, source_target_pairs={{0,4},{4,0},{8,12},{12,8},{16,20},{20,16},{24,28},{28,24},{1,5},{5... | collective-permute-start | bytes 208904 | tf_op jit(solution)/shard_map/ppermute | solution.py:257
  64.4 4.7 %collective-permute-start.20 = (f32[128,128]{1,0:T(8,128)S(1)}, f32[128,128]{1,0:T(8,128)S(1)}, u32[]{:S(2)}, u32[]{:S(2)}) collective-permute-start(f32[128,128]{1,0:T(8,128)S(1)} %get-tuple-element.96), channel_id=1, source_target_pairs={{0,4},{4,0},{8,12},{12,8},{16,20},{20,16},{24,28},{28,24},{1,5},{5... | collective-permute-start | bytes 196616 | tf_op jit(solution)/shard_map/ppermute | solution.py:257
  67.9 4.4 %collective-permute-start.24 = (f32[136,128]{1,0:T(8,128)S(1)}, f32[136,128]{1,0:T(8,128)S(1)}, u32[]{:S(2)}, u32[]{:S(2)}) collective-permute-start(f32[136,128]{1,0:T(8,128)S(1)} %add.137), channel_id=1, source_target_pairs={{0,8},{4,12},{8,0},{12,4},{16,24},{20,28},{24,16},{28,20},{1,9},{5... | collective-permute-start | bytes 208904 | tf_op jit(solution)/shard_map/ppermute | solution.py:257
  69.1 5.0 %collective-permute-start.21 = (f32[128,128]{1,0:T(8,128)S(1)}, f32[128,128]{1,0:T(8,128)S(1)}, u32[]{:S(2)}, u32[]{:S(2)}) collective-permute-start(f32[128,128]{1,0:T(8,128)S(1)} %add.134), channel_id=1, source_target_pairs={{0,8},{4,12},{8,0},{12,4},{16,24},{20,28},{24,16},{28,20},{1,9},{5... | collective-permute-start | bytes 196616 | tf_op jit(solution)/shard_map/ppermute | solution.py:257
  72.3 7.1 %collective-permute-start.25 = (f32[136,128]{1,0:T(8,128)S(1)}, f32[136,128]{1,0:T(8,128)S(1)}, u32[]{:S(2)}, u32[]{:S(2)}) collective-permute-start(f32[136,128]{1,0:T(8,128)S(1)} %add.138), channel_id=1, source_target_pairs={{0,16},{4,20},{8,24},{12,28},{16,0},{20,4},{24,8},{28,12},{1,17},{... | collective-permute-start | bytes 208904 | tf_op jit(solution)/shard_map/ppermute | solution.py:257
  74.2 5.2 %collective-permute-start.22 = (f32[128,128]{1,0:T(8,128)S(1)}, f32[128,128]{1,0:T(8,128)S(1)}, u32[]{:S(2)}, u32[]{:S(2)}) collective-permute-start(f32[128,128]{1,0:T(8,128)S(1)} %add.135), channel_id=1, source_target_pairs={{0,16},{4,20},{8,24},{12,28},{16,0},{20,4},{24,8},{28,12},{1,17},{... | collective-permute-start | bytes 196616 | tf_op jit(solution)/shard_map/ppermute | solution.py:257
  81.4 2.3 %collective-permute-start.28 = (f32[136,128]{1,0:T(8,128)S(1)}, f32[136,128]{1,0:T(8,128)S(1)}, u32[]{:S(2)}, u32[]{:S(2)}) collective-permute-start(f32[136,128]{1,0:T(8,128)S(1)} %get-tuple-element.103), channel_id=1, source_target_pairs={{0,1},{1,0},{2,3},{3,2},{4,5},{5,4},{6,7},{7,6},{8,9},{9,8},{10,11... | collective-permute-start | bytes 208904 | tf_op jit(solution)/shard_map/ppermute | solution.py:257
  81.5 4.9 %collective-permute-start.26 = (f32[128,128]{1,0:T(8,128)S(1)}, f32[128,128]{1,0:T(8,128)S(1)}, u32[]{:S(2)}, u32[]{:S(2)}) collective-permute-start(f32[128,128]{1,0:T(8,128)S(1)} %get-tuple-element.102), channel_id=1, source_target_pairs={{0,2},{1,3},{2,0},{3,1},{4,6},{5,7},{6,4},{7,5},{8,10},{9,11},{10,... | collective-permute-start | bytes 196616 | tf_op jit(solution)/shard_map/ppermute | solution.py:257
  83.7 4.4 %collective-permute-start.29 = (f32[136,128]{1,0:T(8,128)S(1)}, f32[136,128]{1,0:T(8,128)S(1)}, u32[]{:S(2)}, u32[]{:S(2)}) collective-permute-start(f32[136,128]{1,0:T(8,128)S(1)} %add.142), channel_id=1, source_target_pairs={{0,2},{1,3},{2,0},{3,1},{4,6},{5,7},{6,4},{7,5},{8,10},{9,11},{10,... | collective-permute-start | bytes 208904 | tf_op jit(solution)/shard_map/ppermute | solution.py:257
  86.4 1.3 %collective-permute-start.27 = (f32[128,128]{1,0:T(8,128)S(1)}, f32[128,128]{1,0:T(8,128)S(1)}, u32[]{:S(2)}, u32[]{:S(2)}) collective-permute-start(f32[128,128]{1,0:T(8,128)S(1)} %add.140), channel_id=1, source_target_pairs={{0,1},{1,0},{2,3},{3,2},{4,5},{5,4},{6,7},{7,6},{8,9},{9,8},{10,11... | collective-permute-start | bytes 196616 | tf_op jit(solution)/shard_map/ppermute | solution.py:257
  90.0 4.7 %collective-permute-start.33 = (f32[136,128]{1,0:T(8,128)S(1)}, f32[136,128]{1,0:T(8,128)S(1)}, u32[]{:S(2)}, u32[]{:S(2)}) collective-permute-start(f32[136,128]{1,0:T(8,128)S(1)} %get-tuple-element.110), channel_id=1, source_target_pairs={{0,4},{4,0},{8,12},{12,8},{16,20},{20,16},{24,28},{28,24},{1,5},{5... | collective-permute-start | bytes 208904 | tf_op jit(solution)/shard_map/ppermute | solution.py:257
  90.9 5.1 %collective-permute-start.30 = (f32[128,128]{1,0:T(8,128)S(1)}, f32[128,128]{1,0:T(8,128)S(1)}, u32[]{:S(2)}, u32[]{:S(2)}) collective-permute-start(f32[128,128]{1,0:T(8,128)S(1)} %get-tuple-element.109), channel_id=1, source_target_pairs={{0,4},{4,0},{8,12},{12,8},{16,20},{20,16},{24,28},{28,24},{1,5},{5... | collective-permute-start | bytes 196616 | tf_op jit(solution)/shard_map/ppermute | solution.py:257
  94.7 4.4 %collective-permute-start.34 = (f32[136,128]{1,0:T(8,128)S(1)}, f32[136,128]{1,0:T(8,128)S(1)}, u32[]{:S(2)}, u32[]{:S(2)}) collective-permute-start(f32[136,128]{1,0:T(8,128)S(1)} %add.147), channel_id=1, source_target_pairs={{0,8},{4,12},{8,0},{12,4},{16,24},{20,28},{24,16},{28,20},{1,9},{5... | collective-permute-start | bytes 208904 | tf_op jit(solution)/shard_map/ppermute | solution.py:257
  96.0 5.1 %collective-permute-start.31 = (f32[128,128]{1,0:T(8,128)S(1)}, f32[128,128]{1,0:T(8,128)S(1)}, u32[]{:S(2)}, u32[]{:S(2)}) collective-permute-start(f32[128,128]{1,0:T(8,128)S(1)} %add.144), channel_id=1, source_target_pairs={{0,8},{4,12},{8,0},{12,4},{16,24},{20,28},{24,16},{28,20},{1,9},{5... | collective-permute-start | bytes 196616 | tf_op jit(solution)/shard_map/ppermute | solution.py:257
  99.1 7.3 %collective-permute-start.35 = (f32[136,128]{1,0:T(8,128)S(1)}, f32[136,128]{1,0:T(8,128)S(1)}, u32[]{:S(2)}, u32[]{:S(2)}) collective-permute-start(f32[136,128]{1,0:T(8,128)S(1)} %add.148), channel_id=1, source_target_pairs={{0,16},{4,20},{8,24},{12,28},{16,0},{20,4},{24,8},{28,12},{1,17},{... | collective-permute-start | bytes 208904 | tf_op jit(solution)/shard_map/ppermute | solution.py:257
  101.1 5.2 %collective-permute-start.32 = (f32[128,128]{1,0:T(8,128)S(1)}, f32[128,128]{1,0:T(8,128)S(1)}, u32[]{:S(2)}, u32[]{:S(2)}) collective-permute-start(f32[128,128]{1,0:T(8,128)S(1)} %add.145), channel_id=1, source_target_pairs={{0,16},{4,20},{8,24},{12,28},{16,0},{20,4},{24,8},{28,12},{1,17},{... | collective-permute-start | bytes 196616 | tf_op jit(solution)/shard_map/ppermute | solution.py:257
  106.5 1.2 %collective-permute-start.36 = (f32[8,128]{1,0:T(8,128)S(1)}, f32[8,128]{1,0:T(8,128)S(1)}, u32[]{:S(2)}, u32[]{:S(2)}) collective-permute-start(f32[8,128]{1,0:T(8,128)S(1)} %get-tuple-element.114), channel_id=1, source_target_pairs={{0,1},{1,0},{2,3},{3,2},{4,5},{5,4},{6,7},{7,6},{8,9},{9,8},{10,11... | collective-permute-start | bytes 12296 | tf_op jit(solution)/shard_map/ppermute | solution.py:257
  107.8 3.7 %collective-permute-start.37 = (f32[8,128]{1,0:T(8,128)S(1)}, f32[8,128]{1,0:T(8,128)S(1)}, u32[]{:S(2)}, u32[]{:S(2)}) collective-permute-start(f32[8,128]{1,0:T(8,128)S(1)} %add.150), channel_id=1, source_target_pairs={{0,2},{1,3},{2,0},{3,1},{4,6},{5,7},{6,4},{7,5},{8,10},{9,11},{10,... | collective-permute-start | bytes 12296 | tf_op jit(solution)/shard_map/ppermute | solution.py:257

commit v5 on v4

--- a/solution.py
+++ b/solution.py
@@ -164,9 +164,10 @@
     blocks_refs, refs = refs[:pieces], refs[pieces:]
     *previous, top_ref, low_ref, vector_ref, picked_ref, prod_ref = refs
     top = top_in_ref.shape[0]
-    vector_ref[:top] = recur(top_in_ref[...], norm_ref[:1], previous, slice(0, top))
-    vector_ref[top:] = low_vector_ref[...]
-    vector = vector_ref[...]
+    vector = jnp.concatenate(
+        [recur(top_in_ref[...], norm_ref[:1], previous, slice(0, top)), low_vector_ref[...]], 0
+    )
+    vector_ref[...] = vector
     slots, early, share = pick_ref.shape[0], early_ref.shape[0], blocks_refs[0].shape[0]
     picked = pick_pieces(pick_ref[early:], vector)
     prod_ref[:early] = early_ref[...]

time: 112 us -> 112 us (level)
  no operation moved by 1% of the time
where the time goes in v5:
time: 112 us
  waiting for transfers between devices  45.2 us (40%)
  starting transfers between devices  43.6 us (39%)
  Pallas kernels  21.5 us (19%)
  between operations  1.6 us (1%)
    ppermute x38, waiting for transfers between devices, all_sum(): other = lax.ppermute(chunks[at], axis, pairs)  45.2 us
    ppermute x38, starting transfers between devices, all_sum(): other = lax.ppermute(chunks[at], axis, pairs)  43.6 us
    pallas_call x18, Pallas kernels, call(): pl.pallas_call(kernel, out_shape=[jax.ShapeDtypeStruct(o, jnp.float32) if...  21.5 us
  transfers between devices with their start and end apart: 38, of which 27 were waited for; matrix products, arithmetic and copies ran while one was open for 0% of the time, Pallas kernels for 4%

profile of v5, /device:TPU:0, one launch (start us, length us, event | category | flops | bytes accessed | tf_op | source)
XLA Modules:
  0.0 112.3 jit_solution(872653644905383217)
XLA Ops:
  1.3 4.4 %shard_map.76 = (f32[128,128]{1,0:T(8,128)S(1)}, f32[136,128]{1,0:T(8,128)S(1)}, f32[256,128]{1,0:T(8,128)S(1)}, bf16[256,256]{1,0:T(8,128)(2,1)S(1)}, bf16[256,...) custom-call(s32[1,256]{1,0:T(1,128)} %bitcast.9, ...), custom_call_target="tpu_custom_call" | custom-call | flops 2000000000 | bytes 1048576 | tf_op jit(solution)/shard_map/pallas_call | solution.py:241
  5.7 3.0 %collective-permute-start.3 = (f32[136,128]{1,0:T(8,128)S(1)}, f32[136,128]{1,0:T(8,128)S(1)}, u32[]{:S(2)}, u32[]{:S(2)}) collective-permute-start(f32[136,128]{1,0:T(8,128)S(1)} %get-tuple-element.68), channel_id=1, source_target_pairs={{0,4},{4,0},{8,12},{12,8},{16,20},{20,16},{24,28},{28,24},{1,5},{5... | collective-permute-start | bytes 208904 | tf_op jit(solution)/shard_map/ppermute | solution.py:258
  8.8 4.2 %collective-permute-done = f32[128,128]{1,0:T(8,128)S(1)} collective-permute-done((f32[128,128]{1,0:T(8,128)S(1)}, f32[128,128]{1,0:T(8,128)S(1)}, u32[]{:S(2)}, u32[]{:S(2)}) %collective-permute-start) | collective-permute-done | bytes 65568 | tf_op jit(solution)/shard_map/ppermute | solution.py:258
  13.0 1.6 %collective-permute-start.1 = (f32[128,128]{1,0:T(8,128)S(1)}, f32[128,128]{1,0:T(8,128)S(1)}, u32[]{:S(2)}, u32[]{:S(2)}) collective-permute-start(f32[128,128]{1,0:T(8,128)S(1)} %add.114), channel_id=1, source_target_pairs={{0,8},{4,12},{8,0},{12,4},{16,24},{20,28},{24,16},{28,20},{1,9},{5... | collective-permute-start | bytes 196616 | tf_op jit(solution)/shard_map/ppermute | solution.py:258
  15.1 1.9 %shard_map.78 = (bf16[128,128,128]{2,1,0:T(8,128)(2,1)S(1)}, bf16[128,128,128]{2,1,0:T(8,128)(2,1)S(1)}) custom-call(s32[2,256]{1,0:T(2,128)S(1)} %get-tuple-element.69.order_ref, bf16[256,128,128]{2,1,0:T(8,128)(2,1)S(1)} %get-tuple-element.70.blocks_ref), custom_call_target="tpu_custom_call" | custom-call | flops 2000000000 | bytes 1048576 | tf_op jit(solution)/shard_map/pallas_call | solution.py:241
  17.8 2.7 %collective-permute-start.2 = (f32[128,128]{1,0:T(8,128)S(1)}, f32[128,128]{1,0:T(8,128)S(1)}, u32[]{:S(2)}, u32[]{:S(2)}) collective-permute-start(f32[128,128]{1,0:T(8,128)S(1)} %add.115), channel_id=1, source_target_pairs={{0,16},{4,20},{8,24},{12,28},{16,0},{20,4},{24,8},{28,12},{1,17},{... | collective-permute-start | bytes 196616 | tf_op jit(solution)/shard_map/ppermute | solution.py:258
  20.5 1.8 %collective-permute-start.5 = (f32[136,128]{1,0:T(8,128)S(1)}, f32[136,128]{1,0:T(8,128)S(1)}, u32[]{:S(2)}, u32[]{:S(2)}) collective-permute-start(f32[136,128]{1,0:T(8,128)S(1)} %add.118), channel_id=1, source_target_pairs={{0,16},{4,20},{8,24},{12,28},{16,0},{20,4},{24,8},{28,12},{1,17},{... | collective-permute-start | bytes 208904 | tf_op jit(solution)/shard_map/ppermute | solution.py:258
  22.2 1.9 %shard_map.77 = (bf16[128,128,128]{2,1,0:T(8,128)(2,1)S(1)}, bf16[128,128,128]{2,1,0:T(8,128)(2,1)S(1)}) custom-call(s32[2,256]{1,0:T(2,128)S(1)} %get-tuple-element.69.order_ref, bf16[256,128,128]{2,1,0:T(8,128)(2,1)S(1)} %get-tuple-element.70.blocks_ref), custom_call_target="tpu_custom_call" | custom-call | flops 2000000000 | bytes 1048576 | tf_op jit(solution)/shard_map/pallas_call | solution.py:241
  24.7 1.8 %collective-permute-done.5 = f32[136,128]{1,0:T(8,128)S(1)} collective-permute-done((f32[136,128]{1,0:T(8,128)S(1)}, f32[136,128]{1,0:T(8,128)S(1)}, u32[]{:S(2)}, u32[]{:S(2)}) %collective-permute-start.5) | collective-permute-done | bytes 69664 | tf_op jit(solution)/shard_map/ppermute | solution.py:258
  28.5 1.6 %collective-permute-start.6 = (f32[128,128]{1,0:T(8,128)S(1)}, f32[128,128]{1,0:T(8,128)S(1)}, u32[]{:S(2)}, u32[]{:S(2)}) collective-permute-start(f32[128,128]{1,0:T(8,128)S(1)} %get-tuple-element.76), channel_id=1, source_target_pairs={{0,2},{1,3},{2,0},{3,1},{4,6},{5,7},{6,4},{7,5},{8,10},{9,11},{10,... | collective-permute-start | bytes 196616 | tf_op jit(solution)/shard_map/ppermute | solution.py:258
  30.1 1.2 %collective-permute-start.9 = (f32[136,128]{1,0:T(8,128)S(1)}, f32[136,128]{1,0:T(8,128)S(1)}, u32[]{:S(2)}, u32[]{:S(2)}) collective-permute-start(f32[136,128]{1,0:T(8,128)S(1)} %add.122), channel_id=1, source_target_pairs={{0,2},{1,3},{2,0},{3,1},{4,6},{5,7},{6,4},{7,5},{8,10},{9,11},{10,... | collective-permute-start | bytes 208904 | tf_op jit(solution)/shard_map/ppermute | solution.py:258
  31.3 1.7 %collective-permute-done.6 = f32[128,128]{1,0:T(8,128)S(1)} collective-permute-done((f32[128,128]{1,0:T(8,128)S(1)}, f32[128,128]{1,0:T(8,128)S(1)}, u32[]{:S(2)}, u32[]{:S(2)}) %collective-permute-start.6) | collective-permute-done | bytes 65568 | tf_op jit(solution)/shard_map/ppermute | solution.py:258
  33.2 1.2 %collective-permute-done.7 = f32[128,128]{1,0:T(8,128)S(1)} collective-permute-done((f32[128,128]{1,0:T(8,128)S(1)}, f32[128,128]{1,0:T(8,128)S(1)}, u32[]{:S(2)}, u32[]{:S(2)}) %collective-permute-start.7) | collective-permute-done | bytes 65568 | tf_op jit(solution)/shard_map/ppermute | solution.py:258
  35.3 1.1 shard_map.82
  36.5 2.0 %collective-permute-start.10 = (f32[128,128]{1,0:T(8,128)S(1)}, f32[128,128]{1,0:T(8,128)S(1)}, u32[]{:S(2)}, u32[]{:S(2)}) collective-permute-start(f32[128,128]{1,0:T(8,128)S(1)} %get-tuple-element.84), channel_id=1, source_target_pairs={{0,4},{4,0},{8,12},{12,8},{16,20},{20,16},{24,28},{28,24},{1,5},{5... | collective-permute-start | bytes 196616 | tf_op jit(solution)/shard_map/ppermute | solution.py:258
  38.5 2.9 %collective-permute-done.13 = f32[136,128]{1,0:T(8,128)S(1)} collective-permute-done((f32[136,128]{1,0:T(8,128)S(1)}, f32[136,128]{1,0:T(8,128)S(1)}, u32[]{:S(2)}, u32[]{:S(2)}) %collective-permute-start.13) | collective-permute-done | bytes 69664 | tf_op jit(solution)/shard_map/ppermute | solution.py:258
  42.1 1.5 %collective-permute-start.11 = (f32[128,128]{1,0:T(8,128)S(1)}, f32[128,128]{1,0:T(8,128)S(1)}, u32[]{:S(2)}, u32[]{:S(2)}) collective-permute-start(f32[128,128]{1,0:T(8,128)S(1)} %add.124), channel_id=1, source_target_pairs={{0,8},{4,12},{8,0},{12,4},{16,24},{20,28},{24,16},{28,20},{1,9},{5... | collective-permute-start | bytes 196616 | tf_op jit(solution)/shard_map/ppermute | solution.py:258
  43.6 2.2 %collective-permute-done.14 = f32[136,128]{1,0:T(8,128)S(1)} collective-permute-done((f32[136,128]{1,0:T(8,128)S(1)}, f32[136,128]{1,0:T(8,128)S(1)}, u32[]{:S(2)}, u32[]{:S(2)}) %collective-permute-start.14) | collective-permute-done | bytes 69664 | tf_op jit(solution)/shard_map/ppermute | solution.py:258
  45.8 1.1 collective-permute-start.15
  46.9 1.9 %collective-permute-start.12 = (f32[128,128]{1,0:T(8,128)S(1)}, f32[128,128]{1,0:T(8,128)S(1)}, u32[]{:S(2)}, u32[]{:S(2)}) collective-permute-start(f32[128,128]{1,0:T(8,128)S(1)} %add.125), channel_id=1, source_target_pairs={{0,16},{4,20},{8,24},{12,28},{16,0},{20,4},{24,8},{28,12},{1,17},{... | collective-permute-start | bytes 196616 | tf_op jit(solution)/shard_map/ppermute | solution.py:258
  48.9 3.5 %collective-permute-done.12 = f32[128,128]{1,0:T(8,128)S(1)} collective-permute-done((f32[128,128]{1,0:T(8,128)S(1)}, f32[128,128]{1,0:T(8,128)S(1)}, u32[]{:S(2)}, u32[]{:S(2)}) %collective-permute-start.12) | collective-permute-done | bytes 65568 | tf_op jit(solution)/shard_map/ppermute | solution.py:258
  53.2 1.3 %shard_map.84 = (f32[128,128]{1,0:T(8,128)S(1)}, f32[136,128]{1,0:T(8,128)S(1)}, f32[256,128]{1,0:T(8,128)S(1)}) custom-call(s32[8,128]{1,0:T(8,128)S(1)} %get-tuple-element.64.number_ref, bf16[256,256]{1,0:T(8,128)(2,1)S(1)} %get-tuple-element.65.pick_ref, bf16[256,256]{1,0:T(8,128)(2,1)S(1)} %get-tuple-element.66.put_ref, f32[128,128]{1,0:T(8,128)S(1)} %add.126.top_in_ref, ...), custom_call_target="tpu_custom_call" | custom-call | flops 2000000000 | bytes 1048576 | tf_op jit(solution)/shard_map/pallas_call | solution.py:241
  54.6 1.9 %collective-permute-start.16 = (f32[128,128]{1,0:T(8,128)S(1)}, f32[128,128]{1,0:T(8,128)S(1)}, u32[]{:S(2)}, u32[]{:S(2)}) collective-permute-start(f32[128,128]{1,0:T(8,128)S(1)} %get-tuple-element.90), channel_id=1, source_target_pairs={{0,2},{1,3},{2,0},{3,1},{4,6},{5,7},{6,4},{7,5},{8,10},{9,11},{10,... | collective-permute-start | bytes 196616 | tf_op jit(solution)/shard_map/ppermute | solution.py:258
  56.5 1.2 %collective-permute-start.19 = (f32[136,128]{1,0:T(8,128)S(1)}, f32[136,128]{1,0:T(8,128)S(1)}, u32[]{:S(2)}, u32[]{:S(2)}) collective-permute-start(f32[136,128]{1,0:T(8,128)S(1)} %add.132), channel_id=1, source_target_pairs={{0,2},{1,3},{2,0},{3,1},{4,6},{5,7},{6,4},{7,5},{8,10},{9,11},{10,... | collective-permute-start | bytes 208904 | tf_op jit(solution)/shard_map/ppermute | solution.py:258
  57.8 1.4 %collective-permute-done.16 = f32[128,128]{1,0:T(8,128)S(1)} collective-permute-done((f32[128,128]{1,0:T(8,128)S(1)}, f32[128,128]{1,0:T(8,128)S(1)}, u32[]{:S(2)}, u32[]{:S(2)}) %collective-permute-start.16) | collective-permute-done | bytes 65568 | tf_op jit(solution)/shard_map/ppermute | solution.py:258
  59.3 1.2 %collective-permute-done.17 = f32[128,128]{1,0:T(8,128)S(1)} collective-permute-done((f32[128,128]{1,0:T(8,128)S(1)}, f32[128,128]{1,0:T(8,128)S(1)}, u32[]{:S(2)}, u32[]{:S(2)}) %collective-permute-start.17) | collective-permute-done | bytes 65568 | tf_op jit(solution)/shard_map/ppermute | solution.py:258
  61.7 1.1 shard_map.86
  62.9 1.5 %collective-permute-start.23 = (f32[136,128]{1,0:T(8,128)S(1)}, f32[136,128]{1,0:T(8,128)S(1)}, u32[]{:S(2)}, u32[]{:S(2)}) collective-permute-start(f32[136,128]{1,0:T(8,128)S(1)} %get-tuple-element.97), channel_id=1, source_target_pairs={{0,4},{4,0},{8,12},{12,8},{16,20},{20,16},{24,28},{28,24},{1,5},{5... | collective-permute-start | bytes 208904 | tf_op jit(solution)/shard_map/ppermute | solution.py:258
  65.0 3.0 %collective-permute-done.23 = f32[136,128]{1,0:T(8,128)S(1)} collective-permute-done((f32[136,128]{1,0:T(8,128)S(1)}, f32[136,128]{1,0:T(8,128)S(1)}, u32[]{:S(2)}, u32[]{:S(2)}) %collective-permute-start.23) | collective-permute-done | bytes 69664 | tf_op jit(solution)/shard_map/ppermute | solution.py:258
  67.9 1.2 %collective-permute-start.24 = (f32[136,128]{1,0:T(8,128)S(1)}, f32[136,128]{1,0:T(8,128)S(1)}, u32[]{:S(2)}, u32[]{:S(2)}) collective-permute-start(f32[136,128]{1,0:T(8,128)S(1)} %add.137), channel_id=1, source_target_pairs={{0,8},{4,12},{8,0},{12,4},{16,24},{20,28},{24,16},{28,20},{1,9},{5... | collective-permute-start | bytes 208904 | tf_op jit(solution)/shard_map/ppermute | solution.py:258
  70.1 2.2 %collective-permute-done.24 = f32[136,128]{1,0:T(8,128)S(1)} collective-permute-done((f32[136,128]{1,0:T(8,128)S(1)}, f32[136,128]{1,0:T(8,128)S(1)}, u32[]{:S(2)}, u32[]{:S(2)}) %collective-permute-start.24) | collective-permute-done | bytes 69664 | tf_op jit(solution)/shard_map/ppermute | solution.py:258
  72.3 1.4 %collective-permute-start.25 = (f32[136,128]{1,0:T(8,128)S(1)}, f32[136,128]{1,0:T(8,128)S(1)}, u32[]{:S(2)}, u32[]{:S(2)}) collective-permute-start(f32[136,128]{1,0:T(8,128)S(1)} %add.138), channel_id=1, source_target_pairs={{0,16},{4,20},{8,24},{12,28},{16,0},{20,4},{24,8},{28,12},{1,17},{... | collective-permute-start | bytes 208904 | tf_op jit(solution)/shard_map/ppermute | solution.py:258
  74.2 1.6 %collective-permute-start.22 = (f32[128,128]{1,0:T(8,128)S(1)}, f32[128,128]{1,0:T(8,128)S(1)}, u32[]{:S(2)}, u32[]{:S(2)}) collective-permute-start(f32[128,128]{1,0:T(8,128)S(1)} %add.135), channel_id=1, source_target_pairs={{0,16},{4,20},{8,24},{12,28},{16,0},{20,4},{24,8},{28,12},{1,17},{... | collective-permute-start | bytes 196616 | tf_op jit(solution)/shard_map/ppermute | solution.py:258
  75.7 3.7 %collective-permute-done.22 = f32[128,128]{1,0:T(8,128)S(1)} collective-permute-done((f32[128,128]{1,0:T(8,128)S(1)}, f32[128,128]{1,0:T(8,128)S(1)}, u32[]{:S(2)}, u32[]{:S(2)}) %collective-permute-start.22) | collective-permute-done | bytes 65568 | tf_op jit(solution)/shard_map/ppermute | solution.py:258
  80.3 1.1 shard_map.88
  81.5 2.2 %collective-permute-start.26 = (f32[128,128]{1,0:T(8,128)S(1)}, f32[128,128]{1,0:T(8,128)S(1)}, u32[]{:S(2)}, u32[]{:S(2)}) collective-permute-start(f32[128,128]{1,0:T(8,128)S(1)} %get-tuple-element.102), channel_id=1, source_target_pairs={{0,2},{1,3},{2,0},{3,1},{4,6},{5,7},{6,4},{7,5},{8,10},{9,11},{10,... | collective-permute-start | bytes 196616 | tf_op jit(solution)/shard_map/ppermute | solution.py:258
  83.7 1.2 %collective-permute-start.29 = (f32[136,128]{1,0:T(8,128)S(1)}, f32[136,128]{1,0:T(8,128)S(1)}, u32[]{:S(2)}, u32[]{:S(2)}) collective-permute-start(f32[136,128]{1,0:T(8,128)S(1)} %add.142), channel_id=1, source_target_pairs={{0,2},{1,3},{2,0},{3,1},{4,6},{5,7},{6,4},{7,5},{8,10},{9,11},{10,... | collective-permute-start | bytes 208904 | tf_op jit(solution)/shard_map/ppermute | solution.py:258
  84.9 1.4 %collective-permute-done.26 = f32[128,128]{1,0:T(8,128)S(1)} collective-permute-done((f32[128,128]{1,0:T(8,128)S(1)}, f32[128,128]{1,0:T(8,128)S(1)}, u32[]{:S(2)}, u32[]{:S(2)}) %collective-permute-start.26) | collective-permute-done | bytes 65568 | tf_op jit(solution)/shard_map/ppermute | solution.py:258
  86.5 1.2 %collective-permute-done.27 = f32[128,128]{1,0:T(8,128)S(1)} collective-permute-done((f32[128,128]{1,0:T(8,128)S(1)}, f32[128,128]{1,0:T(8,128)S(1)}, u32[]{:S(2)}, u32[]{:S(2)}) %collective-permute-start.27) | collective-permute-done | bytes 65568 | tf_op jit(solution)/shard_map/ppermute | solution.py:258
  90.9 1.2 %collective-permute-start.30 = (f32[128,128]{1,0:T(8,128)S(1)}, f32[128,128]{1,0:T(8,128)S(1)}, u32[]{:S(2)}, u32[]{:S(2)}) collective-permute-start(f32[128,128]{1,0:T(8,128)S(1)} %get-tuple-element.109), channel_id=1, source_target_pairs={{0,4},{4,0},{8,12},{12,8},{16,20},{20,16},{24,28},{28,24},{1,5},{5... | collective-permute-start | bytes 196616 | tf_op jit(solution)/shard_map/ppermute | solution.py:258
  92.1 2.6 %collective-permute-done.33 = f32[136,128]{1,0:T(8,128)S(1)} collective-permute-done((f32[136,128]{1,0:T(8,128)S(1)}, f32[136,128]{1,0:T(8,128)S(1)}, u32[]{:S(2)}, u32[]{:S(2)}) %collective-permute-start.33) | collective-permute-done | bytes 69664 | tf_op jit(solution)/shard_map/ppermute | solution.py:258
  94.7 1.3 %collective-permute-start.34 = (f32[136,128]{1,0:T(8,128)S(1)}, f32[136,128]{1,0:T(8,128)S(1)}, u32[]{:S(2)}, u32[]{:S(2)}) collective-permute-start(f32[136,128]{1,0:T(8,128)S(1)} %add.147), channel_id=1, source_target_pairs={{0,8},{4,12},{8,0},{12,4},{16,24},{20,28},{24,16},{28,20},{1,9},{5... | collective-permute-start | bytes 208904 | tf_op jit(solution)/shard_map/ppermute | solution.py:258
  96.9 2.2 %collective-permute-done.34 = f32[136,128]{1,0:T(8,128)S(1)} collective-permute-done((f32[136,128]{1,0:T(8,128)S(1)}, f32[136,128]{1,0:T(8,128)S(1)}, u32[]{:S(2)}, u32[]{:S(2)}) %collective-permute-start.34) | collective-permute-done | bytes 69664 | tf_op jit(solution)/shard_map/ppermute | solution.py:258
  99.1 1.7 %collective-permute-start.35 = (f32[136,128]{1,0:T(8,128)S(1)}, f32[136,128]{1,0:T(8,128)S(1)}, u32[]{:S(2)}, u32[]{:S(2)}) collective-permute-start(f32[136,128]{1,0:T(8,128)S(1)} %add.148), channel_id=1, source_target_pairs={{0,16},{4,20},{8,24},{12,28},{16,0},{20,4},{24,8},{28,12},{1,17},{... | collective-permute-start | bytes 208904 | tf_op jit(solution)/shard_map/ppermute | solution.py:258
  101.1 1.5 %collective-permute-start.32 = (f32[128,128]{1,0:T(8,128)S(1)}, f32[128,128]{1,0:T(8,128)S(1)}, u32[]{:S(2)}, u32[]{:S(2)}) collective-permute-start(f32[128,128]{1,0:T(8,128)S(1)} %add.145), channel_id=1, source_target_pairs={{0,16},{4,20},{8,24},{12,28},{16,0},{20,4},{24,8},{28,12},{1,17},{... | collective-permute-start | bytes 196616 | tf_op jit(solution)/shard_map/ppermute | solution.py:258
  102.6 3.7 %collective-permute-done.32 = f32[128,128]{1,0:T(8,128)S(1)} collective-permute-done((f32[128,128]{1,0:T(8,128)S(1)}, f32[128,128]{1,0:T(8,128)S(1)}, u32[]{:S(2)}, u32[]{:S(2)}) %collective-permute-start.32) | collective-permute-done | bytes 65568 | tf_op jit(solution)/shard_map/ppermute | solution.py:258
  106.6 1.2 %collective-permute-done.36 = f32[8,128]{1,0:T(8,128)S(1)} collective-permute-done((f32[8,128]{1,0:T(8,128)S(1)}, f32[8,128]{1,0:T(8,128)S(1)}, u32[]{:S(2)}, u32[]{:S(2)}) %collective-permute-start.36) | collective-permute-done | bytes 4128 | tf_op jit(solution)/shard_map/ppermute | solution.py:258
  107.8 2.2 %collective-permute-start.37 = (f32[8,128]{1,0:T(8,128)S(1)}, f32[8,128]{1,0:T(8,128)S(1)}, u32[]{:S(2)}, u32[]{:S(2)}) collective-permute-start(f32[8,128]{1,0:T(8,128)S(1)} %add.150), channel_id=1, source_target_pairs={{0,2},{1,3},{2,0},{3,1},{4,6},{5,7},{6,4},{7,5},{8,10},{9,11},{10,... | collective-permute-start | bytes 12296 | tf_op jit(solution)/shard_map/ppermute | solution.py:258
  (84 shorter events, 18.0 us)
Async XLA Ops:
  5.7 9.0 %collective-permute-start.3 = (f32[136,128]{1,0:T(8,128)S(1)}, f32[136,128]{1,0:T(8,128)S(1)}, u32[]{:S(2)}, u32[]{:S(2)}) collective-permute-start(f32[136,128]{1,0:T(8,128)S(1)} %get-tuple-element.68), channel_id=1, source_target_pairs={{0,4},{4,0},{8,12},{12,8},{16,20},{20,16},{24,28},{28,24},{1,5},{5... | collective-permute-start | bytes 208904 | tf_op jit(solution)/shard_map/ppermute | solution.py:258
  8.7 4.3 %collective-permute-start = (f32[128,128]{1,0:T(8,128)S(1)}, f32[128,128]{1,0:T(8,128)S(1)}, u32[]{:S(2)}, u32[]{:S(2)}) collective-permute-start(f32[128,128]{1,0:T(8,128)S(1)} %get-tuple-element.67), channel_id=1, source_target_pairs={{0,4},{4,0},{8,12},{12,8},{16,20},{20,16},{24,28},{28,24},{1,5},{5... | collective-permute-start | bytes 196616 | tf_op jit(solution)/shard_map/ppermute | solution.py:258
  13.0 4.8 %collective-permute-start.1 = (f32[128,128]{1,0:T(8,128)S(1)}, f32[128,128]{1,0:T(8,128)S(1)}, u32[]{:S(2)}, u32[]{:S(2)}) collective-permute-start(f32[128,128]{1,0:T(8,128)S(1)} %add.114), channel_id=1, source_target_pairs={{0,8},{4,12},{8,0},{12,4},{16,24},{20,28},{24,16},{28,20},{1,9},{5... | collective-permute-start | bytes 196616 | tf_op jit(solution)/shard_map/ppermute | solution.py:258
  14.6 5.8 %collective-permute-start.4 = (f32[136,128]{1,0:T(8,128)S(1)}, f32[136,128]{1,0:T(8,128)S(1)}, u32[]{:S(2)}, u32[]{:S(2)}) collective-permute-start(f32[136,128]{1,0:T(8,128)S(1)} %add.117), channel_id=1, source_target_pairs={{0,8},{4,12},{8,0},{12,4},{16,24},{20,28},{24,16},{28,20},{1,9},{5... | collective-permute-start | bytes 208904 | tf_op jit(solution)/shard_map/ppermute | solution.py:258
  17.8 6.9 %collective-permute-start.2 = (f32[128,128]{1,0:T(8,128)S(1)}, f32[128,128]{1,0:T(8,128)S(1)}, u32[]{:S(2)}, u32[]{:S(2)}) collective-permute-start(f32[128,128]{1,0:T(8,128)S(1)} %add.115), channel_id=1, source_target_pairs={{0,16},{4,20},{8,24},{12,28},{16,0},{20,4},{24,8},{28,12},{1,17},{... | collective-permute-start | bytes 196616 | tf_op jit(solution)/shard_map/ppermute | solution.py:258
  20.5 6.0 %collective-permute-start.5 = (f32[136,128]{1,0:T(8,128)S(1)}, f32[136,128]{1,0:T(8,128)S(1)}, u32[]{:S(2)}, u32[]{:S(2)}) collective-permute-start(f32[136,128]{1,0:T(8,128)S(1)} %add.118), channel_id=1, source_target_pairs={{0,16},{4,20},{8,24},{12,28},{16,0},{20,4},{24,8},{28,12},{1,17},{... | collective-permute-start | bytes 208904 | tf_op jit(solution)/shard_map/ppermute | solution.py:258
  28.4 1.7 %collective-permute-start.8 = (f32[136,128]{1,0:T(8,128)S(1)}, f32[136,128]{1,0:T(8,128)S(1)}, u32[]{:S(2)}, u32[]{:S(2)}) collective-permute-start(f32[136,128]{1,0:T(8,128)S(1)} %get-tuple-element.77), channel_id=1, source_target_pairs={{0,1},{1,0},{2,3},{3,2},{4,5},{5,4},{6,7},{7,6},{8,9},{9,8},{10,11... | collective-permute-start | bytes 208904 | tf_op jit(solution)/shard_map/ppermute | solution.py:258
  28.5 4.6 %collective-permute-start.6 = (f32[128,128]{1,0:T(8,128)S(1)}, f32[128,128]{1,0:T(8,128)S(1)}, u32[]{:S(2)}, u32[]{:S(2)}) collective-permute-start(f32[128,128]{1,0:T(8,128)S(1)} %get-tuple-element.76), channel_id=1, source_target_pairs={{0,2},{1,3},{2,0},{3,1},{4,6},{5,7},{6,4},{7,5},{8,10},{9,11},{10,... | collective-permute-start | bytes 196616 | tf_op jit(solution)/shard_map/ppermute | solution.py:258
  30.1 4.4 %collective-permute-start.9 = (f32[136,128]{1,0:T(8,128)S(1)}, f32[136,128]{1,0:T(8,128)S(1)}, u32[]{:S(2)}, u32[]{:S(2)}) collective-permute-start(f32[136,128]{1,0:T(8,128)S(1)} %add.122), channel_id=1, source_target_pairs={{0,2},{1,3},{2,0},{3,1},{4,6},{5,7},{6,4},{7,5},{8,10},{9,11},{10,... | collective-permute-start | bytes 208904 | tf_op jit(solution)/shard_map/ppermute | solution.py:258
  33.1 1.3 %collective-permute-start.7 = (f32[128,128]{1,0:T(8,128)S(1)}, f32[128,128]{1,0:T(8,128)S(1)}, u32[]{:S(2)}, u32[]{:S(2)}) collective-permute-start(f32[128,128]{1,0:T(8,128)S(1)} %add.120), channel_id=1, source_target_pairs={{0,1},{1,0},{2,3},{3,2},{4,5},{5,4},{6,7},{7,6},{8,9},{9,8},{10,11... | collective-permute-start | bytes 196616 | tf_op jit(solution)/shard_map/ppermute | solution.py:258
  36.4 5.0 %collective-permute-start.13 = (f32[136,128]{1,0:T(8,128)S(1)}, f32[136,128]{1,0:T(8,128)S(1)}, u32[]{:S(2)}, u32[]{:S(2)}) collective-permute-start(f32[136,128]{1,0:T(8,128)S(1)} %get-tuple-element.85), channel_id=1, source_target_pairs={{0,4},{4,0},{8,12},{12,8},{16,20},{20,16},{24,28},{28,24},{1,5},{5... | collective-permute-start | bytes 208904 | tf_op jit(solution)/shard_map/ppermute | solution.py:258
  36.5 5.6 %collective-permute-start.10 = (f32[128,128]{1,0:T(8,128)S(1)}, f32[128,128]{1,0:T(8,128)S(1)}, u32[]{:S(2)}, u32[]{:S(2)}) collective-permute-start(f32[128,128]{1,0:T(8,128)S(1)} %get-tuple-element.84), channel_id=1, source_target_pairs={{0,4},{4,0},{8,12},{12,8},{16,20},{20,16},{24,28},{28,24},{1,5},{5... | collective-permute-start | bytes 196616 | tf_op jit(solution)/shard_map/ppermute | solution.py:258
  41.4 4.4 %collective-permute-start.14 = (f32[136,128]{1,0:T(8,128)S(1)}, f32[136,128]{1,0:T(8,128)S(1)}, u32[]{:S(2)}, u32[]{:S(2)}) collective-permute-start(f32[136,128]{1,0:T(8,128)S(1)} %add.127), channel_id=1, source_target_pairs={{0,8},{4,12},{8,0},{12,4},{16,24},{20,28},{24,16},{28,20},{1,9},{5... | collective-permute-start | bytes 208904 | tf_op jit(solution)/shard_map/ppermute | solution.py:258
  42.1 4.8 %collective-permute-start.11 = (f32[128,128]{1,0:T(8,128)S(1)}, f32[128,128]{1,0:T(8,128)S(1)}, u32[]{:S(2)}, u32[]{:S(2)}) collective-permute-start(f32[128,128]{1,0:T(8,128)S(1)} %add.124), channel_id=1, source_target_pairs={{0,8},{4,12},{8,0},{12,4},{16,24},{20,28},{24,16},{28,20},{1,9},{5... | collective-permute-start | bytes 196616 | tf_op jit(solution)/shard_map/ppermute | solution.py:258
  45.8 6.6 %collective-permute-start.15 = (f32[136,128]{1,0:T(8,128)S(1)}, f32[136,128]{1,0:T(8,128)S(1)}, u32[]{:S(2)}, u32[]{:S(2)}) collective-permute-start(f32[136,128]{1,0:T(8,128)S(1)} %add.128), channel_id=1, source_target_pairs={{0,16},{4,20},{8,24},{12,28},{16,0},{20,4},{24,8},{28,12},{1,17},{... | collective-permute-start | bytes 208904 | tf_op jit(solution)/shard_map/ppermute | solution.py:258
  46.9 5.5 %collective-permute-start.12 = (f32[128,128]{1,0:T(8,128)S(1)}, f32[128,128]{1,0:T(8,128)S(1)}, u32[]{:S(2)}, u32[]{:S(2)}) collective-permute-start(f32[128,128]{1,0:T(8,128)S(1)} %add.125), channel_id=1, source_target_pairs={{0,16},{4,20},{8,24},{12,28},{16,0},{20,4},{24,8},{28,12},{1,17},{... | collective-permute-start | bytes 196616 | tf_op jit(solution)/shard_map/ppermute | solution.py:258
  54.5 2.0 %collective-permute-start.18 = (f32[136,128]{1,0:T(8,128)S(1)}, f32[136,128]{1,0:T(8,128)S(1)}, u32[]{:S(2)}, u32[]{:S(2)}) collective-permute-start(f32[136,128]{1,0:T(8,128)S(1)} %get-tuple-element.91), channel_id=1, source_target_pairs={{0,1},{1,0},{2,3},{3,2},{4,5},{5,4},{6,7},{7,6},{8,9},{9,8},{10,11... | collective-permute-start | bytes 208904 | tf_op jit(solution)/shard_map/ppermute | solution.py:258
  54.6 4.6 %collective-permute-start.16 = (f32[128,128]{1,0:T(8,128)S(1)}, f32[128,128]{1,0:T(8,128)S(1)}, u32[]{:S(2)}, u32[]{:S(2)}) collective-permute-start(f32[128,128]{1,0:T(8,128)S(1)} %get-tuple-element.90), channel_id=1, source_target_pairs={{0,2},{1,3},{2,0},{3,1},{4,6},{5,7},{6,4},{7,5},{8,10},{9,11},{10,... | collective-permute-start | bytes 196616 | tf_op jit(solution)/shard_map/ppermute | solution.py:258
  56.5 4.4 %collective-permute-start.19 = (f32[136,128]{1,0:T(8,128)S(1)}, f32[136,128]{1,0:T(8,128)S(1)}, u32[]{:S(2)}, u32[]{:S(2)}) collective-permute-start(f32[136,128]{1,0:T(8,128)S(1)} %add.132), channel_id=1, source_target_pairs={{0,2},{1,3},{2,0},{3,1},{4,6},{5,7},{6,4},{7,5},{8,10},{9,11},{10,... | collective-permute-start | bytes 208904 | tf_op jit(solution)/shard_map/ppermute | solution.py:258
  59.2 1.3 %collective-permute-start.17 = (f32[128,128]{1,0:T(8,128)S(1)}, f32[128,128]{1,0:T(8,128)S(1)}, u32[]{:S(2)}, u32[]{:S(2)}) collective-permute-start(f32[128,128]{1,0:T(8,128)S(1)} %add.130), channel_id=1, source_target_pairs={{0,1},{1,0},{2,3},{3,2},{4,5},{5,4},{6,7},{7,6},{8,9},{9,8},{10,11... | collective-permute-start | bytes 196616 | tf_op jit(solution)/shard_map/ppermute | solution.py:258
  62.9 5.1 %collective-permute-start.23 = (f32[136,128]{1,0:T(8,128)S(1)}, f32[136,128]{1,0:T(8,128)S(1)}, u32[]{:S(2)}, u32[]{:S(2)}) collective-permute-start(f32[136,128]{1,0:T(8,128)S(1)} %get-tuple-element.97), channel_id=1, source_target_pairs={{0,4},{4,0},{8,12},{12,8},{16,20},{20,16},{24,28},{28,24},{1,5},{5... | collective-permute-start | bytes 208904 | tf_op jit(solution)/shard_map/ppermute | solution.py:258
  64.4 4.7 %collective-permute-start.20 = (f32[128,128]{1,0:T(8,128)S(1)}, f32[128,128]{1,0:T(8,128)S(1)}, u32[]{:S(2)}, u32[]{:S(2)}) collective-permute-start(f32[128,128]{1,0:T(8,128)S(1)} %get-tuple-element.96), channel_id=1, source_target_pairs={{0,4},{4,0},{8,12},{12,8},{16,20},{20,16},{24,28},{28,24},{1,5},{5... | collective-permute-start | bytes 196616 | tf_op jit(solution)/shard_map/ppermute | solution.py:258
  67.9 4.4 %collective-permute-start.24 = (f32[136,128]{1,0:T(8,128)S(1)}, f32[136,128]{1,0:T(8,128)S(1)}, u32[]{:S(2)}, u32[]{:S(2)}) collective-permute-start(f32[136,128]{1,0:T(8,128)S(1)} %add.137), channel_id=1, source_target_pairs={{0,8},{4,12},{8,0},{12,4},{16,24},{20,28},{24,16},{28,20},{1,9},{5... | collective-permute-start | bytes 208904 | tf_op jit(solution)/shard_map/ppermute | solution.py:258
  69.1 5.0 %collective-permute-start.21 = (f32[128,128]{1,0:T(8,128)S(1)}, f32[128,128]{1,0:T(8,128)S(1)}, u32[]{:S(2)}, u32[]{:S(2)}) collective-permute-start(f32[128,128]{1,0:T(8,128)S(1)} %add.134), channel_id=1, source_target_pairs={{0,8},{4,12},{8,0},{12,4},{16,24},{20,28},{24,16},{28,20},{1,9},{5... | collective-permute-start | bytes 196616 | tf_op jit(solution)/shard_map/ppermute | solution.py:258
  72.3 7.1 %collective-permute-start.25 = (f32[136,128]{1,0:T(8,128)S(1)}, f32[136,128]{1,0:T(8,128)S(1)}, u32[]{:S(2)}, u32[]{:S(2)}) collective-permute-start(f32[136,128]{1,0:T(8,128)S(1)} %add.138), channel_id=1, source_target_pairs={{0,16},{4,20},{8,24},{12,28},{16,0},{20,4},{24,8},{28,12},{1,17},{... | collective-permute-start | bytes 208904 | tf_op jit(solution)/shard_map/ppermute | solution.py:258
  74.2 5.2 %collective-permute-start.22 = (f32[128,128]{1,0:T(8,128)S(1)}, f32[128,128]{1,0:T(8,128)S(1)}, u32[]{:S(2)}, u32[]{:S(2)}) collective-permute-start(f32[128,128]{1,0:T(8,128)S(1)} %add.135), channel_id=1, source_target_pairs={{0,16},{4,20},{8,24},{12,28},{16,0},{20,4},{24,8},{28,12},{1,17},{... | collective-permute-start | bytes 196616 | tf_op jit(solution)/shard_map/ppermute | solution.py:258
  81.4 2.3 %collective-permute-start.28 = (f32[136,128]{1,0:T(8,128)S(1)}, f32[136,128]{1,0:T(8,128)S(1)}, u32[]{:S(2)}, u32[]{:S(2)}) collective-permute-start(f32[136,128]{1,0:T(8,128)S(1)} %get-tuple-element.103), channel_id=1, source_target_pairs={{0,1},{1,0},{2,3},{3,2},{4,5},{5,4},{6,7},{7,6},{8,9},{9,8},{10,11... | collective-permute-start | bytes 208904 | tf_op jit(solution)/shard_map/ppermute | solution.py:258
  81.5 4.9 %collective-permute-start.26 = (f32[128,128]{1,0:T(8,128)S(1)}, f32[128,128]{1,0:T(8,128)S(1)}, u32[]{:S(2)}, u32[]{:S(2)}) collective-permute-start(f32[128,128]{1,0:T(8,128)S(1)} %get-tuple-element.102), channel_id=1, source_target_pairs={{0,2},{1,3},{2,0},{3,1},{4,6},{5,7},{6,4},{7,5},{8,10},{9,11},{10,... | collective-permute-start | bytes 196616 | tf_op jit(solution)/shard_map/ppermute | solution.py:258
  83.7 4.4 %collective-permute-start.29 = (f32[136,128]{1,0:T(8,128)S(1)}, f32[136,128]{1,0:T(8,128)S(1)}, u32[]{:S(2)}, u32[]{:S(2)}) collective-permute-start(f32[136,128]{1,0:T(8,128)S(1)} %add.142), channel_id=1, source_target_pairs={{0,2},{1,3},{2,0},{3,1},{4,6},{5,7},{6,4},{7,5},{8,10},{9,11},{10,... | collective-permute-start | bytes 208904 | tf_op jit(solution)/shard_map/ppermute | solution.py:258
  86.4 1.3 %collective-permute-start.27 = (f32[128,128]{1,0:T(8,128)S(1)}, f32[128,128]{1,0:T(8,128)S(1)}, u32[]{:S(2)}, u32[]{:S(2)}) collective-permute-start(f32[128,128]{1,0:T(8,128)S(1)} %add.140), channel_id=1, source_target_pairs={{0,1},{1,0},{2,3},{3,2},{4,5},{5,4},{6,7},{7,6},{8,9},{9,8},{10,11... | collective-permute-start | bytes 196616 | tf_op jit(solution)/shard_map/ppermute | solution.py:258
  90.0 4.7 %collective-permute-start.33 = (f32[136,128]{1,0:T(8,128)S(1)}, f32[136,128]{1,0:T(8,128)S(1)}, u32[]{:S(2)}, u32[]{:S(2)}) collective-permute-start(f32[136,128]{1,0:T(8,128)S(1)} %get-tuple-element.110), channel_id=1, source_target_pairs={{0,4},{4,0},{8,12},{12,8},{16,20},{20,16},{24,28},{28,24},{1,5},{5... | collective-permute-start | bytes 208904 | tf_op jit(solution)/shard_map/ppermute | solution.py:258
  90.9 5.1 %collective-permute-start.30 = (f32[128,128]{1,0:T(8,128)S(1)}, f32[128,128]{1,0:T(8,128)S(1)}, u32[]{:S(2)}, u32[]{:S(2)}) collective-permute-start(f32[128,128]{1,0:T(8,128)S(1)} %get-tuple-element.109), channel_id=1, source_target_pairs={{0,4},{4,0},{8,12},{12,8},{16,20},{20,16},{24,28},{28,24},{1,5},{5... | collective-permute-start | bytes 196616 | tf_op jit(solution)/shard_map/ppermute | solution.py:258
  94.7 4.4 %collective-permute-start.34 = (f32[136,128]{1,0:T(8,128)S(1)}, f32[136,128]{1,0:T(8,128)S(1)}, u32[]{:S(2)}, u32[]{:S(2)}) collective-permute-start(f32[136,128]{1,0:T(8,128)S(1)} %add.147), channel_id=1, source_target_pairs={{0,8},{4,12},{8,0},{12,4},{16,24},{20,28},{24,16},{28,20},{1,9},{5... | collective-permute-start | bytes 208904 | tf_op jit(solution)/shard_map/ppermute | solution.py:258
  96.0 5.1 %collective-permute-start.31 = (f32[128,128]{1,0:T(8,128)S(1)}, f32[128,128]{1,0:T(8,128)S(1)}, u32[]{:S(2)}, u32[]{:S(2)}) collective-permute-start(f32[128,128]{1,0:T(8,128)S(1)} %add.144), channel_id=1, source_target_pairs={{0,8},{4,12},{8,0},{12,4},{16,24},{20,28},{24,16},{28,20},{1,9},{5... | collective-permute-start | bytes 196616 | tf_op jit(solution)/shard_map/ppermute | solution.py:258
  99.1 7.3 %collective-permute-start.35 = (f32[136,128]{1,0:T(8,128)S(1)}, f32[136,128]{1,0:T(8,128)S(1)}, u32[]{:S(2)}, u32[]{:S(2)}) collective-permute-start(f32[136,128]{1,0:T(8,128)S(1)} %add.148), channel_id=1, source_target_pairs={{0,16},{4,20},{8,24},{12,28},{16,0},{20,4},{24,8},{28,12},{1,17},{... | collective-permute-start | bytes 208904 | tf_op jit(solution)/shard_map/ppermute | solution.py:258
  101.1 5.2 %collective-permute-start.32 = (f32[128,128]{1,0:T(8,128)S(1)}, f32[128,128]{1,0:T(8,128)S(1)}, u32[]{:S(2)}, u32[]{:S(2)}) collective-permute-start(f32[128,128]{1,0:T(8,128)S(1)} %add.145), channel_id=1, source_target_pairs={{0,16},{4,20},{8,24},{12,28},{16,0},{20,4},{24,8},{28,12},{1,17},{... | collective-permute-start | bytes 196616 | tf_op jit(solution)/shard_map/ppermute | solution.py:258
  106.5 1.2 %collective-permute-start.36 = (f32[8,128]{1,0:T(8,128)S(1)}, f32[8,128]{1,0:T(8,128)S(1)}, u32[]{:S(2)}, u32[]{:S(2)}) collective-permute-start(f32[8,128]{1,0:T(8,128)S(1)} %get-tuple-element.114), channel_id=1, source_target_pairs={{0,1},{1,0},{2,3},{3,2},{4,5},{5,4},{6,7},{7,6},{8,9},{9,8},{10,11... | collective-permute-start | bytes 12296 | tf_op jit(solution)/shard_map/ppermute | solution.py:258
  107.8 3.7 %collective-permute-start.37 = (f32[8,128]{1,0:T(8,128)S(1)}, f32[8,128]{1,0:T(8,128)S(1)}, u32[]{:S(2)}, u32[]{:S(2)}) collective-permute-start(f32[8,128]{1,0:T(8,128)S(1)} %add.150), channel_id=1, source_target_pairs={{0,2},{1,3},{2,0},{3,1},{4,6},{5,7},{6,4},{7,5},{8,10},{9,11},{10,... | collective-permute-start | bytes 12296 | tf_op jit(solution)/shard_map/ppermute | solution.py:258
